TPU v7x, 32 devices: a whole 2x2x4 slice. The times are simulated.
32 devices in a mesh: grp: 4 (over y, x), own: 8 (over z, core).
Axes of the slice: x: 2, y: 2, z: 4, core: 2. Of those that a mesh axis runs over, the one named last changes fastest.
Arguments:
- embeddings: float32 [24576, 768], P(('grp', 'own')), may hold values from -64 to 64
- cluster_ids: int32 [24576], P(('grp', 'own')), may hold values from 0 to 127, as said below
- owner_map: int32 [128], replicated, may hold values from 0 to 7, as said below
- source_order: int32 [24576], P(('grp', 'own')), may hold values from 0 to 767, as said below
Outputs:
- dup_score: float32 [24576], P(('grp', 'own'))
- centroids: float32 [128, 768], P('own')
Inputs may be any that keep to these rules, and one draw needn't show every extreme that they name: `owner_map`: every owner index is given to exactly 16 clusters. `cluster_ids`: within the 768 rows of one device, at most 192 rows have clusters of one owner index; in every draw some owner index receives exactly 192 rows from every device, and every device sends exactly 192 rows to some owner index. Cluster sizes are uneven and some clusters may be empty. `source_order`: each aligned block of 768 entries is a permutation of 0 to 767.
All inputs are finite; a program needn't handle non-finite values.
Results may differ from a plain program's by a relative error of at most 0.0003.
Values sent between devices are 32-bit elements; how exact they have to be, the bound alone decides.
No kernel may reach another device: no remote copies, remote signals or barrier semaphores. Data moves between devices by JAX's collectives and lax.ppermute only.
A program may use at most 128 MiB of HBM per device.

v0:
```python
import jax
import jax.numpy as jnp
from jax import lax
from jax.sharding import PartitionSpec as P

CL_OWN = 16


sharpness = 6.0


def passed_along(value, axis, steps):
    count = lax.axis_size(axis)
    pairs = [(source, (source + steps) % count) for source in range(count)]
    return lax.ppermute(value, axis, pairs)


def unit_rows(embeddings):
    squares = jnp.sum(embeddings * embeddings, axis=1, keepdims=True)
    return embeddings * lax.rsqrt(squares + 1e-06)


def owner_positions(owner_map):
    cluster_index = jnp.arange(owner_map.shape[0], dtype=jnp.int32)
    same_owner = owner_map[:, None] == owner_map[None, :]
    earlier = cluster_index[None, :] < cluster_index[:, None]
    before = jnp.sum((same_owner & earlier).astype(jnp.int32), axis=1)
    return owner_map * CL_OWN + before


def masked_weights(left_rows, left_ids, right_rows, right_ids):
    scores = jnp.einsum(
        "id,jd->ij",
        left_rows,
        right_rows,
        preferred_element_type=jnp.float32,
        precision=lax.Precision.HIGHEST,
    )
    linked = (left_ids[:, None] == right_ids[None, :]) & (left_ids[:, None] >= 0)
    return jnp.where(linked, jnp.exp(sharpness * (scores - 1.0)), 0.0)


def tile_sums(left_rows, left_ids, right_rows, right_ids, with_columns):
    right_count = right_rows.shape[0]
    block_rows = 512
    block_count = right_count // block_rows
    right_blocks = right_rows.reshape(block_count, block_rows, right_rows.shape[1])
    id_blocks = right_ids.reshape(block_count, block_rows)

    def one_block(row_total, block_pair):
        weights = masked_weights(left_rows, left_ids, block_pair[0], block_pair[1])
        column_part = jnp.sum(weights, axis=0) if with_columns else None
        return (row_total + jnp.sum(weights, axis=1), column_part)

    row_sums, column_sums = lax.scan(
        one_block, jnp.zeros((left_rows.shape[0],), jnp.float32), (right_blocks, id_blocks)
    )
    if with_columns:
        column_sums = column_sums.reshape(right_count)
    return (row_sums, column_sums)


def local(embeddings, cluster_ids, owner_map, source_order):
    row_count, feature_width = embeddings.shape
    owner_count = lax.axis_size("own")
    capacity = 2 * row_count // owner_count
    slot_count = owner_count * capacity
    cluster_count = owner_map.shape[0]
    unit_embed = unit_rows(embeddings)
    cluster_index = jnp.arange(cluster_count, dtype=jnp.int32)
    cluster_match = cluster_ids[:, None] == cluster_index[None, :]
    row_owner = jnp.sum(jnp.where(cluster_match, owner_map[None, :], 0), axis=1)
    owner_hot = (row_owner[:, None] == jnp.arange(owner_count, dtype=jnp.int32)[None, :]).astype(
        jnp.int32
    )
    rank_index = jnp.sum(jnp.cumsum(owner_hot, axis=0) * owner_hot, axis=1) - 1
    slot_index = row_owner * capacity + rank_index
    send_rows = jnp.zeros((slot_count, feature_width), jnp.float32).at[slot_index].set(unit_embed)
    send_ids = jnp.full((slot_count,), -1, jnp.int32).at[slot_index].set(cluster_ids)
    held_rows, held_ids = (
        lax.all_to_all(
            send_rows.reshape(owner_count, capacity, feature_width),
            "own",
            split_axis=0,
            concat_axis=0,
            tiled=True,
        ),
        lax.all_to_all(
            send_ids.reshape(owner_count, capacity), "own", split_axis=0, concat_axis=0, tiled=True
        ),
    )
    held_rows = held_rows.reshape(slot_count, feature_width)
    held_ids = held_ids.reshape(slot_count)
    group_count = lax.axis_size("grp")
    dup_mass, column_sums = tile_sums(held_rows, held_ids, held_rows, held_ids, False)
    for offset in range(1, group_count // 2 + 1):
        far_rows, far_ids = passed_along((held_rows, held_ids), "grp", -offset)
        returning = offset < group_count - offset
        row_sums, column_sums = tile_sums(held_rows, held_ids, far_rows, far_ids, returning)
        dup_mass = dup_mass + row_sums
        if returning:
            dup_mass = dup_mass + passed_along(column_sums, "grp", offset)
    returned = lax.all_to_all(
        dup_mass.reshape(owner_count, capacity), "own", split_axis=0, concat_axis=0, tiled=True
    )
    row_score = jnp.log(returned.reshape(slot_count)[slot_index])
    dup_score = jnp.zeros((row_count,), jnp.float32).at[source_order].set(row_score)
    position = owner_positions(owner_map)
    position_index = jnp.arange(cluster_count, dtype=jnp.int32)
    ordered = jnp.sum(
        jnp.where(position[None, :] == position_index[:, None], cluster_index[None, :], 0), axis=1
    )
    cluster_hot = (cluster_ids[:, None] == ordered[None, :]).astype(jnp.float32)
    cluster_terms = lax.dot_general(
        cluster_hot,
        unit_embed,
        (((0,), (0,)), ((), ())),
        preferred_element_type=jnp.float32,
        precision=lax.Precision.HIGHEST,
    )
    partial_value = lax.psum_scatter(cluster_terms, "own", scatter_dimension=0, tiled=True)
    cluster_sums = lax.psum(partial_value, "grp")
    centroids = cluster_sums * lax.rsqrt(
        jnp.mean(cluster_sums * cluster_sums, axis=1, keepdims=True) + 1e-06
    )
    return (dup_score, centroids)


def solution(mesh):
    placed = (P(("grp", "own"), None), P(("grp", "own")), P(), P(("grp", "own")))
    return jax.shard_map(
        local,
        mesh=mesh,
        in_specs=placed,
        out_specs=(P(("grp", "own")), P("own", None)),
        check_vma=False,
    )
```

profile of v0, /device:TPU:0, one launch (start us, length us, event | category | flops | bytes accessed | tf_op | source)
XLA Modules:
  0.0 413.7 jit_solution(8130020601397739330)
XLA Ops:
  7.2 1.1 select_reduce_fusion
  8.3 1.7 reduce-window.6
  10.6 1.9 multiply_reduce_fusion
  12.6 9.8 %scatter_custom_fusion.1 = f32[1536,768]{1,0:T(8,128)} fusion(s32[768]{0:T(1024)S(1)} %fusion.42, f32[]{:T(128)} %constant.122.clone.1, f32[768,768]{1,0:T(8,128)S(1)} %copy-done, f32[768]{0:T(1024)S(1)} %add_rsqrt_fusion), kind=kCustom, calls=%fused_computation.40 | custom fusion | flops 589824 | bytes 7081988 | tf_op jit(solution)/shard_map/scatter | solution.py:78
  22.3 6.5 %all-to-all-start.1 = ((f32[8,192,768]{2,1,0:T(8,128)}), f32[8,192,768]{2,1,0:T(8,128)}, u32[]{:S(2)}, u32[]{:S(2)}) async-start(f32[8,192,768]{2,1,0:T(8,128)} %bitcast.91), calls=%async_computation.1 | async-start | bytes 9437184 | tf_op jit(solution)/shard_map/all_to_all | solution.py:81
  29.0 105.1 %all-to-all-done.1 = f32[8,192,768]{2,1,0:T(8,128)} async-done(((f32[8,192,768]{2,1,0:T(8,128)}), f32[8,192,768]{2,1,0:T(8,128)}, u32[]{:S(2)}, u32[]{:S(2)}) %all-to-all-start.1) | async-done | bytes 4718624 | tf_op jit(solution)/shard_map/all_to_all | solution.py:81
  134.1 2.4 collective-permute-start.1
  136.7 1.9 fusion.29
  138.6 3.4 scatter_custom_fusion
  142.0 0.7 all_to_all.17
  142.7 3.3 all-to-all-start
  146.1 5.5 %all-to-all-done = s32[8,1,192]{2,1,0:T(1,128)S(1)} async-done(((s32[8,1,192]{2,1,0:T(1,128)}), s32[8,1,192]{2,1,0:T(1,128)S(1)}, u32[]{:S(2)}, u32[]{:S(2)}) %all-to-all-start) | async-done | bytes 6176 | tf_op jit(solution)/shard_map/all_to_all | solution.py:88
  153.1 84.7 %collective-permute-done = s32[1536]{0:T(1024)S(1)} collective-permute-done((s32[1536]{0:T(1024)S(1)}, s32[1536]{0:T(1024)S(1)}, u32[]{:S(2)}, u32[]{:S(2)}) %collective-permute-start) | collective-permute-done | bytes 6176 | tf_op jit(solution)/shard_map/ppermute | solution.py:15
  237.8 18.5 %psum.7 = f32[16,768]{1,0:T(8,128)S(1)} all-reduce(f32[16,768]{1,0:T(8,128)} %reduce-scatter.2.cloned.1.call-done), channel_id=1, replica_groups=mesh['grp'=4,'own'=8] {'grp'}, use_global_device_ids=true, to_apply=%region_21.22 | all-reduce | flops 12288 | bytes 98304 | tf_op jit(solution)/shard_map/psum | solution.py:122
  257.0 33.5 %while.44 = (s32[]{:T(128)}, f32[1536]{0:T(1024)S(1)}, s32[8,192]{1,0:T(8,128)}, s32[3,512]{1,0:T(4,128)S(1)}, f32[3,512,768]{2,1,0:T(8,128)}, /*index=5*/f32[15...) while((s32[]{:T(128)}, f32[1536]{0:T(1024)S(1)}, s32[8,192]{1,0:T(8,128)}, ...), condition=%wide.wide.region_9.10_spmd.clone, body=%wide.wide.region_7.9_spmd.clone.sunk | while | flops 7252478976 | bytes 6338155 | solution.py:55
  257.0 11.5 %fusion.67 = f32[1536]{0:T(1024)S(1)} fusion(f32[1536,768]{1,0:T(8,128)} %get-tuple-element.653, f32[3,512,768]{2,1,0:T(8,128)} %get-tuple-element.652, s32[]{:T(128)} %get-tuple-element.639, pred[1536]{0:T(1024)(128)(4,1)S(1)} %broadcast_compare_fusion.9, s32[512]{0:T(512)S(1)} %bitcast.99, s32[1536]{0:T(1024)S(1)} %get-tuple-element.654), kind=kOutput, calls=%fused_computation.11.clone.clone.1 | convolution fusion | flops 7252474368 | bytes 6307840 | tf_op jit(solution)/shard_map/while/body/eval_jaxpr/id,jd->ij/dot_general | solution.py:32
  268.5 10.9 %fusion.67 = f32[1536]{0:T(1024)S(1)} fusion(f32[1536,768]{1,0:T(8,128)} %get-tuple-element.653, f32[3,512,768]{2,1,0:T(8,128)} %get-tuple-element.652, s32[]{:T(128)} %get-tuple-element.639, pred[1536]{0:T(1024)(128)(4,1)S(1)} %broadcast_compare_fusion.9, s32[512]{0:T(512)S(1)} %bitcast.99, s32[1536]{0:T(1024)S(1)} %get-tuple-element.654), kind=kOutput, calls=%fused_computation.11.clone.clone.1 | convolution fusion | flops 7252474368 | bytes 6307840 | tf_op jit(solution)/shard_map/while/body/eval_jaxpr/id,jd->ij/dot_general | solution.py:32
  279.5 10.9 %fusion.67 = f32[1536]{0:T(1024)S(1)} fusion(f32[1536,768]{1,0:T(8,128)} %get-tuple-element.653, f32[3,512,768]{2,1,0:T(8,128)} %get-tuple-element.652, s32[]{:T(128)} %get-tuple-element.639, pred[1536]{0:T(1024)(128)(4,1)S(1)} %broadcast_compare_fusion.9, s32[512]{0:T(512)S(1)} %bitcast.99, s32[1536]{0:T(1024)S(1)} %get-tuple-element.654), kind=kOutput, calls=%fused_computation.11.clone.clone.1 | convolution fusion | flops 7252474368 | bytes 6307840 | tf_op jit(solution)/shard_map/while/body/eval_jaxpr/id,jd->ij/dot_general | solution.py:32
  290.5 32.8 %while.45 = (s32[]{:T(128)}, f32[1536]{0:T(1024)S(1)}, f32[3,512]{1,0:T(4,128)S(1)}, s32[8,192]{1,0:T(8,128)}, s32[3,512]{1,0:T(4,128)S(1)}, /*index=5*/f32[3,51...) while((s32[]{:T(128)}, f32[1536]{0:T(1024)S(1)}, ...), condition=%wide.wide.region_13.14_spmd.clone, body=%wide.wide.region_10.13_spmd.clone.sunk | while | flops 7253264896 | bytes 6344311 | solution.py:55
  290.5 10.8 %fusion.69 = (f32[512]{0:T(512)S(1)}, f32[1536]{0:T(1024)S(1)}) fusion(f32[1536,768]{1,0:T(8,128)} %get-tuple-element.626, f32[3,512,768]{2,1,0:T(8,128)} %get-tuple-element.625, s32[]{:T(128)} %get-tuple-element.610, pred[1536]{0:T(1024)(128)(4,1)S(1)} %broadcast_compare_fusion.10, s32[512]{0:T(512)S(1)} %bitcast.98, ...), kind=kOutput, calls=%fused_computation.78.clone.clone.1 | convolution fusion | flops 7253260288 | bytes 6309888 | tf_op jit(solution)/shard_map/while/body/eval_jaxpr/id,jd->ij/dot_general | solution.py:32
  301.5 10.8 %fusion.69 = (f32[512]{0:T(512)S(1)}, f32[1536]{0:T(1024)S(1)}) fusion(f32[1536,768]{1,0:T(8,128)} %get-tuple-element.626, f32[3,512,768]{2,1,0:T(8,128)} %get-tuple-element.625, s32[]{:T(128)} %get-tuple-element.610, pred[1536]{0:T(1024)(128)(4,1)S(1)} %broadcast_compare_fusion.10, s32[512]{0:T(512)S(1)} %bitcast.98, ...), kind=kOutput, calls=%fused_computation.78.clone.clone.1 | convolution fusion | flops 7253260288 | bytes 6309888 | tf_op jit(solution)/shard_map/while/body/eval_jaxpr/id,jd->ij/dot_general | solution.py:32
  312.4 10.8 %fusion.69 = (f32[512]{0:T(512)S(1)}, f32[1536]{0:T(1024)S(1)}) fusion(f32[1536,768]{1,0:T(8,128)} %get-tuple-element.626, f32[3,512,768]{2,1,0:T(8,128)} %get-tuple-element.625, s32[]{:T(128)} %get-tuple-element.610, pred[1536]{0:T(1024)(128)(4,1)S(1)} %broadcast_compare_fusion.10, s32[512]{0:T(512)S(1)} %bitcast.98, ...), kind=kOutput, calls=%fused_computation.78.clone.clone.1 | convolution fusion | flops 7253260288 | bytes 6309888 | tf_op jit(solution)/shard_map/while/body/eval_jaxpr/id,jd->ij/dot_general | solution.py:32
  323.6 32.1 %collective-permute-done.4 = f32[1536,768]{1,0:T(8,128)} collective-permute-done((f32[1536,768]{1,0:T(8,128)}, f32[1536,768]{1,0:T(8,128)}, u32[]{:S(2)}, u32[]{:S(2)}) %collective-permute-start.4) | collective-permute-done | bytes 4718624 | tf_op jit(solution)/shard_map/ppermute | solution.py:15
  355.8 32.9 %while.46 = (s32[]{:T(128)}, f32[1536]{0:T(1024)S(1)}, s32[8,192]{1,0:T(8,128)}, s32[3,512]{1,0:T(4,128)S(1)}, f32[3,512,768]{2,1,0:T(8,128)}, /*index=5*/f32[15...) while((s32[]{:T(128)}, f32[1536]{0:T(1024)S(1)}, s32[8,192]{1,0:T(8,128)}, ...), condition=%wide.wide.region_16.17_spmd.clone, body=%wide.wide.region_14.16_spmd.clone.sunk | while | flops 7252478976 | bytes 6338155 | solution.py:55
  355.8 10.9 %fusion.72 = f32[1536]{0:T(1024)S(1)} fusion(f32[1536,768]{1,0:T(8,128)} %get-tuple-element.596, f32[3,512,768]{2,1,0:T(8,128)} %get-tuple-element.595, s32[]{:T(128)} %get-tuple-element.582, pred[1536]{0:T(1024)(128)(4,1)S(1)} %broadcast_compare_fusion.11, s32[512]{0:T(512)S(1)} %bitcast.100, s32[1536]{0:T(1024)S(1)} %get-tuple-element.597), kind=kOutput, calls=%fused_computation.34.clone.clone.1 | convolution fusion | flops 7252474368 | bytes 6307840 | tf_op jit(solution)/shard_map/while/body/eval_jaxpr/id,jd->ij/dot_general | solution.py:32
  366.7 10.9 %fusion.72 = f32[1536]{0:T(1024)S(1)} fusion(f32[1536,768]{1,0:T(8,128)} %get-tuple-element.596, f32[3,512,768]{2,1,0:T(8,128)} %get-tuple-element.595, s32[]{:T(128)} %get-tuple-element.582, pred[1536]{0:T(1024)(128)(4,1)S(1)} %broadcast_compare_fusion.11, s32[512]{0:T(512)S(1)} %bitcast.100, s32[1536]{0:T(1024)S(1)} %get-tuple-element.597), kind=kOutput, calls=%fused_computation.34.clone.clone.1 | convolution fusion | flops 7252474368 | bytes 6307840 | tf_op jit(solution)/shard_map/while/body/eval_jaxpr/id,jd->ij/dot_general | solution.py:32
  377.7 10.9 %fusion.72 = f32[1536]{0:T(1024)S(1)} fusion(f32[1536,768]{1,0:T(8,128)} %get-tuple-element.596, f32[3,512,768]{2,1,0:T(8,128)} %get-tuple-element.595, s32[]{:T(128)} %get-tuple-element.582, pred[1536]{0:T(1024)(128)(4,1)S(1)} %broadcast_compare_fusion.11, s32[512]{0:T(512)S(1)} %bitcast.100, s32[1536]{0:T(1024)S(1)} %get-tuple-element.597), kind=kOutput, calls=%fused_computation.34.clone.clone.1 | convolution fusion | flops 7252474368 | bytes 6307840 | tf_op jit(solution)/shard_map/while/body/eval_jaxpr/id,jd->ij/dot_general | solution.py:32
  389.4 3.4 all-to-all-start.2
  392.7 0.7 broadcast_multiply_fusion
  393.4 4.9 %all-to-all-done.2 = f32[8,1,192]{2,1,0:T(1,128)S(1)} async-done(((f32[8,1,192]{2,1,0:T(1,128)}), f32[8,1,192]{2,1,0:T(1,128)S(1)}, u32[]{:S(2)}, u32[]{:S(2)}) %all-to-all-start.2) | async-done | bytes 6176 | tf_op jit(solution)/shard_map/all_to_all | solution.py:103
  398.4 4.5 %gather_fusion = f32[768]{0:T(1024)S(1)} fusion(f32[1536]{0:T(1024)S(1)} %reshape.150, s32[1024]{0:T(1024)S(1)} %pad_clamp_fusion), kind=kCustom, calls=%fused_computation | custom fusion | bytes 9216 | tf_op jit(solution)/shard_map/gather | solution.py:106
  402.9 3.9 scatter_custom_fusion.2
  (85 shorter events, 4.5 us)
Async XLA Ops:
  7.2 5.4 %copy-start = (f32[768,768]{1,0:T(8,128)S(1)}, f32[768,768]{1,0:T(8,128)}, u32[]{:S(2)}) copy-start(f32[768,768]{1,0:T(8,128)} %param.10) | copy-start | bytes 7077892
  22.3 6.5 %copy-start.4 = (s32[128]{0:T(128)S(1)}, s32[128]{0:T(128)}, u32[]{:S(2)}) copy-start(s32[128]{0:T(128)} %param.12) | copy-start | bytes 1540
  22.3 114.4 %copy-start.2 = (s32[768]{0:T(1024)S(1)}, s32[768]{0:T(1024)}, u32[]{:S(2)}) copy-start(s32[768]{0:T(1024)} %param.11) | copy-start | bytes 9220
  22.3 111.8 %all-to-all-start.1 = ((f32[8,192,768]{2,1,0:T(8,128)}), f32[8,192,768]{2,1,0:T(8,128)}, u32[]{:S(2)}, u32[]{:S(2)}) async-start(f32[8,192,768]{2,1,0:T(8,128)} %bitcast.91), calls=%async_computation.1 | async-start | bytes 9437184 | tf_op jit(solution)/shard_map/all_to_all | solution.py:81
  28.8 117.3 %copy-start.3 = (s32[768]{0:T(1024)S(1)}, s32[768]{0:T(1024)}, u32[]{:S(2)}) copy-start(s32[768]{0:T(1024)} %param.13) | copy-start | bytes 9220
  28.8 209.0 %reduce-scatter.2.cloned.1.call-start = ((), (), s32[]{:S(2)}) async-start(), calls=%async_computation.4 | async-start | bytes 442368 | tf_op jit(solution)/shard_map/reduce_scatter | solution.py:121
  134.1 156.3 %collective-permute-start.1 = (f32[1536,768]{1,0:T(8,128)}, f32[1536,768]{1,0:T(8,128)}, u32[]{:S(2)}, u32[]{:S(2)}) collective-permute-start(f32[1536,768]{1,0:T(8,128)} %bitcast.6), channel_id=1, source_target_pairs={{0,24},{8,0},{16,8},{24,16},{1,25},{9,1},{17,9},{25,17},{2,26},{10... | collective-permute-start | bytes 14155784 | tf_op jit(solution)/shard_map/ppermute | solution.py:15
  142.7 8.9 %all-to-all-start = ((s32[8,1,192]{2,1,0:T(1,128)}), s32[8,1,192]{2,1,0:T(1,128)S(1)}, u32[]{:S(2)}, u32[]{:S(2)}) async-start(s32[8,1,192]{2,1,0:T(1,128)} %all_to_all.17), calls=%async_computation | async-start | bytes 16384 | tf_op jit(solution)/shard_map/all_to_all | solution.py:88
  151.7 86.1 %collective-permute-start = (s32[1536]{0:T(1024)S(1)}, s32[1536]{0:T(1024)S(1)}, u32[]{:S(2)}, u32[]{:S(2)}) collective-permute-start(s32[1536]{0:T(1024)S(1)} %reshape.144), channel_id=1, source_target_pairs={{0,24},{8,0},{16,8},{24,16},{1,25},{9,1},{17,9},{25,17},{2,26},{10... | collective-permute-start | bytes 18440 | tf_op jit(solution)/shard_map/ppermute | solution.py:15
  152.2 85.6 %collective-permute-start.3 = (s32[1536]{0:T(1024)S(1)}, s32[1536]{0:T(1024)S(1)}, u32[]{:S(2)}, u32[]{:S(2)}) collective-permute-start(s32[1536]{0:T(1024)S(1)} %reshape.144), channel_id=1, source_target_pairs={{0,16},{8,24},{16,0},{24,8},{1,17},{9,25},{17,1},{25,9},{2,18},{10... | collective-permute-start | bytes 18440 | tf_op jit(solution)/shard_map/ppermute | solution.py:15
  152.8 104.2 %copy-start.1 = (s32[8,1,192]{2,0,1:T(8,128)}, s32[8,1,192]{2,0,1:T(8,128)S(1)}, u32[]{:S(2)}) copy-start(s32[8,1,192]{2,0,1:T(8,128)S(1)} %copy.16) | copy-start | bytes 18436
  256.4 99.3 %collective-permute-start.4 = (f32[1536,768]{1,0:T(8,128)}, f32[1536,768]{1,0:T(8,128)}, u32[]{:S(2)}, u32[]{:S(2)}) collective-permute-start(f32[1536,768]{1,0:T(8,128)} %bitcast.6), channel_id=1, source_target_pairs={{0,16},{8,24},{16,0},{24,8},{1,17},{9,25},{17,1},{25,9},{2,18},{10... | collective-permute-start | bytes 14155784 | tf_op jit(solution)/shard_map/ppermute | solution.py:15
  323.3 65.3 %collective-permute-start.2 = (f32[1536]{0:T(1024)S(1)}, f32[1536]{0:T(1024)S(1)}, u32[]{:S(2)}, u32[]{:S(2)}) collective-permute-start(f32[1536]{0:T(1024)S(1)} %reshape.147), channel_id=1, source_target_pairs={{0,8},{8,16},{16,24},{24,0},{1,9},{9,17},{17,25},{25,1},{2,10},{10... | collective-permute-start | bytes 18440 | tf_op jit(solution)/shard_map/ppermute | solution.py:15
  389.4 9.0 %all-to-all-start.2 = ((f32[8,1,192]{2,1,0:T(1,128)}), f32[8,1,192]{2,1,0:T(1,128)S(1)}, u32[]{:S(2)}, u32[]{:S(2)}) async-start(f32[8,1,192]{2,1,0:T(1,128)} %all_to_all.21), calls=%async_computation.2 | async-start | bytes 16384 | tf_op jit(solution)/shard_map/all_to_all | solution.py:103
Sparse Core Ops, SparseCore 0:
  138.8 28.2 reduce-scatter.1
where the time goes:
time: 414 us
  waiting for transfers between devices  232 us (56%)
  matrix products  100 us (24%)
  blocking collectives  18.5 us (4%)
  starting transfers between devices  17.5 us (4%)
  other arithmetic  16.1 us (4%)
  between operations  14.3 us (3%)
  local copies, waits for them, and re-layouts  14.2 us (3%)
    ppermute x5, waiting for transfers between devices, passed_along(): return lax.ppermute(value, axis, pairs)  117 us
    all_to_all x1, waiting for transfers between devices, local(): lax.all_to_all(send_rows.reshape(owner_count, capacity, feature_width), '...  105 us
    dot_general x9, matrix products, masked_weights(): jnp.einsum('id,jd->ij', left_rows, right_rows, preferred_element_type=jnp...  98.5 us
    psum x1, blocking collectives, local(): cluster_sums = lax.psum(partial_value, 'grp')  18.5 us
    scatter x1, other arithmetic, local(): jnp.zeros((slot_count, feature_width), jnp.float32).at[slot_index]  9.76 us
  transfers between devices with their start and end apart: 9, of which 5 were waited for; matrix products, arithmetic and copies ran while one was open for 26% of the time, Pallas kernels for 0%

commit v1 on v0

v1 whole, which is shorter than its diff:
```python
import functools

import jax
import jax.numpy as jnp
from jax import lax
from jax.experimental import pallas as pl
from jax.experimental.pallas import tpu as pltpu
from jax.sharding import Mesh
from jax.sharding import PartitionSpec as P


SHARPNESS = 6.0
CHUNKS = 3
TILES = 2
LANES = 128
VMEM = pltpu.VMEM
EVERY = ("grp", "outer", "inner")
PLANE = ("grp", "inner")
LINE = ("outer", "inner")
BY_LEVEL = ("outer", "grp", "inner")
NT = (((1,), (1,)), ((), ()))


def iota(shape, axis):
    return lax.broadcasted_iota(jnp.int32, shape, axis)


def mm(left, right):
    return jnp.dot(left, right, preferred_element_type=jnp.float32)


def mm_nt(left, right):
    return lax.dot_general(left, right, NT, preferred_element_type=jnp.float32)


def halves(value):
    high = value.astype(jnp.bfloat16)
    low = (value - high.astype(jnp.float32)).astype(jnp.bfloat16)
    return high, low


def hot(mask):
    return jnp.where(mask, 1.0, 0.0).astype(jnp.bfloat16)


def cost(micros):
    return pl.CostEstimate(flops=int(micros * 1.1e9), transcendentals=0, bytes_accessed=0)


def call(body, outs, *args, micros, scratch=(), smem=0, aliases=None):
    spec = [pl.BlockSpec(memory_space=pltpu.SMEM)] * smem
    spec += [pl.BlockSpec(memory_space=VMEM)] * (len(args) - smem)
    return pl.pallas_call(
        body,
        out_shape=outs,
        in_specs=spec,
        out_specs=jax.tree.map(lambda _: pl.BlockSpec(memory_space=VMEM), outs),
        scratch_shapes=list(scratch),
        input_output_aliases=aliases or {},
        cost_estimate=cost(micros),
    )(*args)


def out(shape, dtype=jnp.float32):
    return jax.ShapeDtypeStruct(shape, dtype)


def chunk_rows(owner, rank, high, low, k, owners, per):
    inside = (rank >= k * per) & (rank < (k + 1) * per)
    dest = jnp.where(inside, owner * per + rank - k * per, -1)
    pick = hot(iota((owners * per, dest.shape[1]), 0) == dest)
    return mm(pick, high) + mm(pick, low)


def front_body(owners, per, x_ref, ids_ref, om_ref, omr_ref, chunk_ref, high_ref, low_ref, info_ref, sid_ref):
    x = x_ref[...]
    ids = ids_ref[...]
    om = om_ref[...]
    rows = x.shape[0]
    clusters = om.shape[0]
    cap = sid_ref.shape[1]
    square = (clusters, clusters)
    here = iota((clusters, rows), 0) == ids
    owner = jnp.sum(jnp.where(here, om, 0), axis=0, keepdims=True)
    mine = iota((owners, rows), 0) == owner
    member = hot(here)
    within = mm(member, hot(iota((rows, rows), 0) < iota((rows, rows), 1)))
    earlier = hot((om == omr_ref[...]) & (iota(square, 1) < iota(square, 0)))
    base = jnp.sum(mm(earlier, member), axis=1, keepdims=True)
    rank = jnp.sum(jnp.where(here, within + base, 0.0), axis=0, keepdims=True)
    count = jnp.sum(mine.astype(jnp.float32), axis=1, keepdims=True)
    count = jnp.sum(jnp.where(mine, count, 0.0), axis=0, keepdims=True)
    rank = jnp.floor((rank * cap + 0.5) / count).astype(jnp.int32)
    info_ref[...] = jnp.concatenate([owner, rank] * 4, axis=0)
    unit = x * lax.rsqrt(jnp.sum(x * x, axis=1, keepdims=True) + 1e-6)
    high, low = halves(unit)
    high_ref[...] = high
    low_ref[...] = low
    chunk_ref[...] = chunk_rows(owner, rank, high, low, 0, owners, per)
    at_rank = hot(iota((cap, rows), 0) == rank)
    coarse = (ids + 1) // 16
    fine = ids + 1 - coarse * 16
    coarse = jnp.where(mine, coarse.astype(jnp.float32), 0.0).astype(jnp.bfloat16)
    fine = jnp.where(mine, fine.astype(jnp.float32), 0.0).astype(jnp.bfloat16)
    sid = mm_nt(coarse, at_rank) * 16.0 + mm_nt(fine, at_rank)
    sid_ref[...] = sid.astype(jnp.int32) - 1


def back_body(owners, per, chunks, held, high_ref, low_ref, info_ref, ids_ref, om_ref, omr_ref, so_ref, *outs):
    high = high_ref[...]
    low = low_ref[...]
    owner = info_ref[0:1, :]
    rank = info_ref[1:2, :]
    rows = high.shape[0]
    clusters = om_ref.shape[0]
    for k in range(1, chunks):
        outs[k - 1][...] = chunk_rows(owner, rank, high, low, k, owners, per)
    sums_ref, q_ref = outs[chunks - 1 :]
    om = om_ref[...]
    square = (clusters, clusters)
    earlier = (om == omr_ref[...]) & (iota(square, 1) < iota(square, 0))
    position = om * held + jnp.sum(earlier.astype(jnp.int32), axis=1, keepdims=True)
    here = iota((clusters, rows), 0) == ids_ref[...]
    row_position = jnp.sum(jnp.where(here, position, 0), axis=0, keepdims=True)
    pick = hot(iota((clusters, rows), 0) == row_position)
    sums_ref[...] = mm(pick, high) + mm(pick, low)
    target = hot(iota((rows, rows), 0) == so_ref[...])
    values = info_ref[...].astype(jnp.float32).astype(jnp.bfloat16)
    q_ref[...] = mm_nt(values, target).astype(jnp.int32)


def by_tile(owners, value_ref, high_ref, low_ref, start):
    size = value_ref.shape[0]
    per = size // owners
    strip = per // TILES
    for t in range(TILES):
        for p in range(owners):
            high, low = halves(value_ref[p * per + t * strip : p * per + (t + 1) * strip, :])
            to = start + (t * owners + p) * strip
            high_ref[to : to + strip, :] = high
            low_ref[to : to + strip, :] = low


def local_body(owners, chunks, *refs):
    parts = refs[:chunks]
    ids_ref, high_ref, low_ref, lid_ref = refs[chunks:]
    size = parts[0].shape[0]
    for k in range(chunks):
        by_tile(owners, parts[k], high_ref, low_ref, k * size)
    for b in range(chunks * size // LANES):
        row = ids_ref[:, b * LANES : (b + 1) * LANES].astype(jnp.float32)
        wide = jnp.transpose(jnp.broadcast_to(row, (LANES, LANES)))
        lid_ref[b * LANES : (b + 1) * LANES, :] = wide.astype(jnp.int32)


def gram_body(owners, items, last, level_ref, flag_ref, *refs):
    count = len(items)
    visitors = refs[:count]
    high_ref, low_ref, lid_ref, ids_ref, acc_ref, part_ref, acc_out, part_out = refs[count : count + 8]
    v_ref, vh_ref, vl_ref, col_ref, sem = refs[count + 8 :]
    size, _ = visitors[0].shape
    slots = high_ref.shape[0]
    tile = size // TILES
    blocks = slots // tile
    acc_out[...] = acc_ref[...]
    part_out[...] = part_ref[...]

    def fetch(n):
        return pltpu.make_async_copy(visitors[n], v_ref.at[n], sem.at[n])

    for n, (at, k) in enumerate(items):

        @pl.when(level_ref[at] >= 0)
        def _(n=n):
            fetch(n).start()

    for n, (at, k) in enumerate(items):

        @pl.when(level_ref[at] >= 0)
        def _(n=n, at=at, k=k):
            fetch(n).wait()
            by_tile(owners, v_ref.at[n], vh_ref, vl_ref, 0)
            col_ref[...] = jnp.zeros_like(col_ref)
            level = level_ref[at]
            first = level * (slots // tile) + k * TILES

            def step(i, _):
                t = i // blocks
                b = i - t * blocks

                @pl.when(flag_ref[(first + t) * blocks + b] > 0)
                def _():
                    rows = pl.ds(pl.multiple_of(b * tile, tile), tile)
                    cols = pl.ds(pl.multiple_of(t * tile, tile), tile)
                    left_h = high_ref[rows, :]
                    right_h = vh_ref[cols, :]
                    score = mm_nt(left_h, right_h) + mm_nt(left_h, vl_ref[cols, :]) + mm_nt(low_ref[rows, :], right_h)
                    lid = lid_ref[rows, :]
                    vid = ids_ref[first + t]
                    row_part = acc_out[rows, :]
                    for c in range(tile // LANES):
                        lanes = slice(c * LANES, (c + 1) * LANES)
                        weight = jnp.exp(SHARPNESS * (score[:, lanes] - 1.0))
                        weight = jnp.where(lid == vid[:, lanes], weight, 0.0)
                        row_part = row_part + weight
                        col_ref[t, :, lanes] += jnp.sum(weight.reshape(tile // 8, 8, LANES), axis=0)
                    acc_out[rows, :] = row_part

                return 0

            lax.fori_loop(0, TILES * blocks, step, 0)
            if at > 0:
                for t in range(TILES):
                    where = slice(k * size + t * tile, k * size + (t + 1) * tile)
                    part_out[pl.ds(level, 1), where] += jnp.sum(col_ref[t], axis=0, keepdims=True)

    if last:
        first, rest = halves(acc_out[...])
        second, _ = halves(acc_out[...] - first.astype(jnp.float32) - rest.astype(jnp.float32))
        ones = jnp.ones((8, LANES), jnp.bfloat16)
        total = mm_nt(ones, first) + mm_nt(ones, rest) + mm_nt(ones, second)
        part_out[pl.ds(level_ref[0], 1), :] += total[0:1, :]


def last_body(levels, owners, mass_ref, q_ref, score_ref):
    mass = mass_ref[0:owners, :]
    for z in range(1, levels):
        mass = mass + mass_ref[z * owners : (z + 1) * owners, :]
    cap = mass.shape[1]
    owner = q_ref[0:1, :]
    rank = q_ref[1:2, :]
    rows = owner.shape[1]
    at_rank = hot(iota((cap, rows), 0) == rank)
    first = mass.astype(jnp.bfloat16)
    rest = mass - first.astype(jnp.float32)
    second, third = halves(rest)
    value = mm(first, at_rank) + mm(second, at_rank) + mm(third, at_rank)
    mine = iota((owners, rows), 0) == owner
    score_ref[...] = jnp.log(jnp.sum(jnp.where(mine, value, 0.0), axis=0, keepdims=True))


def body(embeddings, cluster_ids, owner_map, source_order):
    rows, width = embeddings.shape
    clusters = owner_map.shape[0]
    levels = lax.axis_size("outer")
    inner = lax.axis_size("inner")
    groups = lax.axis_size("grp")
    owners = levels * inner
    held = clusters // owners
    cap = 2 * rows // owners
    per = cap // CHUNKS
    size = owners * per
    slots = CHUNKS * size
    ids = cluster_ids.reshape(1, rows)
    om = owner_map.reshape(clusters, 1)
    omr = owner_map.reshape(1, clusters)
    bf, i32 = jnp.bfloat16, jnp.int32

    first, high, low, info, sid = call(
        functools.partial(front_body, owners, per),
        (out((size, width)), out((rows, width), bf), out((rows, width), bf), out((8, rows), i32), out((owners, cap), i32)),
        embeddings, ids, om, omr, micros=5,
    )
    back = call(
        functools.partial(back_body, owners, per, CHUNKS, held),
        tuple(out((size, width)) for _ in range(CHUNKS - 1)) + (out((clusters, width)), out((8, rows), i32)),
        high, low, info, ids, om, omr, source_order.reshape(1, rows), micros=6,
    )
    sends = (first,) + tuple(back[: CHUNKS - 1])
    sums, q_info = back[CHUNKS - 1 :]

    tile = size // TILES
    strip = per // TILES
    blocks = slots // tile

    def to_owner(value):
        got = lax.all_to_all(value.reshape(owners, per, width), PLANE, 0, 0, tiled=True)
        return got.reshape(size, width)

    all_ids = lax.all_to_all(jnp.tile(sid, (levels, 1)), BY_LEVEL, 0, 0, tiled=True)
    mine = []
    for k in range(CHUNKS):
        send = sends[k] if k == 0 else lax.optimization_barrier((sends[k], mine[-1]))[0]
        mine.append(to_owner(send))
    all_ids = all_ids.reshape(levels, owners, CHUNKS, TILES, strip).transpose(0, 2, 3, 1, 4)
    all_ids = all_ids.reshape(levels * blocks, 1, tile)

    level = lax.axis_index("outer")
    down = lax.axis_index("inner") % 2
    seat = jnp.where(down == 1, levels - 1 - level, level)

    def pairs(moves):
        found = []
        for lane in range(inner):
            for a, b in moves:
                if lane % 2:
                    a, b = levels - 1 - a, levels - 1 - b
                found.append((a * inner + lane, b * inner + lane))
        return found

    top = levels - 1
    moves = []
    for s in range(1, top + 1):
        moves.append([(a, a + 1) for a in range(s - 1, top) if not (s == 1 and a == top - 1)])
    back_move = [(top, top - 1)]

    arrived = {}
    for k in range(CHUNKS):
        value = mine[k]
        for s in range(1, top + 1):
            value = lax.ppermute(value, LINE, pairs(moves[s - 1]))
            arrived[s, k] = value
        arrived["b", k] = lax.ppermute(mine[k], LINE, pairs(back_move))

    keys = [1, "b"] + list(range(2, top + 1))

    def source_seat(key):
        if key == "b":
            return jnp.where(seat == top - 1, top, -1)
        got = seat >= key
        if key == 1:
            got = got & (seat < top)
        return jnp.where(got, seat - key, -1)

    seats = [seat] + [source_seat(key) for key in keys]
    level_of = jnp.stack([jnp.where(a < 0, -1, jnp.where(down == 1, top - a, a)) for a in seats]).astype(i32)
    low_id = jnp.min(jnp.where(all_ids < 0, clusters, all_ids), axis=(1, 2))
    high_id = jnp.max(all_ids, axis=(1, 2))
    own_ids = lax.dynamic_slice_in_dim(all_ids, level * blocks, blocks, 0)
    own_low = lax.dynamic_slice_in_dim(low_id, level * blocks, blocks, 0)
    own_high = lax.dynamic_slice_in_dim(high_id, level * blocks, blocks, 0)
    flags = (low_id[:, None] <= own_high[None, :]) & (own_low[None, :] <= high_id[:, None])
    flags = flags.astype(i32).reshape(-1)
    lh, ll, lid = call(
        functools.partial(local_body, owners, CHUNKS),
        (out((slots, width), bf), out((slots, width), bf), out((slots, LANES), i32)),
        *mine, own_ids.reshape(1, slots), micros=5,
    )

    def finish(sums):
        piece = lax.all_to_all(sums.reshape(owners, held, width), PLANE, 0, 0, tiled=True)
        piece = jnp.sum(piece, axis=0)
        total = None
        for s in range(groups):
            route = [(g * levels + z, ((z + s) % groups) * levels + g) for g in range(groups) for z in range(levels)]
            got = lax.ppermute(piece, ("grp", "outer"), route)
            total = got if total is None else total + got
        return total * lax.rsqrt(jnp.mean(total * total, axis=1, keepdims=True) + 1e-6)

    centroids = finish(lax.optimization_barrier((sums, mine[0]))[0])
    acc = jnp.zeros((slots, LANES), jnp.float32)
    part = jnp.zeros((levels, slots), jnp.float32)

    def gram(acc, part, items, after, last, micros):
        flag = flags
        for value in after:
            flag = lax.optimization_barrier((flag, value))[0]
        visitors = [mine[k] if key == "own" else arrived[key, k] for key, k in items]
        at = tuple((0 if key == "own" else 1 + keys.index(key), k) for key, k in items)
        count = len(items)
        vm = pl.BlockSpec(memory_space=VMEM)
        return pl.pallas_call(
            functools.partial(gram_body, owners, at, last),
            out_shape=(out((slots, LANES)), out((levels, slots))),
            in_specs=[pl.BlockSpec(memory_space=pltpu.SMEM)] * 2 + [pl.BlockSpec(memory_space=pl.ANY)] * count + [vm] * 6,
            out_specs=(vm, vm),
            scratch_shapes=[
                VMEM((count, size, width), jnp.float32),
                VMEM((size, width), bf),
                VMEM((size, width), bf),
                VMEM((TILES, 8, tile), jnp.float32),
                pltpu.SemaphoreType.DMA((count,)),
            ],
            cost_estimate=cost(micros),
            name="gram",
        )(level_of, flag, *visitors, lh, ll, lid, all_ids, acc, part)

    plan = [
        ([("own", k) for k in range(CHUNKS)], [(1, 1), (2, 0)], 10),
        ([(1, 0), ("b", 0), (2, 0), (1, 1)], [(1, 2), (2, 1)], 12),
        ([("b", 1), (2, 1), (1, 2), ("b", 2), (3, 0)], [(2, 2)], 12),
        ([(2, 2), (3, 1)], [], 7),
        ([(3, 2)], [], 5),
    ]
    for n, (items, after, micros) in enumerate(plan):
        last = n == len(plan) - 1
        acc, part = gram(acc, part, items, [], last, micros)
    parts = part.reshape(levels, CHUNKS, TILES, owners, strip).transpose(0, 3, 1, 2, 4).reshape(levels * owners, cap)
    home = lax.all_to_all(parts, BY_LEVEL, 0, 0, tiled=True)
    score = call(functools.partial(last_body, levels, owners), out((1, rows)), home, q_info, micros=2)

    return score.reshape(rows), centroids


def solution(mesh):
    groups, owned = mesh.shape["grp"], mesh.shape["own"]
    split = Mesh(mesh.devices.reshape(groups, groups, owned // groups), EVERY)
    return jax.shard_map(
        body,
        mesh=split,
        in_specs=(P(EVERY, None), P(EVERY), P(), P(EVERY)),
        out_specs=(P(EVERY), P(LINE, None)),
        check_vma=False,
    )
```

time: 414 us -> 278 us (0.67)
  waiting for transfers between devices: 232 us -> 74.2 us
  matrix products: 100 us -> 0 us
  starting transfers between devices: 17.5 us -> 113 us
  Pallas kernels: 0 us -> 50.1 us
  between operations: 14.3 us -> 0.93 us
  other arithmetic: 16.1 us -> 3.4 us
  blocking collectives: 18.5 us -> 24.4 us
    ppermute x5 -> x16, waiting for transfers between devices: 117 us -> 8.25 us  [the longest x4 8.22 us: finish(): got = lax.ppermute(piece, ('grp', 'outer'), route)]
    dot_general x10 -> x0, matrix products: 100 us -> none  [the longest x9 98.5 us: masked_weights(): jnp.einsum('id,jd->ij', left_rows, right_rows, preferred_element_type=jnp...]
    all_to_all x3 -> x5, starting transfers between devices: 13.2 us -> 73.4 us  [the longest x1 54 us: body(): home = lax.all_to_all(parts, BY_LEVEL, 0, 0, tiled=True)]
    pallas_call x0 -> x9, Pallas kernels: none -> 50.1 us  [the longest x5 32.3 us: gram(): pl.pallas_call(functools.partial(gram_body, owners, at, last), out_shape=...]
    all_to_all x3 -> x5, waiting for transfers between devices: 116 us -> 66 us  [the longest x1 31.8 us: body(): lax.all_to_all(jnp.tile(sid, (levels, 1)), BY_LEVEL, 0, 0, tiled=True)]
    ppermute x5 -> x16, starting transfers between devices: 4.3 us -> 39.1 us  [the longest x9 25.1 us: body(): value = lax.ppermute(value, LINE, pairs(moves[s - 1]))]
    all_to_all x0 -> x1, blocking collectives: none -> 24.4 us  [to_owner(): lax.all_to_all(value.reshape(owners, per, width), PLANE, 0, 0, tiled=True)]
    psum x1 -> x0, blocking collectives: 18.5 us -> none  [local(): cluster_sums = lax.psum(partial_value, 'grp')]
  transfers between devices with their start and end apart: 9 -> 21, of which waited for: 5 -> 7; matrix products, arithmetic and copies ran while one was open for 26% -> 2% of each run, Pallas kernels for 0% -> 14%
where the time goes in v1:
time: 278 us; the launch traced here: 277 us
  starting transfers between devices  113 us (41%)
  waiting for transfers between devices  74.2 us (27%)
  Pallas kernels  50.1 us (18%)
  blocking collectives  24.4 us (9%)
  local copies, waits for them, and re-layouts  11.4 us (4%)
  other arithmetic  3.4 us (1%)
    all_to_all x1, starting transfers between devices, body(): home = lax.all_to_all(parts, BY_LEVEL, 0, 0, tiled=True)  54 us
    pallas_call x5, Pallas kernels, gram(): pl.pallas_call(functools.partial(gram_body, owners, at, last), out_shape=...  32.3 us
    all_to_all x1, waiting for transfers between devices, body(): lax.all_to_all(jnp.tile(sid, (levels, 1)), BY_LEVEL, 0, 0, tiled=True)  31.8 us
    all_to_all x2, waiting for transfers between devices, to_owner(): lax.all_to_all(value.reshape(owners, per, width), PLANE, 0, 0, tiled=True)  27.6 us
    ppermute x9, starting transfers between devices, body(): value = lax.ppermute(value, LINE, pairs(moves[s - 1]))  25.1 us
    all_to_all x1, blocking collectives, to_owner(): lax.all_to_all(value.reshape(owners, per, width), PLANE, 0, 0, tiled=True)  24.4 us
    pallas_call x4, Pallas kernels, call(): pl.pallas_call(body, out_shape=outs, in_specs=spec, out_specs=jax.tree.ma...  17.8 us
    all_to_all x2, starting transfers between devices, to_owner(): lax.all_to_all(value.reshape(owners, per, width), PLANE, 0, 0, tiled=True)  9.04 us
  transfers between devices with their start and end apart: 21, of which 7 were waited for; matrix products, arithmetic and copies ran while one was open for 2% of the time, Pallas kernels for 14%

profile of v1, /device:TPU:0, one launch (start us, length us, event | category | flops | bytes accessed | tf_op | source)
XLA Modules:
  0.0 277.0 jit_solution(13098871839954684030)
XLA Ops:
  3.3 5.1 %shard_map.59 = (f32[512,768]{1,0:T(8,128)}, bf16[768,768]{1,0:T(8,128)(2,1)}, bf16[768,768]{1,0:T(8,128)(2,1)}, s32[8,768]{1,0:T(8,128)}, s32[8,192]{1,0:T(8,128)}) custom-call(f32[768,768]{1,0:T(8,128)} %x_ref.1, s32[1,768]{1,0:T(1,128)} %reshape.96.ids_ref, s32[128,1]{1,0:T(8,128)} %copy.13.om_ref, s32[1,128]{1,0:T(1,128)} %bitcast.45), custom_call_target="tpu_custom_call" | custom-call | flops 5500000256 | tf_op jit(solution)/shard_map/pallas_call | solution.py:53
  8.4 5.3 %all-to-all-start.1 = ((f32[8,64,768]{2,1,0:T(8,128)}), f32[8,64,768]{2,1,0:T(8,128)S(1)}, u32[]{:S(2)}, u32[]{:S(2)}) async-start(f32[8,64,768]{2,1,0:T(8,128)} %bitcast.37), calls=%async_computation.1 | async-start | bytes 3145728 | tf_op jit(solution)/shard_map/all_to_all | solution.py:277
  14.3 5.6 %shard_map.60 = (f32[512,768]{1,0:T(8,128)}, f32[512,768]{1,0:T(8,128)}, f32[128,768]{1,0:T(8,128)}, s32[8,768]{1,0:T(8,128)}) custom-call(bf16[768,768]{1,0:T(8,128)(2,1)} %get-tuple-element.27.high_ref, bf16[768,768]{1,0:T(8,128)(2,1)} %get-tuple-element.28.low_ref, s32[8,768]{1,0:T(8,128)} %get-tuple-element.29.info_ref, s32[1,768]{1,0:T(1,128)} %reshape.96.ids_ref, ...), custom_call_target="tpu_custom_call" | custom-call | flops 6600000000 | tf_op jit(solution)/shard_map/pallas_call | solution.py:53
  19.9 14.8 %all-to-all-done.1 = f32[8,64,768]{2,1,0:T(8,128)S(1)} async-done(((f32[8,64,768]{2,1,0:T(8,128)}), f32[8,64,768]{2,1,0:T(8,128)S(1)}, u32[]{:S(2)}, u32[]{:S(2)}) %all-to-all-start.1) | async-done | bytes 1572896 | tf_op jit(solution)/shard_map/all_to_all | solution.py:277
  35.9 24.4 %all_to_all.40 = f32[8,64,768]{2,1,0:T(8,128)S(1)} all-to-all(f32[8,64,768]{2,1,0:T(8,128)} %bitcast.38), channel_id=1, replica_groups=mesh['grp'=4,'outer'=4,'inner'=2] {'grp','inner'}, dimensions={0} | all-to-all | bytes 3145728 | tf_op jit(solution)/shard_map/all_to_all | solution.py:277
  60.3 3.7 %all-to-all-start.3 = ((f32[8,64,768]{2,1,0:T(8,128)}), f32[8,64,768]{2,1,0:T(8,128)S(1)}, u32[]{:S(2)}, u32[]{:S(2)}) async-start(f32[8,64,768]{2,1,0:T(8,128)} %bitcast.36), calls=%async_computation.3 | async-start | bytes 3145728 | tf_op jit(solution)/shard_map/all_to_all | solution.py:277
  64.1 4.7 %collective-permute-start.8 = (f32[512,768]{1,0:T(8,128)}, f32[512,768]{1,0:T(8,128)}, u32[]{:S(2)}, u32[]{:S(2)}) collective-permute-start(f32[512,768]{1,0:T(8,128)} %bitcast.32), channel_id=1, source_target_pairs={{0,2},{2,4},{7,5},{5,3},{8,10},{10,12},{15,13},{13,11},{16,18},{18... | collective-permute-start | bytes 4718600 | tf_op jit(solution)/shard_map/ppermute | solution.py:311
  68.7 3.5 %collective-permute-start.3 = (f32[512,768]{1,0:T(8,128)S(1)}, f32[512,768]{1,0:T(8,128)}, u32[]{:S(2)}, u32[]{:S(2)}) collective-permute-start(f32[512,768]{1,0:T(8,128)S(1)} %bitcast.28), channel_id=1, source_target_pairs={{0,2},{2,4},{7,5},{5,3},{8,10},{10,12},{15,13},{13,11},{16,18},{18... | collective-permute-start | bytes 4718600 | tf_op jit(solution)/shard_map/ppermute | solution.py:311
  72.2 12.8 %all-to-all-done.3 = f32[8,64,768]{2,1,0:T(8,128)S(1)} async-done(((f32[8,64,768]{2,1,0:T(8,128)}), f32[8,64,768]{2,1,0:T(8,128)S(1)}, u32[]{:S(2)}, u32[]{:S(2)}) %all-to-all-start.3) | async-done | bytes 1572896 | tf_op jit(solution)/shard_map/all_to_all | solution.py:277
  85.0 3.5 %all-to-all-start.5 = ((f32[8,16,768]{2,1,0:T(8,128)}), f32[8,16,768]{2,1,0:T(8,128)S(1)}, u32[]{:S(2)}, u32[]{:S(2)}) async-start(f32[8,16,768]{2,1,0:T(8,128)} %bitcast.40), calls=%async_computation.5 | async-start | bytes 786432 | tf_op jit(solution)/shard_map/all_to_all | solution.py:341
  88.4 1.8 collective-permute-start.11
  90.3 1.9 collective-permute-start.9
  92.2 7.0 %collective-permute-start = (f32[512,768]{1,0:T(8,128)S(1)}, f32[512,768]{1,0:T(8,128)}, u32[]{:S(2)}, u32[]{:S(2)}) collective-permute-start(f32[512,768]{1,0:T(8,128)S(1)} %bitcast.24), channel_id=1, source_target_pairs={{0,2},{2,4},{7,5},{5,3},{8,10},{10,12},{15,13},{13,11},{16,18},{18... | collective-permute-start | bytes 4718600 | tf_op jit(solution)/shard_map/ppermute | solution.py:311
  101.9 6.9 %all-to-all-start = ((s32[32,1,192]{2,1,0:T(1,128)}), s32[32,1,192]{2,1,0:T(1,128)S(1)}, u32[]{:S(2)}, u32[]{:S(2)}) async-start(s32[32,1,192]{2,1,0:T(1,128)} %all_to_all.25), calls=%async_computation | async-start | bytes 65536 | tf_op jit(solution)/shard_map/all_to_all | solution.py:280
  109.6 31.8 %all-to-all-done = s32[32,1,192]{2,1,0:T(1,128)S(1)} async-done(((s32[32,1,192]{2,1,0:T(1,128)}), s32[32,1,192]{2,1,0:T(1,128)S(1)}, u32[]{:S(2)}, u32[]{:S(2)}) %all-to-all-start) | async-done | bytes 24608 | tf_op jit(solution)/shard_map/all_to_all | solution.py:280
  143.8 4.5 %collective-permute-done.13 = f32[16,768]{1,0:T(8,128)S(1)} collective-permute-done((f32[16,768]{1,0:T(8,128)}, f32[16,768]{1,0:T(8,128)S(1)}, u32[]{:S(2)}, u32[]{:S(2)}) %collective-permute-start.13) | collective-permute-done | bytes 49184 | tf_op jit(solution)/shard_map/ppermute | solution.py:346
  148.3 2.1 collective-permute-start.14
  150.6 2.9 %collective-permute-done.14 = f32[16,768]{1,0:T(8,128)S(1)} collective-permute-done((f32[16,768]{1,0:T(8,128)}, f32[16,768]{1,0:T(8,128)S(1)}, u32[]{:S(2)}, u32[]{:S(2)}) %collective-permute-start.14) | collective-permute-done | bytes 49184 | tf_op jit(solution)/shard_map/ppermute | solution.py:346
  153.5 3.7 %collective-permute-start.15 = (f32[16,768]{1,0:T(8,128)}, f32[16,768]{1,0:T(8,128)S(1)}, u32[]{:S(2)}, u32[]{:S(2)}) collective-permute-start(f32[16,768]{1,0:T(8,128)} %reduce_sum.18), channel_id=1, source_target_pairs={{0,24},{2,0},{4,8},{6,16},{8,26},{10,2},{12,10},{14,18},{16,28},{1... | collective-permute-start | bytes 147464 | tf_op jit(solution)/shard_map/ppermute | solution.py:346
  159.4 1.8 collective-permute-start.4
  163.0 5.5 %shard_map.61 = (bf16[1536,768]{1,0:T(8,128)(2,1)}, bf16[1536,768]{1,0:T(8,128)(2,1)}, s32[1536,128]{1,0:T(8,128)}) custom-call(f32[512,768]{1,0:T(8,128)} %bitcast.34, f32[512,768]{1,0:T(8,128)} %bitcast.30, f32[512,768]{1,0:T(8,128)} %bitcast.25, s32[1,1536]{1,0:T(1,128)} %bitcast.43), custom_call_target="tpu_custom_call" | custom-call | flops 5500000256 | tf_op jit(solution)/shard_map/pallas_call | solution.py:53
  168.5 1.9 collective-permute-start.7
  170.4 1.8 collective-permute-start.10
  174.6 16.7 %gram.5 = (f32[1536,128]{1,0:T(8,128)}, f32[4,1536]{1,0:T(4,128)}) custom-call(s32[5]{0:T(128)} %stack.23.level_ref, s32[144]{0:T(256)} %reshape.112.flag_ref, f32[512,768]{1,0:T(8,128)} %bitcast.35, f32[512,768]{1,0:T(8,128)} %bitcast.31, f32[512,768]{1,0:T(8,128)} %bitcast.27, bf16[1536,768]{1,0:T(8,128)(2,1)} %get-tuple-element.35.refs_3_.refs_4_.refs_5_.refs_2_.refs_1_, ...), custom_call_target="tpu_custom_call" | custom-call | flops 11000000512 | tf_op jit(solution)/shard_map/gram/pallas_call | solution.py:362
  191.4 1.8 collective-permute-start.5
  193.2 4.0 %gram.6 = (f32[1536,128]{1,0:T(8,128)}, f32[4,1536]{1,0:T(4,128)}) custom-call(s32[5]{0:T(128)} %stack.23.level_ref, s32[144]{0:T(256)} %reshape.112.flag_ref, f32[512,768]{1,0:T(8,128)} %collective-permute-done.8.refs_0_, f32[512,768]{1,0:T(8,128)} %collective-permute-done.11.refs_1_, f32[512,768]{1,0:T(8,128)} %collective-permute-done.9.refs_2_, ...), custom_call_target="tpu_custom_call" | custom-call | flops 13200000000 | tf_op jit(solution)/shard_map/gram/pallas_call | solution.py:362
  197.3 1.8 collective-permute-start.2
  199.1 3.8 %gram.7 = (f32[1536,128]{1,0:T(8,128)}, f32[4,1536]{1,0:T(4,128)}) custom-call(s32[5]{0:T(128)} %stack.23.level_ref, s32[144]{0:T(256)} %reshape.112.flag_ref, f32[512,768]{1,0:T(8,128)} %collective-permute-done.6.refs_0_, f32[512,768]{1,0:T(8,128)} %collective-permute-done.4.refs_1_, f32[512,768]{1,0:T(8,128)} %collective-permute-done.refs_2_, ...), custom_call_target="tpu_custom_call" | custom-call | flops 13200000000 | tf_op jit(solution)/shard_map/gram/pallas_call | solution.py:362
  202.9 3.8 %gram.8 = (f32[1536,128]{1,0:T(8,128)}, f32[4,1536]{1,0:T(4,128)}) custom-call(s32[5]{0:T(128)} %stack.23.level_ref, s32[144]{0:T(256)} %reshape.112.flag_ref, f32[512,768]{1,0:T(8,128)} %copy-done.6, f32[512,768]{1,0:T(8,128)} %collective-permute-done.5.refs_1_, bf16[1536,768]{1,0:T(8,128)(2,1)} %get-tuple-element.35.refs_3_.refs_4_.refs_5_.refs_2_.refs_1_, ...), custom_call_target="tpu_custom_call" | custom-call | flops 7699999744 | tf_op jit(solution)/shard_map/gram/pallas_call | solution.py:362
  206.8 3.9 %gram.9 = (f32[1536,128]{1,0:T(8,128)}, f32[4,1536]{1,0:T(4,128)}) custom-call(s32[5]{0:T(128)} %stack.23.level_ref, s32[144]{0:T(256)} %reshape.112.flag_ref, f32[512,768]{1,0:T(8,128)} %collective-permute-done.2.refs_0_, bf16[1536,768]{1,0:T(8,128)(2,1)} %get-tuple-element.35.refs_3_.refs_4_.refs_5_.refs_2_.refs_1_, ...), custom_call_target="tpu_custom_call" | custom-call | flops 5500000256 | tf_op jit(solution)/shard_map/gram/pallas_call | solution.py:362
  212.3 54.0 %all-to-all-start.4 = ((f32[32,1,192]{2,1,0:T(1,128)}), f32[32,1,192]{2,1,0:T(1,128)S(1)}, u32[]{:S(2)}, u32[]{:S(2)}) async-start(f32[32,1,192]{2,1,0:T(1,128)} %all_to_all.30), calls=%async_computation.4 | async-start | bytes 65536 | tf_op jit(solution)/shard_map/all_to_all | solution.py:389
  267.0 6.6 %all-to-all-done.4 = f32[32,1,192]{2,1,0:T(1,128)S(1)} async-done(((f32[32,1,192]{2,1,0:T(1,128)}), f32[32,1,192]{2,1,0:T(1,128)S(1)}, u32[]{:S(2)}, u32[]{:S(2)}) %all-to-all-start.4) | async-done | bytes 24608 | tf_op jit(solution)/shard_map/all_to_all | solution.py:389
  (63 shorter events, 22.6 us)
Async XLA Ops:
  8.4 5.3 %copy-start.5 = (s32[768]{0:T(1024)S(1)}, s32[768]{0:T(1024)}, u32[]{:S(2)}) copy-start(s32[768]{0:T(1024)} %param.7) | copy-start | bytes 9220
  8.4 26.3 %all-to-all-start.1 = ((f32[8,64,768]{2,1,0:T(8,128)}), f32[8,64,768]{2,1,0:T(8,128)S(1)}, u32[]{:S(2)}, u32[]{:S(2)}) async-start(f32[8,64,768]{2,1,0:T(8,128)} %bitcast.37), calls=%async_computation.1 | async-start | bytes 3145728 | tf_op jit(solution)/shard_map/all_to_all | solution.py:277
  34.7 1.2 copy-start.2
  60.3 100.9 %copy-start.1 = (f32[8,64,768]{2,1,0:T(8,128)}, f32[8,64,768]{2,1,0:T(8,128)S(1)}, u32[]{:S(2)}) copy-start(f32[8,64,768]{2,1,0:T(8,128)S(1)} %all_to_all.40) | copy-start | bytes 4718596
  60.3 40.9 %copy-start.4 = (s32[8,192]{1,0:T(8,128)S(1)}, s32[8,192]{1,0:T(8,128)}, u32[]{:S(2)}) copy-start(s32[8,192]{1,0:T(8,128)} %get-tuple-element.26) | copy-start | bytes 18436
  60.3 24.6 %all-to-all-start.3 = ((f32[8,64,768]{2,1,0:T(8,128)}), f32[8,64,768]{2,1,0:T(8,128)S(1)}, u32[]{:S(2)}, u32[]{:S(2)}) async-start(f32[8,64,768]{2,1,0:T(8,128)} %bitcast.36), calls=%async_computation.3 | async-start | bytes 3145728 | tf_op jit(solution)/shard_map/all_to_all | solution.py:277
  64.1 26.2 %collective-permute-start.8 = (f32[512,768]{1,0:T(8,128)}, f32[512,768]{1,0:T(8,128)}, u32[]{:S(2)}, u32[]{:S(2)}) collective-permute-start(f32[512,768]{1,0:T(8,128)} %bitcast.32), channel_id=1, source_target_pairs={{0,2},{2,4},{7,5},{5,3},{8,10},{10,12},{15,13},{13,11},{16,18},{18... | collective-permute-start | bytes 4718600 | tf_op jit(solution)/shard_map/ppermute | solution.py:311
  68.7 90.7 %collective-permute-start.3 = (f32[512,768]{1,0:T(8,128)S(1)}, f32[512,768]{1,0:T(8,128)}, u32[]{:S(2)}, u32[]{:S(2)}) collective-permute-start(f32[512,768]{1,0:T(8,128)S(1)} %bitcast.28), channel_id=1, source_target_pairs={{0,2},{2,4},{7,5},{5,3},{8,10},{10,12},{15,13},{13,11},{16,18},{18... | collective-permute-start | bytes 4718600 | tf_op jit(solution)/shard_map/ppermute | solution.py:311
  85.0 78.1 %copy-start = (f32[8,64,768]{2,1,0:T(8,128)}, f32[8,64,768]{2,1,0:T(8,128)S(1)}, u32[]{:S(2)}) copy-start(f32[8,64,768]{2,1,0:T(8,128)S(1)} %all-to-all-done.3) | copy-start | bytes 4718596
  85.0 14.2 %all-to-all-start.5 = ((f32[8,16,768]{2,1,0:T(8,128)}), f32[8,16,768]{2,1,0:T(8,128)S(1)}, u32[]{:S(2)}, u32[]{:S(2)}) async-start(f32[8,16,768]{2,1,0:T(8,128)} %bitcast.40), calls=%async_computation.5 | async-start | bytes 786432 | tf_op jit(solution)/shard_map/all_to_all | solution.py:341
  88.4 80.1 %collective-permute-start.11 = (f32[512,768]{1,0:T(8,128)}, f32[512,768]{1,0:T(8,128)}, u32[]{:S(2)}, u32[]{:S(2)}) collective-permute-start(f32[512,768]{1,0:T(8,128)} %bitcast.33), channel_id=1, source_target_pairs={{6,4},{1,3},{14,12},{9,11},{22,20},{17,19},{30,28},{25,27}} | collective-permute-start | bytes 4718600 | tf_op jit(solution)/shard_map/ppermute | solution.py:313
  90.3 80.1 %collective-permute-start.9 = (f32[512,768]{1,0:T(8,128)}, f32[512,768]{1,0:T(8,128)}, u32[]{:S(2)}, u32[]{:S(2)}) collective-permute-start(f32[512,768]{1,0:T(8,128)} %collective-permute-done.8.refs_0_), channel_id=1, source_target_pairs={{2,4},{4,6},{5,3},{3,1},{10,12},{12,14},{13,11},{11,9},{18,20},{20... | collective-permute-start | bytes 4718600 | tf_op jit(solution)/shard_map/ppermute | solution.py:311
  92.2 80.0 %collective-permute-start = (f32[512,768]{1,0:T(8,128)S(1)}, f32[512,768]{1,0:T(8,128)}, u32[]{:S(2)}, u32[]{:S(2)}) collective-permute-start(f32[512,768]{1,0:T(8,128)S(1)} %bitcast.24), channel_id=1, source_target_pairs={{0,2},{2,4},{7,5},{5,3},{8,10},{10,12},{15,13},{13,11},{16,18},{18... | collective-permute-start | bytes 4718600 | tf_op jit(solution)/shard_map/ppermute | solution.py:311
  99.8 41.8 %collective-permute-start.12 = (f32[16,768]{1,0:T(8,128)}, f32[16,768]{1,0:T(8,128)S(1)}, u32[]{:S(2)}, u32[]{:S(2)}) collective-permute-start(f32[16,768]{1,0:T(8,128)} %reduce_sum.18), channel_id=1, source_target_pairs={{0,0},{2,8},{4,16},{6,24},{8,2},{10,10},{12,18},{14,26},{16,4},{18... | collective-permute-start | bytes 147464 | tf_op jit(solution)/shard_map/ppermute | solution.py:346
  101.9 39.5 %all-to-all-start = ((s32[32,1,192]{2,1,0:T(1,128)}), s32[32,1,192]{2,1,0:T(1,128)S(1)}, u32[]{:S(2)}, u32[]{:S(2)}) async-start(s32[32,1,192]{2,1,0:T(1,128)} %all_to_all.25), calls=%async_computation | async-start | bytes 65536 | tf_op jit(solution)/shard_map/all_to_all | solution.py:280
  141.6 6.6 %collective-permute-start.13 = (f32[16,768]{1,0:T(8,128)}, f32[16,768]{1,0:T(8,128)S(1)}, u32[]{:S(2)}, u32[]{:S(2)}) collective-permute-start(f32[16,768]{1,0:T(8,128)} %reduce_sum.18), channel_id=1, source_target_pairs={{0,8},{2,16},{4,24},{6,0},{8,10},{10,18},{12,26},{14,2},{16,12},{1... | collective-permute-start | bytes 147464 | tf_op jit(solution)/shard_map/ppermute | solution.py:346
  148.3 5.2 %collective-permute-start.14 = (f32[16,768]{1,0:T(8,128)}, f32[16,768]{1,0:T(8,128)S(1)}, u32[]{:S(2)}, u32[]{:S(2)}) collective-permute-start(f32[16,768]{1,0:T(8,128)} %reduce_sum.18), channel_id=1, source_target_pairs={{0,16},{2,24},{4,0},{6,8},{8,18},{10,26},{12,2},{14,10},{16,20},{1... | collective-permute-start | bytes 147464 | tf_op jit(solution)/shard_map/ppermute | solution.py:346
  150.6 18.0 %copy-start.3 = (s32[24,1,256]{2,1,0:T(1,128)}, s32[24,1,256]{2,1,0:T(1,128)S(1)}, u32[]{:S(2)}) copy-start(s32[24,1,256]{2,1,0:T(1,128)S(1)} %reshape.107.refs_6_.refs_7_.refs_8_.refs_5_.refs_4_) | copy-start | bytes 73732
  153.5 5.8 %collective-permute-start.15 = (f32[16,768]{1,0:T(8,128)}, f32[16,768]{1,0:T(8,128)S(1)}, u32[]{:S(2)}, u32[]{:S(2)}) collective-permute-start(f32[16,768]{1,0:T(8,128)} %reduce_sum.18), channel_id=1, source_target_pairs={{0,24},{2,0},{4,8},{6,16},{8,26},{10,2},{12,10},{14,18},{16,28},{1... | collective-permute-start | bytes 147464 | tf_op jit(solution)/shard_map/ppermute | solution.py:346
  159.4 32.0 %collective-permute-start.4 = (f32[512,768]{1,0:T(8,128)}, f32[512,768]{1,0:T(8,128)}, u32[]{:S(2)}, u32[]{:S(2)}) collective-permute-start(f32[512,768]{1,0:T(8,128)} %collective-permute-done.3.refs_3_), channel_id=1, source_target_pairs={{2,4},{4,6},{5,3},{3,1},{10,12},{12,14},{13,11},{11,9},{18,20},{20... | collective-permute-start | bytes 4718600 | tf_op jit(solution)/shard_map/ppermute | solution.py:311
  161.2 37.8 %collective-permute-start.6 = (f32[512,768]{1,0:T(8,128)S(1)}, f32[512,768]{1,0:T(8,128)}, u32[]{:S(2)}, u32[]{:S(2)}) collective-permute-start(f32[512,768]{1,0:T(8,128)S(1)} %bitcast.29), channel_id=1, source_target_pairs={{6,4},{1,3},{14,12},{9,11},{22,20},{17,19},{30,28},{25,27}} | collective-permute-start | bytes 4718600 | tf_op jit(solution)/shard_map/ppermute | solution.py:313
  168.5 30.5 %collective-permute-start.7 = (f32[512,768]{1,0:T(8,128)}, f32[512,768]{1,0:T(8,128)}, u32[]{:S(2)}, u32[]{:S(2)}) collective-permute-start(f32[512,768]{1,0:T(8,128)} %bitcast.26), channel_id=1, source_target_pairs={{6,4},{1,3},{14,12},{9,11},{22,20},{17,19},{30,28},{25,27}} | collective-permute-start | bytes 4718600 | tf_op jit(solution)/shard_map/ppermute | solution.py:313
  170.4 28.7 %collective-permute-start.10 = (f32[512,768]{1,0:T(8,128)}, f32[512,768]{1,0:T(8,128)}, u32[]{:S(2)}, u32[]{:S(2)}) collective-permute-start(f32[512,768]{1,0:T(8,128)} %collective-permute-done.9.refs_2_), channel_id=1, source_target_pairs={{4,6},{3,1},{12,14},{11,9},{20,22},{19,17},{28,30},{27,25}} | collective-permute-start | bytes 4718600 | tf_op jit(solution)/shard_map/ppermute | solution.py:311
  172.2 25.0 %collective-permute-start.1 = (f32[512,768]{1,0:T(8,128)}, f32[512,768]{1,0:T(8,128)S(1)}, u32[]{:S(2)}, u32[]{:S(2)}) collective-permute-start(f32[512,768]{1,0:T(8,128)} %collective-permute-done.refs_2_), channel_id=1, source_target_pairs={{2,4},{4,6},{5,3},{3,1},{10,12},{12,14},{13,11},{11,9},{18,20},{20... | collective-permute-start | bytes 4718600 | tf_op jit(solution)/shard_map/ppermute | solution.py:311
  191.4 11.6 %collective-permute-start.5 = (f32[512,768]{1,0:T(8,128)}, f32[512,768]{1,0:T(8,128)}, u32[]{:S(2)}, u32[]{:S(2)}) collective-permute-start(f32[512,768]{1,0:T(8,128)} %collective-permute-done.4.refs_1_), channel_id=1, source_target_pairs={{4,6},{3,1},{12,14},{11,9},{20,22},{19,17},{28,30},{27,25}} | collective-permute-start | bytes 4718600 | tf_op jit(solution)/shard_map/ppermute | solution.py:311
  197.2 5.7 %copy-start.6 = (f32[512,768]{1,0:T(8,128)}, f32[512,768]{1,0:T(8,128)S(1)}, u32[]{:S(2)}) copy-start(f32[512,768]{1,0:T(8,128)S(1)} %collective-permute-done.1.refs_0_) | copy-start | bytes 4718596
  197.3 9.5 %collective-permute-start.2 = (f32[512,768]{1,0:T(8,128)S(1)}, f32[512,768]{1,0:T(8,128)}, u32[]{:S(2)}, u32[]{:S(2)}) collective-permute-start(f32[512,768]{1,0:T(8,128)S(1)} %collective-permute-done.1.refs_0_), channel_id=1, source_target_pairs={{4,6},{3,1},{12,14},{11,9},{20,22},{19,17},{28,30},{27,25}} | collective-permute-start | bytes 4718600 | tf_op jit(solution)/shard_map/ppermute | solution.py:311
  212.3 61.2 %all-to-all-start.4 = ((f32[32,1,192]{2,1,0:T(1,128)}), f32[32,1,192]{2,1,0:T(1,128)S(1)}, u32[]{:S(2)}, u32[]{:S(2)}) async-start(f32[32,1,192]{2,1,0:T(1,128)} %all_to_all.30), calls=%async_computation.4 | async-start | bytes 65536 | tf_op jit(solution)/shard_map/all_to_all | solution.py:389

commit v2 on v1

v2 whole, which is shorter than its diff:
```python
import functools
import math

import jax
import jax.numpy as jnp
from jax import lax
from jax.experimental import pallas as pl
from jax.experimental.pallas import tpu as pltpu
from jax.sharding import Mesh
from jax.sharding import PartitionSpec as P


SHARPNESS = 6.0
SCALE = (SHARPNESS * 1.4426950408889634) ** 0.5
CHUNKS = 3
TILES = 2
LANES = 128
VMEM = pltpu.VMEM
EVERY = ("grp", "outer", "inner")
PLANE = ("grp", "inner")
LINE = ("outer", "inner")
BY_LEVEL = ("outer", "grp", "inner")
NT = (((1,), (1,)), ((), ()))


def iota(shape, axis):
    return lax.broadcasted_iota(jnp.int32, shape, axis)


def mm(left, right):
    return jnp.dot(left, right, preferred_element_type=jnp.float32)


def mm_nt(left, right):
    return lax.dot_general(left, right, NT, preferred_element_type=jnp.float32)


def halves(value):
    high = value.astype(jnp.bfloat16)
    low = (value - high.astype(jnp.float32)).astype(jnp.bfloat16)
    return high, low


def hot(mask):
    return jnp.where(mask, 1.0, 0.0).astype(jnp.bfloat16)


def cost(micros):
    return pl.CostEstimate(flops=int(micros * 1.1e9), transcendentals=0, bytes_accessed=0)


def call(body, outs, *args, micros, scratch=(), smem=0, aliases=None):
    spec = [pl.BlockSpec(memory_space=pltpu.SMEM)] * smem
    spec += [pl.BlockSpec(memory_space=VMEM)] * (len(args) - smem)
    return pl.pallas_call(
        body,
        out_shape=outs,
        in_specs=spec,
        out_specs=jax.tree.map(lambda _: pl.BlockSpec(memory_space=VMEM), outs),
        scratch_shapes=list(scratch),
        input_output_aliases=aliases or {},
        cost_estimate=cost(micros),
    )(*args)


def out(shape, dtype=jnp.float32):
    return jax.ShapeDtypeStruct(shape, dtype)


def chunk_rows(owner, rank, high, low, k, owners, per):
    inside = (rank >= k * per) & (rank < (k + 1) * per)
    dest = jnp.where(inside, owner * per + rank - k * per, -1)
    pick = hot(iota((owners * per, dest.shape[1]), 0) == dest)
    return mm(pick, high) + mm(pick, low)


def front_body(owners, per, cap, x_ref, ids_ref, om_ref, chunk_ref, high_ref, low_ref, info_ref):
    x = x_ref[...]
    rows, width = x.shape
    clusters = om_ref.shape[0]
    ids = ids_ref[...].reshape(1, rows)
    square = (clusters, clusters)
    om_row = jnp.broadcast_to(om_ref[...].reshape(1, clusters), square)
    om_col = jnp.transpose(om_row.astype(jnp.float32)).astype(jnp.int32)
    om = om_col[:, 0:1]
    here = iota((clusters, rows), 0) == ids
    owner = jnp.sum(jnp.where(here, om, 0), axis=0, keepdims=True)
    mine = iota((owners, rows), 0) == owner
    member = hot(here)
    within = mm(member, hot(iota((rows, rows), 0) < iota((rows, rows), 1)))
    earlier = (om_col == om_row) & (iota(square, 1) < iota(square, 0))
    base = jnp.sum(mm(hot(earlier), member), axis=1, keepdims=True)
    rank = jnp.sum(jnp.where(here, within + base, 0.0), axis=0, keepdims=True)
    count = jnp.sum(mine.astype(jnp.float32), axis=1, keepdims=True)
    count = jnp.sum(jnp.where(mine, count, 0.0), axis=0, keepdims=True)
    rank = jnp.floor((rank * cap + 0.5) / count).astype(jnp.int32)
    order = om * (clusters // owners) + jnp.sum(earlier.astype(jnp.int32), axis=1, keepdims=True)
    position = jnp.sum(jnp.where(here, order, 0), axis=0, keepdims=True)
    info_ref[...] = jnp.concatenate([owner, rank, position, position] * 2, axis=0)
    unit = x * lax.rsqrt(jnp.sum(x * x, axis=1, keepdims=True) + 1e-6)
    high, low = halves(unit)
    high_ref[...] = high
    low_ref[...] = low
    chunk_ref[:, 0:per, :] = chunk_rows(owner, rank, high, low, 0, owners, per).reshape(owners, per, width)
    at_rank = hot(iota((width, rows), 0) == rank)
    coarse = (ids + 1) // 16
    fine = ids + 1 - coarse * 16
    coarse = jnp.where(mine, coarse.astype(jnp.float32), 0.0).astype(jnp.bfloat16)
    fine = jnp.where(mine, fine.astype(jnp.float32), 0.0).astype(jnp.bfloat16)
    sid = mm_nt(coarse, at_rank) * 16.0 + mm_nt(fine, at_rank) - 1.0
    for p in range(owners):
        chunk_ref[p, per:, :] = jnp.broadcast_to(sid[p : p + 1, :], chunk_ref[p, per:, :].shape)


def back_body(owners, per, chunks, held, high_ref, low_ref, info_ref, so_ref, *outs):
    high = high_ref[...]
    low = low_ref[...]
    owner = info_ref[0:1, :]
    rank = info_ref[1:2, :]
    position = info_ref[2:3, :]
    rows, width = high.shape
    clusters = owners * held
    pick = hot(iota((clusters, rows), 0) == position)
    sums = (mm(pick, high) + mm(pick, low)).reshape(owners, held, width)
    share = held // (chunks - 1)
    for k in range(1, chunks):
        outs[k - 1][:, 0:per, :] = chunk_rows(owner, rank, high, low, k, owners, per).reshape(owners, per, width)
        outs[k - 1][:, per:, :] = sums[:, (k - 1) * share : k * share, :]
    q_ref = outs[chunks - 1]
    target = hot(iota((rows, rows), 0) == so_ref[...].reshape(1, rows))
    values = info_ref[...].astype(jnp.float32).astype(jnp.bfloat16)
    q_ref[...] = mm_nt(values, target).astype(jnp.int32)


def by_tile(owners, value_ref, high_ref, low_ref, start):
    size = value_ref.shape[0]
    per = size // owners
    strip = per // TILES
    for t in range(TILES):
        for p in range(owners):
            rows = value_ref[p * per + t * strip : p * per + (t + 1) * strip, :]
            high, low = halves(rows * SCALE)
            to = start + (t * owners + p) * strip
            high_ref[to : to + strip, :] = high
            low_ref[to : to + strip, :] = low


def tick_body(value_ref, tick_ref):
    tick_ref[...] = jnp.zeros_like(tick_ref)


def meta_body(owners, chunks, *refs):
    count = len(refs) - 3
    ids_out, flag_out = refs[count + 1 :]
    cap = refs[0].shape[1]
    blocks = chunks * TILES
    tile = ids_out.shape[3]
    strip = cap // blocks
    slots = blocks * tile
    ids = jnp.concatenate([ref[...] for ref in refs[:count]], axis=0)
    coarse = jnp.floor(ids * 0.0625)
    fine = ids - coarse * 16.0
    lane = iota((cap, slots), 1)
    spread = hot(iota((cap, slots), 0) == lane // tile * strip + lane % strip)
    wide = mm(coarse.astype(jnp.bfloat16), spread) * 16.0 + mm(fine.astype(jnp.bfloat16), spread)
    sender = iota((owners, slots), 1) % tile // strip == iota((owners, slots), 0)
    flag_lane = iota((1, LANES), 1)
    ends = []
    for key in range(count):
        row = jnp.sum(jnp.where(sender, wide[key * owners : (key + 1) * owners, :], 0.0), axis=0, keepdims=True)
        found = []
        for t in range(blocks):
            part = row[:, t * tile : (t + 1) * tile]
            ids_out[key, t] = part
            least = jnp.min(jnp.where(part < 0.0, 1e6, part), axis=1, keepdims=True)
            found.append((least, jnp.max(part, axis=1, keepdims=True)))
        ends.append(found)
        flags = jnp.zeros((1, LANES), jnp.int32)
        for t in range(blocks):
            for b in range(blocks):
                met = (found[t][0] <= ends[0][b][1]) & (ends[0][b][0] <= found[t][1])
                flags = jnp.where((flag_lane == t * blocks + b) & met, 1, flags)
        flag_out[key : key + 1, :] = flags
    flag_out[count:, :] = jnp.zeros((flag_out.shape[0] - count, LANES), jnp.int32)


def gram_body(owners, items, own, level_ref, flag_ref, *refs):
    count = len(items)
    visitors = refs[:count]
    refs = refs[count:]
    if own:
        ids_ref, part_ref, part_out, high_ref, low_ref, lid_ref = refs[:6]
        acc_ref, v_ref, col_ref, pair_ref, sem = refs[6:]
        vh_ref, vl_ref = high_ref, low_ref
    else:
        high_any, low_any, lid_any, ids_ref, part_ref, part_out = refs[:6]
        acc_ref, v_ref, col_ref, pair_ref, sem, high_ref, low_ref, lid_ref, vh_ref, vl_ref, own_sem = refs[6:]
    size = v_ref.shape[1]
    slots = high_ref.shape[0]
    tile = size // TILES
    blocks = slots // tile
    part_out[...] = part_ref[...]
    alive = level_ref[items[0][0]] >= 0
    for at, k in items[1:]:
        alive = alive | (level_ref[at] >= 0)

    def fetch(n):
        return pltpu.make_async_copy(visitors[n], v_ref.at[n], sem.at[n])

    for n, (at, k) in enumerate(items):

        @pl.when(level_ref[at] >= 0)
        def _(n=n):
            fetch(n).start()

    held = []
    if not own:
        for n, (source, target) in enumerate(((high_any, high_ref), (low_any, low_ref), (lid_any, lid_ref))):
            held.append(pltpu.make_async_copy(source, target, own_sem.at[n]))

    @pl.when(alive)
    def _():
        for copy in held:
            copy.start()
        acc_ref[...] = jnp.zeros_like(acc_ref)
        col_ref[...] = jnp.zeros_like(col_ref)
        if own:
            for b in range(slots // LANES):
                row = ids_ref[0, b * LANES // tile, :, b * LANES % tile : b * LANES % tile + LANES]
                lid_ref[b * LANES : (b + 1) * LANES, :] = jnp.transpose(jnp.broadcast_to(row, (LANES, LANES)))

    total = jnp.int32(0)
    for n, (at, k) in enumerate(items):
        live = level_ref[at] >= 0
        for t in range(TILES):
            begin, end = jnp.int32(blocks), jnp.int32(-1)
            for b in range(blocks):
                met = flag_ref[at, (k * TILES + t) * blocks + b] > 0
                if own and b < k * TILES + t:
                    continue
                begin = jnp.where(met, jnp.minimum(begin, b), begin)
                end = jnp.where(met, b, end)
            for w in range((blocks + 1) // 2):
                start = begin + 2 * w
                used = jnp.minimum(start, blocks - 2)
                pair_ref[0, total] = used
                pair_ref[1, total] = n * TILES + t
                pair_ref[2, total] = k * TILES + t
                pair_ref[3, total] = at
                pair_ref[4, total] = (used == start).astype(jnp.int32)
                pair_ref[5, total] = (used < end).astype(jnp.int32)
                total = total + (live & (start <= end)).astype(jnp.int32)

    for n, (at, k) in enumerate(items):

        @pl.when(level_ref[at] >= 0)
        def _(n=n):
            fetch(n).wait()
            by_tile(owners, v_ref.at[n], vh_ref, vl_ref, n * size)

    @pl.when(alive)
    def _():
        for copy in held:
            copy.wait()

        def step(i, _):
            b = pair_ref[0, i]
            v = pair_ref[1, i]
            vid = ids_ref[pair_ref[3, i], pair_ref[2, i]]
            rows = pl.ds(pl.multiple_of(b * tile, tile), 2 * tile)
            cols = pl.ds(pl.multiple_of(v * tile, tile), tile)
            left_h = high_ref[rows, :]
            right_h = vh_ref[cols, :]
            left = jnp.concatenate([left_h, left_h, low_ref[rows, :]], axis=1)
            right = jnp.concatenate([right_h, vl_ref[cols, :], right_h], axis=1)
            score = mm_nt(left, right)
            for h in range(2):
                half = pl.ds(pl.multiple_of((b + h) * tile, tile), tile)
                lid = lid_ref[half, :]
                row_part = acc_ref[half, :]
                wanted = vid + jnp.where(pair_ref[4 + h, i] > 0, 0.0, 1e6)
                for c in range(tile // LANES):
                    lanes = slice(c * LANES, (c + 1) * LANES)
                    weight = jnp.exp2(score[h * tile : (h + 1) * tile, lanes])
                    weight = jnp.where(lid == wanted[:, lanes], weight, 0.0)
                    row_part = row_part + weight
                    col = jnp.sum(weight.reshape(tile // 8, 8, LANES), axis=0)
                    col_ref[v, :, lanes] += col * jnp.where(b + h > v, 1.0, 0.0) if own else col
                acc_ref[half, :] = row_part
            return 0

        lax.fori_loop(0, total, step, 0)
        first, rest = halves(acc_ref[...])
        second, _ = halves(acc_ref[...] - first.astype(jnp.float32) - rest.astype(jnp.float32))
        ones = jnp.ones((8, LANES), jnp.bfloat16)
        rows = mm_nt(ones, first) + mm_nt(ones, rest) + mm_nt(ones, second)
        part_out[pl.ds(level_ref[0], 1), :] += rows[0:1, :]

    for n, (at, k) in enumerate(items):

        @pl.when(level_ref[at] >= 0)
        def _(n=n, at=at, k=k):
            for t in range(TILES):
                where = slice(k * size + t * tile, k * size + (t + 1) * tile)
                part_out[pl.ds(level_ref[at], 1), where] += jnp.sum(col_ref[n * TILES + t], axis=0, keepdims=True)


def last_body(levels, owners, mass_ref, q_ref, score_ref):
    mass = mass_ref[0:owners, :]
    for z in range(1, levels):
        mass = mass + mass_ref[z * owners : (z + 1) * owners, :]
    cap = mass.shape[1]
    owner = q_ref[0:1, :]
    rank = q_ref[1:2, :]
    rows = owner.shape[1]
    at_rank = hot(iota((cap, rows), 0) == rank)
    first = mass.astype(jnp.bfloat16)
    rest = mass - first.astype(jnp.float32)
    second, third = halves(rest)
    value = mm(first, at_rank) + mm(second, at_rank) + mm(third, at_rank)
    mine = iota((owners, rows), 0) == owner
    total = jnp.sum(jnp.where(mine, value, 0.0), axis=0, keepdims=True)
    score_ref[...] = jnp.log(total * math.exp(-SHARPNESS))


def body(embeddings, cluster_ids, owner_map, source_order):
    rows, width = embeddings.shape
    clusters = owner_map.shape[0]
    levels = lax.axis_size("outer")
    inner = lax.axis_size("inner")
    groups = lax.axis_size("grp")
    owners = levels * inner
    held = clusters // owners
    cap = 2 * rows // owners
    per = cap // CHUNKS
    size = owners * per
    slots = CHUNKS * size
    share = held // (CHUNKS - 1)
    bf, i32 = jnp.bfloat16, jnp.int32
    dealt = out((owners, per + share, width))

    first, high, low, info = call(
        functools.partial(front_body, owners, per, cap),
        (dealt, out((rows, width), bf), out((rows, width), bf), out((8, rows), i32)),
        embeddings, cluster_ids, owner_map, micros=5,
    )
    back = call(
        functools.partial(back_body, owners, per, CHUNKS, held),
        (dealt,) * (CHUNKS - 1) + (out((8, rows), i32),),
        high, low, info, source_order, micros=6,
    )
    sends = (first,) + tuple(back[: CHUNKS - 1])
    q_info = back[CHUNKS - 1]
    tile = size // TILES
    strip = per // TILES
    blocks = slots // tile

    got, mine = [], []
    for k in range(CHUNKS):
        send = sends[k] if k == 0 else lax.optimization_barrier((sends[k], mine[-1]))[0]
        got.append(lax.all_to_all(send, PLANE, 0, 0, tiled=True))
        mine.append(got[k][:, :per, :].reshape(size, width))
    own_ids = got[0][:, per, :cap].reshape(owners, cap)
    piece = jnp.concatenate([jnp.sum(got[k][:, per:, :], axis=0) for k in range(1, CHUNKS)], axis=0)

    level = lax.axis_index("outer")
    down = lax.axis_index("inner") % 2
    seat = jnp.where(down == 1, levels - 1 - level, level)

    def pairs(moves):
        found = []
        for lane in range(inner):
            for a, b in moves:
                if lane % 2:
                    a, b = levels - 1 - a, levels - 1 - b
                found.append((a * inner + lane, b * inner + lane))
        return found

    top = levels - 1
    moves = []
    for s in range(1, top + 1):
        moves.append([(a, a + 1) for a in range(s - 1, top) if not (s == 1 and a == top - 1)])
    back_move = [(top, top - 1)]

    arrived = {}

    def direct(steps):
        return [(a, a + steps) for a in range(top + 1 - steps) if not (steps == 1 and a == top - 1)]

    ids_of = [own_ids]
    for s in range(1, top + 1):
        ids_of.append(lax.ppermute(own_ids, LINE, pairs(direct(s))))
    ids_of.insert(2, lax.ppermute(own_ids, LINE, pairs(back_move)))
    for k in range(CHUNKS):
        value = mine[k]
        for s in range(1, top + 1):
            value = lax.ppermute(value, LINE, pairs(moves[s - 1]))
            arrived[s, k] = value
        arrived["b", k] = lax.ppermute(mine[k], LINE, pairs(back_move))

    tick = pl.pallas_call(
        tick_body,
        out_shape=out((8, LANES)),
        in_specs=[pl.BlockSpec(memory_space=pl.ANY)],
        out_specs=pl.BlockSpec(memory_space=VMEM),
        name="tick",
    )(arrived[1, 0])
    keys_held = len(ids_of)
    ids, flags = call(
        functools.partial(meta_body, owners, CHUNKS),
        (out((keys_held, blocks, 1, tile)), out((8, LANES), i32)),
        *ids_of, tick, micros=3,
    )
    keys = [1, "b"] + list(range(2, top + 1))

    def source_seat(key):
        if key == "b":
            return jnp.where(seat == top - 1, top, -1)
        got = seat >= key
        if key == 1:
            got = got & (seat < top)
        return jnp.where(got, seat - key, -1)

    seats = [seat] + [source_seat(key) for key in keys]
    level_of = jnp.stack([jnp.where(a < 0, -1, jnp.where(down == 1, top - a, a)) for a in seats]).astype(i32)
    part = jnp.zeros((levels, slots), jnp.float32)

    def gram(part, items, held, micros):
        own = not held
        visitors = [mine[k] if key == "own" else arrived[key, k] for key, k in items]
        at = tuple((0 if key == "own" else 1 + keys.index(key), k) for key, k in items)
        count = len(items)
        vm = pl.BlockSpec(memory_space=VMEM)
        any_ = pl.BlockSpec(memory_space=pl.ANY)
        own_out = (out((slots, width), bf), out((slots, width), bf), out((slots, LANES)))
        scratch = [
            VMEM((slots, LANES), jnp.float32),
            VMEM((count, size, width), jnp.float32),
            VMEM((count * TILES, 8, tile), jnp.float32),
            pltpu.SMEM((6, count * TILES * blocks + 1), i32),
            pltpu.SemaphoreType.DMA((count,)),
        ]
        if not own:
            scratch += [
                VMEM((slots, width), bf),
                VMEM((slots, width), bf),
                VMEM((slots, LANES), jnp.float32),
                VMEM((count * size, width), bf),
                VMEM((count * size, width), bf),
                pltpu.SemaphoreType.DMA((3,)),
            ]
        return pl.pallas_call(
            functools.partial(gram_body, owners, at, own),
            out_shape=(out((levels, slots)),) + (own_out if own else ()),
            in_specs=[pl.BlockSpec(memory_space=pltpu.SMEM)] * 2 + [any_] * (count + len(held)) + [vm] * 2,
            out_specs=(vm,) * (4 if own else 1),
            scratch_shapes=scratch,
            cost_estimate=cost(micros),
            name="gram",
        )(level_of, flags, *visitors, *held, ids, part)

    plan = [
        ([("own", k) for k in range(CHUNKS)], 10),
        ([(1, 0), ("b", 0), (2, 0), (1, 1)], 12),
        ([("b", 1), (2, 1), (1, 2)], 10),
        ([("b", 2), (2, 2), (3, 0)], 9),
        ([(3, 1)], 5),
        ([(3, 2)], 5),
    ]
    held_here = ()
    for n, (items, micros) in enumerate(plan):
        part, *made = gram(part, items, held_here, micros)
        held_here = held_here or tuple(made)
        if n == 2:
            piece = lax.optimization_barrier((piece, part))[0]
    total = None
    for s in range(groups):
        route = [(g * levels + z, ((z + s) % groups) * levels + g) for g in range(groups) for z in range(levels)]
        came = lax.ppermute(piece, ("grp", "outer"), route)
        total = came if total is None else total + came
    centroids = total * lax.rsqrt(jnp.mean(total * total, axis=1, keepdims=True) + 1e-6)
    parts = part.reshape(levels, CHUNKS, TILES, owners, strip).transpose(0, 3, 1, 2, 4).reshape(levels * owners, cap)
    home = lax.all_to_all(parts, BY_LEVEL, 0, 0, tiled=True)
    score = call(functools.partial(last_body, levels, owners), out((1, rows)), home, q_info, micros=2)

    return score.reshape(rows), centroids


def solution(mesh):
    groups, owned = mesh.shape["grp"], mesh.shape["own"]
    split = Mesh(mesh.devices.reshape(groups, groups, owned // groups), EVERY)
    return jax.shard_map(
        body,
        mesh=split,
        in_specs=(P(EVERY, None), P(EVERY), P(), P(EVERY)),
        out_specs=(P(EVERY), P(LINE, None)),
        check_vma=False,
    )
```

time: 278 us -> 255 us (0.917)
  blocking collectives: 24.4 us -> 0 us
  starting transfers between devices: 113 us -> 132 us
  Pallas kernels: 50.1 us -> 36.2 us
  waiting for transfers between devices: 74.2 us -> 70.9 us
    ppermute x4 -> x8, starting transfers between devices: 8.52 us -> 50.1 us  [the longest x4 41.7 us: body(): came = lax.ppermute(piece, ('grp', 'outer'), route)]
    all_to_all x1 -> x0, blocking collectives: 24.4 us -> none  [to_owner(): lax.all_to_all(value.reshape(owners, per, width), PLANE, 0, 0, tiled=True)]
    all_to_all x4 -> x3, waiting for transfers between devices: 59.4 us -> 42.8 us  [body(): got.append(lax.all_to_all(send, PLANE, 0, 0, tiled=True))]
    all_to_all x1, starting transfers between devices: 54 us -> 38.8 us  [body(): home = lax.all_to_all(parts, BY_LEVEL, 0, 0, tiled=True)]
    ppermute x9, waiting for transfers between devices: 0.02 us -> 13.7 us  [body(): value = lax.ppermute(value, LINE, pairs(moves[s - 1]))]
    pallas_call x5 -> x7, Pallas kernels: 32.3 us -> 21 us  [the longest x6 20.4 us: gram(): pl.pallas_call(functools.partial(gram_body, owners, at, own), out_shape=(...]
    all_to_all x4 -> x3, starting transfers between devices: 19.4 us -> 12.4 us  [body(): got.append(lax.all_to_all(send, PLANE, 0, 0, tiled=True))]
    slice x0 -> x4, local copies, waits for them, and re-layouts: none -> 4.96 us  [the longest x3 4.12 us: body(): mine.append(got[k][:, :per, :].reshape(size, width))]
  transfers between devices with their start and end apart: 21 -> 24, of which waited for: 7 -> 8; matrix products, arithmetic and copies ran while one was open for 2% -> 2% of each run, Pallas kernels for 14% -> 11%
where the time goes in v2:
time: 255 us; the launch traced here: 253 us
  starting transfers between devices  132 us (52%)
  waiting for transfers between devices  70.9 us (28%)
  Pallas kernels  36.2 us (14%)
  local copies, waits for them, and re-layouts  9.97 us (4%)
  other arithmetic  2.74 us (1%)
    all_to_all x3, waiting for transfers between devices, body(): got.append(lax.all_to_all(send, PLANE, 0, 0, tiled=True))  42.8 us
    ppermute x4, starting transfers between devices, body(): came = lax.ppermute(piece, ('grp', 'outer'), route)  41.7 us
    all_to_all x1, starting transfers between devices, body(): home = lax.all_to_all(parts, BY_LEVEL, 0, 0, tiled=True)  38.8 us
    ppermute x9, starting transfers between devices, body(): value = lax.ppermute(value, LINE, pairs(moves[s - 1]))  25.7 us
    pallas_call x6, Pallas kernels, gram(): pl.pallas_call(functools.partial(gram_body, owners, at, own), out_shape=(...  20.4 us
    pallas_call x4, Pallas kernels, call(): pl.pallas_call(body, out_shape=outs, in_specs=spec, out_specs=jax.tree.ma...  15.2 us
    ppermute x9, waiting for transfers between devices, body(): value = lax.ppermute(value, LINE, pairs(moves[s - 1]))  13.7 us
    all_to_all x3, starting transfers between devices, body(): got.append(lax.all_to_all(send, PLANE, 0, 0, tiled=True))  12.4 us
  transfers between devices with their start and end apart: 24, of which 8 were waited for; matrix products, arithmetic and copies ran while one was open for 2% of the time, Pallas kernels for 11%

profile of v2, /device:TPU:0, one launch (start us, length us, event | category | flops | bytes accessed | tf_op | source)
XLA Modules:
  0.0 253.1 jit_solution(7352906806379403215)
XLA Ops:
  0.6 5.7 %shard_map.59 = (f32[8,72,768]{2,1,0:T(8,128)}, bf16[768,768]{1,0:T(8,128)(2,1)}, bf16[768,768]{1,0:T(8,128)(2,1)}, s32[8,768]{1,0:T(8,128)}) custom-call(f32[768,768]{1,0:T(8,128)} %x_ref.1, s32[768]{0:T(1024)} %ids_ref.1, s32[128]{0:T(128)} %om_ref.1), custom_call_target="tpu_custom_call" | custom-call | flops 5500000256 | tf_op jit(solution)/shard_map/pallas_call | solution.py:55
  6.3 5.2 %all-to-all-start = ((f32[8,72,768]{2,1,0:T(8,128)}), f32[8,72,768]{2,1,0:T(8,128)S(1)}, u32[]{:S(2)}, u32[]{:S(2)}) async-start(f32[8,72,768]{2,1,0:T(8,128)} %get-tuple-element.18), calls=%async_computation | async-start | bytes 3538944 | tf_op jit(solution)/shard_map/all_to_all | solution.py:361
  11.5 6.0 %shard_map.61 = (f32[8,72,768]{2,1,0:T(8,128)}, f32[8,72,768]{2,1,0:T(8,128)}, s32[8,768]{1,0:T(8,128)}) custom-call(bf16[768,768]{1,0:T(8,128)(2,1)} %get-tuple-element.20.high_ref, bf16[768,768]{1,0:T(8,128)(2,1)} %get-tuple-element.21.low_ref, s32[8,768]{1,0:T(8,128)} %get-tuple-element.22.info_ref, s32[768]{0:T(1024)} %so_ref.1), custom_call_target="tpu_custom_call" | custom-call | flops 6600000000 | tf_op jit(solution)/shard_map/pallas_call | solution.py:55
  17.4 17.2 %all-to-all-done = f32[8,72,768]{2,1,0:T(8,128)S(1)} async-done(((f32[8,72,768]{2,1,0:T(8,128)}), f32[8,72,768]{2,1,0:T(8,128)S(1)}, u32[]{:S(2)}, u32[]{:S(2)}) %all-to-all-start) | async-done | bytes 1769504 | tf_op jit(solution)/shard_map/all_to_all | solution.py:361
  36.4 3.6 %all-to-all-start.1 = ((f32[8,72,768]{2,1,0:T(8,128)}), f32[8,72,768]{2,1,0:T(8,128)S(1)}, u32[]{:S(2)}, u32[]{:S(2)}) async-start(f32[8,72,768]{2,1,0:T(8,128)} %get-tuple-element.25), calls=%async_computation.1 | async-start | bytes 3538944 | tf_op jit(solution)/shard_map/all_to_all | solution.py:361
  40.0 4.7 %collective-permute-start.4 = (f32[512,768]{1,0:T(8,128)}, f32[512,768]{1,0:T(8,128)}, u32[]{:S(2)}, u32[]{:S(2)}) collective-permute-start(f32[512,768]{1,0:T(8,128)} %bitcast.6.refs_0_), channel_id=1, source_target_pairs={{0,2},{2,4},{7,5},{5,3},{8,10},{10,12},{15,13},{13,11},{16,18},{18... | collective-permute-start | bytes 4718600 | tf_op jit(solution)/shard_map/ppermute | solution.py:397
  44.7 18.3 %all-to-all-done.1 = f32[8,72,768]{2,1,0:T(8,128)S(1)} async-done(((f32[8,72,768]{2,1,0:T(8,128)}), f32[8,72,768]{2,1,0:T(8,128)S(1)}, u32[]{:S(2)}, u32[]{:S(2)}) %all-to-all-start.1) | async-done | bytes 1769504 | tf_op jit(solution)/shard_map/all_to_all | solution.py:361
  64.4 3.6 %all-to-all-start.2 = ((f32[8,72,768]{2,1,0:T(8,128)}), f32[8,72,768]{2,1,0:T(8,128)S(1)}, u32[]{:S(2)}, u32[]{:S(2)}) async-start(f32[8,72,768]{2,1,0:T(8,128)} %get-tuple-element.26), calls=%async_computation.2 | async-start | bytes 3538944 | tf_op jit(solution)/shard_map/all_to_all | solution.py:361
  68.0 4.6 %collective-permute-start.8 = (f32[512,768]{1,0:T(8,128)}, f32[512,768]{1,0:T(8,128)}, u32[]{:S(2)}, u32[]{:S(2)}) collective-permute-start(f32[512,768]{1,0:T(8,128)} %bitcast.15), channel_id=1, source_target_pairs={{0,2},{2,4},{7,5},{5,3},{8,10},{10,12},{15,13},{13,11},{16,18},{18... | collective-permute-start | bytes 4718600 | tf_op jit(solution)/shard_map/ppermute | solution.py:397
  74.1 2.4 collective-permute-start
  77.8 1.9 collective-permute-start.2
  79.6 2.8 %collective-permute-start.3 = (f32[8,192]{1,0:T(8,128)S(1)}, f32[8,192]{1,0:T(8,128)}, u32[]{:S(2)}, u32[]{:S(2)}) collective-permute-start(f32[8,192]{1,0:T(8,128)S(1)} %bitcast.23), channel_id=1, source_target_pairs={{0,6},{7,1},{8,14},{15,9},{16,22},{23,17},{24,30},{31,25}} | collective-permute-start | bytes 18440 | tf_op jit(solution)/shard_map/ppermute | solution.py:392
  83.7 7.4 %all-to-all-done.2 = f32[8,72,768]{2,1,0:T(8,128)S(1)} async-done(((f32[8,72,768]{2,1,0:T(8,128)}), f32[8,72,768]{2,1,0:T(8,128)S(1)}, u32[]{:S(2)}, u32[]{:S(2)}) %all-to-all-start.2) | async-done | bytes 1769504 | tf_op jit(solution)/shard_map/all_to_all | solution.py:361
  92.3 1.8 collective-permute-start.15
  96.0 1.8 collective-permute-start.12
  97.8 6.5 %collective-permute-start.5 = (f32[512,768]{1,0:T(8,128)}, f32[512,768]{1,0:T(8,128)}, u32[]{:S(2)}, u32[]{:S(2)}) collective-permute-start(f32[512,768]{1,0:T(8,128)} %bitcast.8.refs_2_), channel_id=1, source_target_pairs={{0,2},{2,4},{7,5},{5,3},{8,10},{10,12},{15,13},{13,11},{16,18},{18... | collective-permute-start | bytes 4718600 | tf_op jit(solution)/shard_map/ppermute | solution.py:397
  104.2 2.0 shard_map.60
  106.3 1.8 collective-permute-start.9
  108.7 12.1 %gram.6 = (f32[4,1536]{1,0:T(4,128)}, bf16[1536,768]{1,0:T(8,128)(2,1)}, bf16[1536,768]{1,0:T(8,128)(2,1)}, f32[1536,128]{1,0:T(8,128)}) custom-call(s32[5]{0:T(128)} %stack.23.level_ref, s32[8,128]{1,0:T(8,128)} %get-tuple-element.19.flag_ref, f32[512,768]{1,0:T(8,128)} %bitcast.6.refs_0_, f32[512,768]{1,0:T(8,128)} %bitcast.16, ...), custom_call_target="tpu_custom_call" | custom-call | flops 11000000512 | tf_op jit(solution)/shard_map/gram/pallas_call | solution.py:452
  120.8 1.9 collective-permute-start.11
  122.7 1.8 collective-permute-start.13
  124.5 13.7 %collective-permute-done.5.refs_2_ = f32[512,768]{1,0:T(8,128)} collective-permute-done((f32[512,768]{1,0:T(8,128)}, f32[512,768]{1,0:T(8,128)}, u32[]{:S(2)}, u32[]{:S(2)}) %collective-permute-start.5) | collective-permute-done | bytes 1572896 | tf_op jit(solution)/shard_map/ppermute | solution.py:397
  138.1 1.8 collective-permute-start.6
  140.0 2.0 gram.7.refs_7_
  145.1 22.6 %collective-permute-start.17 = (f32[16,768]{1,0:T(8,128)S(1)}, f32[16,768]{1,0:T(8,128)S(1)}, u32[]{:S(2)}, u32[]{:S(2)}) collective-permute-start(f32[16,768]{1,0:T(8,128)S(1)} %pad_maximum_fusion), channel_id=1, source_target_pairs={{0,8},{2,16},{4,24},{6,0},{8,10},{10,18},{12,26},{14,2},{16,12},{1... | collective-permute-start | bytes 147464 | tf_op jit(solution)/shard_map/ppermute | solution.py:479
  167.7 3.0 %collective-permute-done.17 = f32[16,768]{1,0:T(8,128)S(1)} collective-permute-done((f32[16,768]{1,0:T(8,128)S(1)}, f32[16,768]{1,0:T(8,128)S(1)}, u32[]{:S(2)}, u32[]{:S(2)}) %collective-permute-start.17) | collective-permute-done | bytes 49184 | tf_op jit(solution)/shard_map/ppermute | solution.py:479
  170.7 14.6 %collective-permute-start.18 = (f32[16,768]{1,0:T(8,128)S(1)}, f32[16,768]{1,0:T(8,128)S(1)}, u32[]{:S(2)}, u32[]{:S(2)}) collective-permute-start(f32[16,768]{1,0:T(8,128)S(1)} %pad_maximum_fusion), channel_id=1, source_target_pairs={{0,16},{2,24},{4,0},{6,8},{8,18},{10,26},{12,2},{14,10},{16,20},{1... | collective-permute-start | bytes 147464 | tf_op jit(solution)/shard_map/ppermute | solution.py:479
  185.4 3.0 %collective-permute-done.18 = f32[16,768]{1,0:T(8,128)S(1)} collective-permute-done((f32[16,768]{1,0:T(8,128)S(1)}, f32[16,768]{1,0:T(8,128)S(1)}, u32[]{:S(2)}, u32[]{:S(2)}) %collective-permute-start.18) | collective-permute-done | bytes 49184 | tf_op jit(solution)/shard_map/ppermute | solution.py:479
  188.4 3.8 %collective-permute-start.19 = (f32[16,768]{1,0:T(8,128)S(1)}, f32[16,768]{1,0:T(8,128)S(1)}, u32[]{:S(2)}, u32[]{:S(2)}) collective-permute-start(f32[16,768]{1,0:T(8,128)S(1)} %pad_maximum_fusion), channel_id=1, source_target_pairs={{0,24},{2,0},{4,8},{6,16},{8,26},{10,2},{12,10},{14,18},{16,28},{1... | collective-permute-start | bytes 147464 | tf_op jit(solution)/shard_map/ppermute | solution.py:479
  194.1 1.9 collective-permute-start.7
  203.6 38.8 %all-to-all-start.3 = ((f32[32,1,192]{2,1,0:T(1,128)}), f32[32,1,192]{2,1,0:T(1,128)S(1)}, u32[]{:S(2)}, u32[]{:S(2)}) async-start(f32[32,1,192]{2,1,0:T(1,128)} %all_to_all.19), calls=%async_computation.3 | async-start | bytes 65536 | tf_op jit(solution)/shard_map/all_to_all | solution.py:483
  243.1 6.6 %all-to-all-done.3 = f32[32,1,192]{2,1,0:T(1,128)S(1)} async-done(((f32[32,1,192]{2,1,0:T(1,128)}), f32[32,1,192]{2,1,0:T(1,128)S(1)}, u32[]{:S(2)}, u32[]{:S(2)}) %all-to-all-start.3) | async-done | bytes 24608 | tf_op jit(solution)/shard_map/all_to_all | solution.py:483
  (57 shorter events, 27.6 us)
Async XLA Ops:
  6.3 28.3 %all-to-all-start = ((f32[8,72,768]{2,1,0:T(8,128)}), f32[8,72,768]{2,1,0:T(8,128)S(1)}, u32[]{:S(2)}, u32[]{:S(2)}) async-start(f32[8,72,768]{2,1,0:T(8,128)} %get-tuple-element.18), calls=%async_computation | async-start | bytes 3538944 | tf_op jit(solution)/shard_map/all_to_all | solution.py:361
  34.6 1.8 copy-start
  36.4 26.6 %all-to-all-start.1 = ((f32[8,72,768]{2,1,0:T(8,128)}), f32[8,72,768]{2,1,0:T(8,128)S(1)}, u32[]{:S(2)}, u32[]{:S(2)}) async-start(f32[8,72,768]{2,1,0:T(8,128)} %get-tuple-element.25), calls=%async_computation.1 | async-start | bytes 3538944 | tf_op jit(solution)/shard_map/all_to_all | solution.py:361
  40.0 39.7 %collective-permute-start.4 = (f32[512,768]{1,0:T(8,128)}, f32[512,768]{1,0:T(8,128)}, u32[]{:S(2)}, u32[]{:S(2)}) collective-permute-start(f32[512,768]{1,0:T(8,128)} %bitcast.6.refs_0_), channel_id=1, source_target_pairs={{0,2},{2,4},{7,5},{5,3},{8,10},{10,12},{15,13},{13,11},{16,18},{18... | collective-permute-start | bytes 4718600 | tf_op jit(solution)/shard_map/ppermute | solution.py:397
  64.4 26.6 %all-to-all-start.2 = ((f32[8,72,768]{2,1,0:T(8,128)}), f32[8,72,768]{2,1,0:T(8,128)S(1)}, u32[]{:S(2)}, u32[]{:S(2)}) async-start(f32[8,72,768]{2,1,0:T(8,128)} %get-tuple-element.26), calls=%async_computation.2 | async-start | bytes 3538944 | tf_op jit(solution)/shard_map/all_to_all | solution.py:361
  68.0 38.3 %collective-permute-start.8 = (f32[512,768]{1,0:T(8,128)}, f32[512,768]{1,0:T(8,128)}, u32[]{:S(2)}, u32[]{:S(2)}) collective-permute-start(f32[512,768]{1,0:T(8,128)} %bitcast.15), channel_id=1, source_target_pairs={{0,2},{2,4},{7,5},{5,3},{8,10},{10,12},{15,13},{13,11},{16,18},{18... | collective-permute-start | bytes 4718600 | tf_op jit(solution)/shard_map/ppermute | solution.py:397
  74.1 18.2 %copy-start.3 = (f32[8,1,192]{2,0,1:T(8,128)}, f32[8,1,192]{2,0,1:T(8,128)S(1)}, u32[]{:S(2)}) copy-start(f32[8,1,192]{2,0,1:T(8,128)S(1)} %copy.16) | copy-start | bytes 18436
  74.1 18.2 %collective-permute-start = (f32[8,192]{1,0:T(8,128)S(1)}, f32[8,192]{1,0:T(8,128)S(1)}, u32[]{:S(2)}, u32[]{:S(2)}) collective-permute-start(f32[8,192]{1,0:T(8,128)S(1)} %bitcast.20), channel_id=1, source_target_pairs={{0,2},{2,4},{7,5},{5,3},{8,10},{10,12},{15,13},{13,11},{16,18},{18... | collective-permute-start | bytes 18440 | tf_op jit(solution)/shard_map/ppermute | solution.py:392
  76.5 17.7 %collective-permute-start.1 = (f32[8,192]{1,0:T(8,128)S(1)}, f32[8,192]{1,0:T(8,128)}, u32[]{:S(2)}, u32[]{:S(2)}) collective-permute-start(f32[8,192]{1,0:T(8,128)S(1)} %bitcast.21), channel_id=1, source_target_pairs={{6,4},{1,3},{14,12},{9,11},{22,20},{17,19},{30,28},{25,27}} | collective-permute-start | bytes 18440 | tf_op jit(solution)/shard_map/ppermute | solution.py:393
  77.8 18.2 %collective-permute-start.2 = (f32[8,192]{1,0:T(8,128)S(1)}, f32[8,192]{1,0:T(8,128)}, u32[]{:S(2)}, u32[]{:S(2)}) collective-permute-start(f32[8,192]{1,0:T(8,128)S(1)} %bitcast.22), channel_id=1, source_target_pairs={{0,4},{2,6},{7,3},{5,1},{8,12},{10,14},{15,11},{13,9},{16,20},{18,... | collective-permute-start | bytes 18440 | tf_op jit(solution)/shard_map/ppermute | solution.py:392
  79.6 18.1 %collective-permute-start.3 = (f32[8,192]{1,0:T(8,128)S(1)}, f32[8,192]{1,0:T(8,128)}, u32[]{:S(2)}, u32[]{:S(2)}) collective-permute-start(f32[8,192]{1,0:T(8,128)S(1)} %bitcast.23), channel_id=1, source_target_pairs={{0,6},{7,1},{8,14},{15,9},{16,22},{23,17},{24,30},{31,25}} | collective-permute-start | bytes 18440 | tf_op jit(solution)/shard_map/ppermute | solution.py:392
  83.7 10.5 %copy-start.1 = (f32[8,64,768]{2,1,0:T(8,128)S(1)}, f32[8,64,768]{2,1,0:T(8,128)}, u32[]{:S(2)}) copy-start(f32[8,64,768]{2,1,0:T(8,128)} %slice.26) | copy-start | bytes 4718596
  92.3 11.9 %copy-start.5 = (f32[8,192]{1,0:T(8,128)}, f32[8,192]{1,0:T(8,128)S(1)}, u32[]{:S(2)}) copy-start(f32[8,192]{1,0:T(8,128)S(1)} %collective-permute-done.refs_1_) | copy-start | bytes 18436
  92.3 28.5 %collective-permute-start.15 = (f32[512,768]{1,0:T(8,128)}, f32[512,768]{1,0:T(8,128)}, u32[]{:S(2)}, u32[]{:S(2)}) collective-permute-start(f32[512,768]{1,0:T(8,128)} %bitcast.6.refs_0_), channel_id=1, source_target_pairs={{6,4},{1,3},{14,12},{9,11},{22,20},{17,19},{30,28},{25,27}} | collective-permute-start | bytes 4718600 | tf_op jit(solution)/shard_map/ppermute | solution.py:399
  94.2 47.8 %collective-permute-start.14 = (f32[512,768]{1,0:T(8,128)S(1)}, f32[512,768]{1,0:T(8,128)}, u32[]{:S(2)}, u32[]{:S(2)}) collective-permute-start(f32[512,768]{1,0:T(8,128)S(1)} %bitcast.17), channel_id=1, source_target_pairs={{6,4},{1,3},{14,12},{9,11},{22,20},{17,19},{30,28},{25,27}} | collective-permute-start | bytes 4718600 | tf_op jit(solution)/shard_map/ppermute | solution.py:399
  96.0 26.7 %collective-permute-start.12 = (f32[512,768]{1,0:T(8,128)}, f32[512,768]{1,0:T(8,128)}, u32[]{:S(2)}, u32[]{:S(2)}) collective-permute-start(f32[512,768]{1,0:T(8,128)} %collective-permute-done.4.value_ref.refs_0_), channel_id=1, source_target_pairs={{2,4},{4,6},{5,3},{3,1},{10,12},{12,14},{13,11},{11,9},{18,20},{20... | collective-permute-start | bytes 4718600 | tf_op jit(solution)/shard_map/ppermute | solution.py:397
  97.8 40.4 %collective-permute-start.5 = (f32[512,768]{1,0:T(8,128)}, f32[512,768]{1,0:T(8,128)}, u32[]{:S(2)}, u32[]{:S(2)}) collective-permute-start(f32[512,768]{1,0:T(8,128)} %bitcast.8.refs_2_), channel_id=1, source_target_pairs={{0,2},{2,4},{7,5},{5,3},{8,10},{10,12},{15,13},{13,11},{16,18},{18... | collective-permute-start | bytes 4718600 | tf_op jit(solution)/shard_map/ppermute | solution.py:397
  106.3 35.7 %collective-permute-start.9 = (f32[512,768]{1,0:T(8,128)}, f32[512,768]{1,0:T(8,128)}, u32[]{:S(2)}, u32[]{:S(2)}) collective-permute-start(f32[512,768]{1,0:T(8,128)} %collective-permute-done.8.refs_3_), channel_id=1, source_target_pairs={{2,4},{4,6},{5,3},{3,1},{10,12},{12,14},{13,11},{11,9},{18,20},{20... | collective-permute-start | bytes 4718600 | tf_op jit(solution)/shard_map/ppermute | solution.py:397
  108.7 12.1 %copy-start.2 = (f32[8,768]{1,0:T(8,128)S(1)}, f32[8,768]{1,0:T(8,128)}, u32[]{:S(2)}) copy-start(f32[8,768]{1,0:T(8,128)} %slice_reduce_fusion.1) | copy-start | bytes 73732
  120.8 75.2 %collective-permute-start.11 = (f32[512,768]{1,0:T(8,128)}, f32[512,768]{1,0:T(8,128)}, u32[]{:S(2)}, u32[]{:S(2)}) collective-permute-start(f32[512,768]{1,0:T(8,128)} %bitcast.8.refs_2_), channel_id=1, source_target_pairs={{6,4},{1,3},{14,12},{9,11},{22,20},{17,19},{30,28},{25,27}} | collective-permute-start | bytes 4718600 | tf_op jit(solution)/shard_map/ppermute | solution.py:399
  122.7 73.4 %collective-permute-start.13 = (f32[512,768]{1,0:T(8,128)}, f32[512,768]{1,0:T(8,128)}, u32[]{:S(2)}, u32[]{:S(2)}) collective-permute-start(f32[512,768]{1,0:T(8,128)} %collective-permute-done.12.refs_2_), channel_id=1, source_target_pairs={{4,6},{3,1},{12,14},{11,9},{20,22},{19,17},{28,30},{27,25}} | collective-permute-start | bytes 4718600 | tf_op jit(solution)/shard_map/ppermute | solution.py:397
  138.1 56.0 %collective-permute-start.6 = (f32[512,768]{1,0:T(8,128)}, f32[512,768]{1,0:T(8,128)}, u32[]{:S(2)}, u32[]{:S(2)}) collective-permute-start(f32[512,768]{1,0:T(8,128)} %collective-permute-done.5.refs_2_), channel_id=1, source_target_pairs={{2,4},{4,6},{5,3},{3,1},{10,12},{12,14},{13,11},{11,9},{18,20},{20... | collective-permute-start | bytes 4718600 | tf_op jit(solution)/shard_map/ppermute | solution.py:397
  143.7 1.4 collective-permute-start.16
  144.4 53.4 %collective-permute-start.10 = (f32[512,768]{1,0:T(8,128)}, f32[512,768]{1,0:T(8,128)S(1)}, u32[]{:S(2)}, u32[]{:S(2)}) collective-permute-start(f32[512,768]{1,0:T(8,128)} %collective-permute-done.9.refs_1_), channel_id=1, source_target_pairs={{4,6},{3,1},{12,14},{11,9},{20,22},{19,17},{28,30},{27,25}} | collective-permute-start | bytes 4718600 | tf_op jit(solution)/shard_map/ppermute | solution.py:397
  145.1 25.6 %collective-permute-start.17 = (f32[16,768]{1,0:T(8,128)S(1)}, f32[16,768]{1,0:T(8,128)S(1)}, u32[]{:S(2)}, u32[]{:S(2)}) collective-permute-start(f32[16,768]{1,0:T(8,128)S(1)} %pad_maximum_fusion), channel_id=1, source_target_pairs={{0,8},{2,16},{4,24},{6,0},{8,10},{10,18},{12,26},{14,2},{16,12},{1... | collective-permute-start | bytes 147464 | tf_op jit(solution)/shard_map/ppermute | solution.py:479
  170.7 17.7 %collective-permute-start.18 = (f32[16,768]{1,0:T(8,128)S(1)}, f32[16,768]{1,0:T(8,128)S(1)}, u32[]{:S(2)}, u32[]{:S(2)}) collective-permute-start(f32[16,768]{1,0:T(8,128)S(1)} %pad_maximum_fusion), channel_id=1, source_target_pairs={{0,16},{2,24},{4,0},{6,8},{8,18},{10,26},{12,2},{14,10},{16,20},{1... | collective-permute-start | bytes 147464 | tf_op jit(solution)/shard_map/ppermute | solution.py:479
  188.4 5.6 %collective-permute-start.19 = (f32[16,768]{1,0:T(8,128)S(1)}, f32[16,768]{1,0:T(8,128)S(1)}, u32[]{:S(2)}, u32[]{:S(2)}) collective-permute-start(f32[16,768]{1,0:T(8,128)S(1)} %pad_maximum_fusion), channel_id=1, source_target_pairs={{0,24},{2,0},{4,8},{6,16},{8,26},{10,2},{12,10},{14,18},{16,28},{1... | collective-permute-start | bytes 147464 | tf_op jit(solution)/shard_map/ppermute | solution.py:479
  194.1 6.3 %collective-permute-start.7 = (f32[512,768]{1,0:T(8,128)}, f32[512,768]{1,0:T(8,128)}, u32[]{:S(2)}, u32[]{:S(2)}) collective-permute-start(f32[512,768]{1,0:T(8,128)} %collective-permute-done.6.refs_1_), channel_id=1, source_target_pairs={{4,6},{3,1},{12,14},{11,9},{20,22},{19,17},{28,30},{27,25}} | collective-permute-start | bytes 4718600 | tf_op jit(solution)/shard_map/ppermute | solution.py:397
  197.7 1.2 copy-start.4
  203.6 46.1 %all-to-all-start.3 = ((f32[32,1,192]{2,1,0:T(1,128)}), f32[32,1,192]{2,1,0:T(1,128)S(1)}, u32[]{:S(2)}, u32[]{:S(2)}) async-start(f32[32,1,192]{2,1,0:T(1,128)} %all_to_all.19), calls=%async_computation.3 | async-start | bytes 65536 | tf_op jit(solution)/shard_map/all_to_all | solution.py:483

commit v3 on v2

--- a/solution.py
+++ b/solution.py
@@ -145,13 +145,13 @@
             low_ref[to : to + strip, :] = low
 
 
-def tick_body(value_ref, tick_ref):
-    tick_ref[...] = jnp.zeros_like(tick_ref)
+def tick_body(value_ref, through_ref, out_ref):
+    out_ref[...] = through_ref[...]
 
 
 def meta_body(owners, chunks, *refs):
-    count = len(refs) - 3
-    ids_out, flag_out = refs[count + 1 :]
+    count = len(refs) - 2
+    ids_out, flag_out = refs[count:]
     cap = refs[0].shape[1]
     blocks = chunks * TILES
     tile = ids_out.shape[3]
@@ -184,17 +184,24 @@
     flag_out[count:, :] = jnp.zeros((flag_out.shape[0] - count, LANES), jnp.int32)
 
 
-def gram_body(owners, items, own, level_ref, flag_ref, *refs):
+def gram_body(owners, items, own, held, level_ref, flag_ref, *refs):
     count = len(items)
     visitors = refs[:count]
     refs = refs[count:]
+    kept = refs[:held]
+    refs = refs[held:]
     if own:
-        ids_ref, part_ref, part_out, high_ref, low_ref, lid_ref = refs[:6]
-        acc_ref, v_ref, col_ref, pair_ref, sem = refs[6:]
+        ids_ref, part_ref, part_out, high_out, low_out, lid_out = refs[:6] if held == 0 else refs[:5] + (None,)
+        refs = refs[6 if held == 0 else 5 :]
+    else:
+        ids_ref, part_ref, part_out = refs[:3]
+        refs = refs[3:]
+    acc_ref, v_ref, col_ref, pair_ref, sem, high_ref, low_ref, lid_ref = refs[:8]
+    if own:
         vh_ref, vl_ref = high_ref, low_ref
+        own_sem = refs[8]
     else:
-        high_any, low_any, lid_any, ids_ref, part_ref, part_out = refs[:6]
-        acc_ref, v_ref, col_ref, pair_ref, sem, high_ref, low_ref, lid_ref, vh_ref, vl_ref, own_sem = refs[6:]
+        vh_ref, vl_ref, own_sem = refs[8:]
     size = v_ref.shape[1]
     slots = high_ref.shape[0]
     tile = size // TILES
@@ -213,21 +220,25 @@
         def _(n=n):
             fetch(n).start()
 
-    held = []
-    if not own:
-        for n, (source, target) in enumerate(((high_any, high_ref), (low_any, low_ref), (lid_any, lid_ref))):
-            held.append(pltpu.make_async_copy(source, target, own_sem.at[n]))
+    copies = []
+    if held:
+        early = kept[0].shape[0]
+        places = [(kept[0], high_ref.at[0:early]), (kept[1], low_ref.at[0:early]), (kept[2], lid_ref)]
+        if held > 3:
+            places += [(kept[3], high_ref.at[early:slots]), (kept[4], low_ref.at[early:slots])]
+        copies = [pltpu.make_async_copy(*place, own_sem.at[n]) for n, place in enumerate(places)]
 
     @pl.when(alive)
     def _():
-        for copy in held:
+        for copy in copies:
             copy.start()
         acc_ref[...] = jnp.zeros_like(acc_ref)
         col_ref[...] = jnp.zeros_like(col_ref)
-        if own:
+        if own and held == 0:
             for b in range(slots // LANES):
                 row = ids_ref[0, b * LANES // tile, :, b * LANES % tile : b * LANES % tile + LANES]
                 lid_ref[b * LANES : (b + 1) * LANES, :] = jnp.transpose(jnp.broadcast_to(row, (LANES, LANES)))
+            lid_out[...] = lid_ref[...]
 
     total = jnp.int32(0)
     for n, (at, k) in enumerate(items):
@@ -236,7 +247,7 @@
             begin, end = jnp.int32(blocks), jnp.int32(-1)
             for b in range(blocks):
                 met = flag_ref[at, (k * TILES + t) * blocks + b] > 0
-                if own and b < k * TILES + t:
+                if own and b > k * TILES + t:
                     continue
                 begin = jnp.where(met, jnp.minimum(begin, b), begin)
                 end = jnp.where(met, b, end)
@@ -244,7 +255,7 @@
                 start = begin + 2 * w
                 used = jnp.minimum(start, blocks - 2)
                 pair_ref[0, total] = used
-                pair_ref[1, total] = n * TILES + t
+                pair_ref[1, total] = (k if own else n) * TILES + t
                 pair_ref[2, total] = k * TILES + t
                 pair_ref[3, total] = at
                 pair_ref[4, total] = (used == start).astype(jnp.int32)
@@ -256,11 +267,11 @@
         @pl.when(level_ref[at] >= 0)
         def _(n=n):
             fetch(n).wait()
-            by_tile(owners, v_ref.at[n], vh_ref, vl_ref, n * size)
+            by_tile(owners, v_ref.at[n], vh_ref, vl_ref, (items[n][1] if own else n) * size)
 
     @pl.when(alive)
     def _():
-        for copy in held:
+        for copy in copies:
             copy.wait()
 
         def step(i, _):
@@ -285,7 +296,7 @@
                     weight = jnp.where(lid == wanted[:, lanes], weight, 0.0)
                     row_part = row_part + weight
                     col = jnp.sum(weight.reshape(tile // 8, 8, LANES), axis=0)
-                    col_ref[v, :, lanes] += col * jnp.where(b + h > v, 1.0, 0.0) if own else col
+                    col_ref[v, :, lanes] += col * jnp.where(b + h < v, 1.0, 0.0) if own else col
                 acc_ref[half, :] = row_part
             return 0
 
@@ -302,7 +313,12 @@
         def _(n=n, at=at, k=k):
             for t in range(TILES):
                 where = slice(k * size + t * tile, k * size + (t + 1) * tile)
-                part_out[pl.ds(level_ref[at], 1), where] += jnp.sum(col_ref[n * TILES + t], axis=0, keepdims=True)
+                part_out[pl.ds(level_ref[at], 1), where] += jnp.sum(col_ref[(k if own else n) * TILES + t], axis=0, keepdims=True)
+
+    if own:
+        begin, end = items[0][1] * size, (items[-1][1] + 1) * size
+        high_out[...] = high_ref[begin:end, :]
+        low_out[...] = low_ref[begin:end, :]
 
 
 def last_body(levels, owners, mass_ref, q_ref, score_ref):
@@ -320,7 +336,7 @@
     value = mm(first, at_rank) + mm(second, at_rank) + mm(third, at_rank)
     mine = iota((owners, rows), 0) == owner
     total = jnp.sum(jnp.where(mine, value, 0.0), axis=0, keepdims=True)
-    score_ref[...] = jnp.log(total * math.exp(-SHARPNESS))
+    score_ref[...] = jnp.log(total * math.exp(-SHARPNESS)).reshape(rows)
 
 
 def body(embeddings, cluster_ids, owner_map, source_order):
@@ -398,18 +414,18 @@
             arrived[s, k] = value
         arrived["b", k] = lax.ppermute(mine[k], LINE, pairs(back_move))
 
-    tick = pl.pallas_call(
-        tick_body,
-        out_shape=out((8, LANES)),
-        in_specs=[pl.BlockSpec(memory_space=pl.ANY)],
-        out_specs=pl.BlockSpec(memory_space=VMEM),
-        name="tick",
-    )(arrived[1, 0])
+    def mark(value, through):
+        vm = pl.BlockSpec(memory_space=VMEM)
+        return pl.pallas_call(
+            tick_body, out_shape=out(through.shape), in_specs=[pl.BlockSpec(memory_space=pl.ANY), vm], out_specs=vm
+        )(value, through)
+
+    ids_of[0] = mark(arrived[1, 0], own_ids)
     keys_held = len(ids_of)
     ids, flags = call(
         functools.partial(meta_body, owners, CHUNKS),
         (out((keys_held, blocks, 1, tile)), out((8, LANES), i32)),
-        *ids_of, tick, micros=3,
+        *ids_of, micros=3,
     )
     keys = [1, "b"] + list(range(2, top + 1))
 
@@ -426,53 +442,50 @@
     part = jnp.zeros((levels, slots), jnp.float32)
 
     def gram(part, items, held, micros):
-        own = not held
+        own = items[0][0] == "own"
         visitors = [mine[k] if key == "own" else arrived[key, k] for key, k in items]
         at = tuple((0 if key == "own" else 1 + keys.index(key), k) for key, k in items)
         count = len(items)
         vm = pl.BlockSpec(memory_space=VMEM)
         any_ = pl.BlockSpec(memory_space=pl.ANY)
-        own_out = (out((slots, width), bf), out((slots, width), bf), out((slots, LANES)))
+        own_out = ()
+        if own:
+            own_out = (out((count * size, width), bf),) * 2 + ((out((slots, LANES)),) if not held else ())
         scratch = [
             VMEM((slots, LANES), jnp.float32),
             VMEM((count, size, width), jnp.float32),
-            VMEM((count * TILES, 8, tile), jnp.float32),
+            VMEM((blocks if own else count * TILES, 8, tile), jnp.float32),
             pltpu.SMEM((6, count * TILES * blocks + 1), i32),
             pltpu.SemaphoreType.DMA((count,)),
+            VMEM((slots, width), bf),
+            VMEM((slots, width), bf),
+            VMEM((slots, LANES), jnp.float32),
         ]
         if not own:
-            scratch += [
-                VMEM((slots, width), bf),
-                VMEM((slots, width), bf),
-                VMEM((slots, LANES), jnp.float32),
-                VMEM((count * size, width), bf),
-                VMEM((count * size, width), bf),
-                pltpu.SemaphoreType.DMA((3,)),
-            ]
+            scratch += [VMEM((count * size, width), bf)] * 2
+        scratch += [pltpu.SemaphoreType.DMA((5,))]
         return pl.pallas_call(
-            functools.partial(gram_body, owners, at, own),
-            out_shape=(out((levels, slots)),) + (own_out if own else ()),
+            functools.partial(gram_body, owners, at, own, len(held)),
+            out_shape=(out((levels, slots)),) + own_out,
             in_specs=[pl.BlockSpec(memory_space=pltpu.SMEM)] * 2 + [any_] * (count + len(held)) + [vm] * 2,
-            out_specs=(vm,) * (4 if own else 1),
+            out_specs=(vm,) * (1 + len(own_out)),
             scratch_shapes=scratch,
             cost_estimate=cost(micros),
             name="gram",
         )(level_of, flags, *visitors, *held, ids, part)
 
     plan = [
-        ([("own", k) for k in range(CHUNKS)], 10),
-        ([(1, 0), ("b", 0), (2, 0), (1, 1)], 12),
-        ([("b", 1), (2, 1), (1, 2)], 10),
-        ([("b", 2), (2, 2), (3, 0)], 9),
-        ([(3, 1)], 5),
-        ([(3, 2)], 5),
+        ([("own", k) for k in range(CHUNKS)], 13),
+        ([(1, 0), ("b", 0), (2, 0)], 14),
+        ([(1, 1), ("b", 1), (2, 1)], 14),
+        ([(1, 2), ("b", 2), (2, 2), (3, 0)], 17),
+        ([(3, 1)], 8),
+        ([(3, 2)], 8),
     ]
     held_here = ()
-    for n, (items, micros) in enumerate(plan):
+    for items, micros in plan:
         part, *made = gram(part, items, held_here, micros)
-        held_here = held_here or tuple(made)
-        if n == 2:
-            piece = lax.optimization_barrier((piece, part))[0]
+        held_here += tuple(made)
     total = None
     for s in range(groups):
         route = [(g * levels + z, ((z + s) % groups) * levels + g) for g in range(groups) for z in range(levels)]
@@ -481,9 +494,9 @@
     centroids = total * lax.rsqrt(jnp.mean(total * total, axis=1, keepdims=True) + 1e-6)
     parts = part.reshape(levels, CHUNKS, TILES, owners, strip).transpose(0, 3, 1, 2, 4).reshape(levels * owners, cap)
     home = lax.all_to_all(parts, BY_LEVEL, 0, 0, tiled=True)
-    score = call(functools.partial(last_body, levels, owners), out((1, rows)), home, q_info, micros=2)
-
-    return score.reshape(rows), centroids
+    score = call(functools.partial(last_body, levels, owners), out((rows,)), home, q_info, micros=2)
+
+    return score, centroids
 
 
 def solution(mesh):

time: 255 us -> 273 us (1.071)
  starting transfers between devices: 132 us -> 150 us
    all_to_all x1, starting transfers between devices: 38.8 us -> 71.2 us  [body(): home = lax.all_to_all(parts, BY_LEVEL, 0, 0, tiled=True)]
    ppermute x4, starting transfers between devices: 41.7 us -> 24.4 us  [body(): came = lax.ppermute(piece, ('grp', 'outer'), route)]
    ppermute x9, waiting for transfers between devices: 13.7 us -> 24.1 us  [body(): value = lax.ppermute(value, LINE, pairs(moves[s - 1]))]
    ppermute x4, waiting for transfers between devices: 7.79 us -> 0.01 us  [body(): came = lax.ppermute(piece, ('grp', 'outer'), route)]
    ppermute x3, starting transfers between devices: 7.1 us -> 10.4 us  [body(): ids_of.append(lax.ppermute(own_ids, LINE, pairs(direct(s))))]
  transfers between devices with their start and end apart: 24 -> 24, of which waited for: 8 -> 5; matrix products, arithmetic and copies ran while one was open for 2% -> 2% of each run, Pallas kernels for 11% -> 10%
where the time goes in v3:
time: 273 us; the launch traced here: 272 us
  starting transfers between devices  150 us (55%)
  waiting for transfers between devices  72.3 us (26%)
  Pallas kernels  37.2 us (14%)
  local copies, waits for them, and re-layouts  9.8 us (4%)
    all_to_all x1, starting transfers between devices, body(): home = lax.all_to_all(parts, BY_LEVEL, 0, 0, tiled=True)  71.2 us
    all_to_all x3, waiting for transfers between devices, body(): got.append(lax.all_to_all(send, PLANE, 0, 0, tiled=True))  41.6 us
    ppermute x9, starting transfers between devices, body(): value = lax.ppermute(value, LINE, pairs(moves[s - 1]))  24.7 us
    ppermute x4, starting transfers between devices, body(): came = lax.ppermute(piece, ('grp', 'outer'), route)  24.4 us
    ppermute x9, waiting for transfers between devices, body(): value = lax.ppermute(value, LINE, pairs(moves[s - 1]))  24.1 us
    pallas_call x6, Pallas kernels, gram(): pl.pallas_call(functools.partial(gram_body, owners, at, own, len(held)),...  20.7 us
    pallas_call x4, Pallas kernels, call(): pl.pallas_call(body, out_shape=outs, in_specs=spec, out_specs=jax.tree.ma...  15.2 us
    all_to_all x3, starting transfers between devices, body(): got.append(lax.all_to_all(send, PLANE, 0, 0, tiled=True))  12.4 us
  transfers between devices with their start and end apart: 24, of which 5 were waited for; matrix products, arithmetic and copies ran while one was open for 2% of the time, Pallas kernels for 10%

profile of v3, /device:TPU:0, one launch (start us, length us, event | category | flops | bytes accessed | tf_op | source)
XLA Modules:
  0.0 271.6 jit_solution(13013320761488041374)
XLA Ops:
  0.6 5.7 %shard_map.59 = (f32[8,72,768]{2,1,0:T(8,128)}, bf16[768,768]{1,0:T(8,128)(2,1)}, bf16[768,768]{1,0:T(8,128)(2,1)}, s32[8,768]{1,0:T(8,128)}) custom-call(f32[768,768]{1,0:T(8,128)} %x_ref.1, s32[768]{0:T(1024)} %ids_ref.1, s32[128]{0:T(128)} %om_ref.1), custom_call_target="tpu_custom_call" | custom-call | flops 5500000256 | tf_op jit(solution)/shard_map/pallas_call | solution.py:55
  6.3 5.2 %all-to-all-start = ((f32[8,72,768]{2,1,0:T(8,128)}), f32[8,72,768]{2,1,0:T(8,128)S(1)}, u32[]{:S(2)}, u32[]{:S(2)}) async-start(f32[8,72,768]{2,1,0:T(8,128)} %get-tuple-element.17), calls=%async_computation | async-start | bytes 3538944 | tf_op jit(solution)/shard_map/all_to_all | solution.py:377
  11.5 5.9 %shard_map.62 = (f32[8,72,768]{2,1,0:T(8,128)}, f32[8,72,768]{2,1,0:T(8,128)}, s32[8,768]{1,0:T(8,128)}) custom-call(bf16[768,768]{1,0:T(8,128)(2,1)} %get-tuple-element.19.high_ref, bf16[768,768]{1,0:T(8,128)(2,1)} %get-tuple-element.20.low_ref, s32[8,768]{1,0:T(8,128)} %get-tuple-element.21.info_ref, s32[768]{0:T(1024)} %so_ref.1), custom_call_target="tpu_custom_call" | custom-call | flops 6600000000 | tf_op jit(solution)/shard_map/pallas_call | solution.py:55
  17.4 17.2 %all-to-all-done = f32[8,72,768]{2,1,0:T(8,128)S(1)} async-done(((f32[8,72,768]{2,1,0:T(8,128)}), f32[8,72,768]{2,1,0:T(8,128)S(1)}, u32[]{:S(2)}, u32[]{:S(2)}) %all-to-all-start) | async-done | bytes 1769504 | tf_op jit(solution)/shard_map/all_to_all | solution.py:377
  36.3 3.6 %all-to-all-start.1 = ((f32[8,72,768]{2,1,0:T(8,128)}), f32[8,72,768]{2,1,0:T(8,128)S(1)}, u32[]{:S(2)}, u32[]{:S(2)}) async-start(f32[8,72,768]{2,1,0:T(8,128)} %get-tuple-element.24), calls=%async_computation.1 | async-start | bytes 3538944 | tf_op jit(solution)/shard_map/all_to_all | solution.py:377
  39.9 4.7 %collective-permute-start = (f32[512,768]{1,0:T(8,128)}, f32[512,768]{1,0:T(8,128)}, u32[]{:S(2)}, u32[]{:S(2)}) collective-permute-start(f32[512,768]{1,0:T(8,128)} %bitcast.5.refs_0_), channel_id=1, source_target_pairs={{0,2},{2,4},{7,5},{5,3},{8,10},{10,12},{15,13},{13,11},{16,18},{18... | collective-permute-start | bytes 4718600 | tf_op jit(solution)/shard_map/ppermute | solution.py:413
  44.6 18.4 %all-to-all-done.1 = f32[8,72,768]{2,1,0:T(8,128)S(1)} async-done(((f32[8,72,768]{2,1,0:T(8,128)}), f32[8,72,768]{2,1,0:T(8,128)S(1)}, u32[]{:S(2)}, u32[]{:S(2)}) %all-to-all-start.1) | async-done | bytes 1769504 | tf_op jit(solution)/shard_map/all_to_all | solution.py:377
  64.3 3.6 %all-to-all-start.2 = ((f32[8,72,768]{2,1,0:T(8,128)}), f32[8,72,768]{2,1,0:T(8,128)S(1)}, u32[]{:S(2)}, u32[]{:S(2)}) async-start(f32[8,72,768]{2,1,0:T(8,128)} %get-tuple-element.25), calls=%async_computation.2 | async-start | bytes 3538944 | tf_op jit(solution)/shard_map/all_to_all | solution.py:377
  69.4 3.5 %collective-permute-start.1 = (f32[8,192]{1,0:T(8,128)S(1)}, f32[8,192]{1,0:T(8,128)S(1)}, u32[]{:S(2)}, u32[]{:S(2)}) collective-permute-start(f32[8,192]{1,0:T(8,128)S(1)} %bitcast.22), channel_id=1, source_target_pairs={{0,2},{2,4},{7,5},{5,3},{8,10},{10,12},{15,13},{13,11},{16,18},{18... | collective-permute-start | bytes 18440 | tf_op jit(solution)/shard_map/ppermute | solution.py:408
  74.1 2.9 %collective-permute-start.3 = (f32[8,192]{1,0:T(8,128)S(1)}, f32[8,192]{1,0:T(8,128)}, u32[]{:S(2)}, u32[]{:S(2)}) collective-permute-start(f32[8,192]{1,0:T(8,128)S(1)} %bitcast.24), channel_id=1, source_target_pairs={{0,4},{2,6},{7,3},{5,1},{8,12},{10,14},{15,11},{13,9},{16,20},{18,... | collective-permute-start | bytes 18440 | tf_op jit(solution)/shard_map/ppermute | solution.py:408
  77.1 4.0 %collective-permute-start.4 = (f32[8,192]{1,0:T(8,128)S(1)}, f32[8,192]{1,0:T(8,128)}, u32[]{:S(2)}, u32[]{:S(2)}) collective-permute-start(f32[8,192]{1,0:T(8,128)S(1)} %bitcast.25), channel_id=1, source_target_pairs={{0,6},{7,1},{8,14},{15,9},{16,22},{23,17},{24,30},{31,25}} | collective-permute-start | bytes 18440 | tf_op jit(solution)/shard_map/ppermute | solution.py:408
  81.7 1.9 collective-permute-start.15
  84.9 6.0 %all-to-all-done.2 = f32[8,72,768]{2,1,0:T(8,128)S(1)} async-done(((f32[8,72,768]{2,1,0:T(8,128)}), f32[8,72,768]{2,1,0:T(8,128)S(1)}, u32[]{:S(2)}, u32[]{:S(2)}) %all-to-all-start.2) | async-done | bytes 1769504 | tf_op jit(solution)/shard_map/all_to_all | solution.py:377
  91.0 4.7 %collective-permute-start.8 = (f32[512,768]{1,0:T(8,128)S(1)}, f32[512,768]{1,0:T(8,128)}, u32[]{:S(2)}, u32[]{:S(2)}) collective-permute-start(f32[512,768]{1,0:T(8,128)S(1)} %bitcast.16), channel_id=1, source_target_pairs={{0,2},{2,4},{7,5},{5,3},{8,10},{10,12},{15,13},{13,11},{16,18},{18... | collective-permute-start | bytes 4718600 | tf_op jit(solution)/shard_map/ppermute | solution.py:413
  95.7 1.8 collective-permute-start.12
  98.2 3.7 %collective-permute-start.17 = (f32[16,768]{1,0:T(8,128)S(1)}, f32[16,768]{1,0:T(8,128)S(1)}, u32[]{:S(2)}, u32[]{:S(2)}) collective-permute-start(f32[16,768]{1,0:T(8,128)S(1)} %pad_maximum_fusion), channel_id=1, source_target_pairs={{0,8},{2,16},{4,24},{6,0},{8,10},{10,18},{12,26},{14,2},{16,12},{1... | collective-permute-start | bytes 147464 | tf_op jit(solution)/shard_map/ppermute | solution.py:492
  101.9 2.0 shard_map.61
  105.2 11.9 %collective-permute-start.18 = (f32[16,768]{1,0:T(8,128)S(1)}, f32[16,768]{1,0:T(8,128)S(1)}, u32[]{:S(2)}, u32[]{:S(2)}) collective-permute-start(f32[16,768]{1,0:T(8,128)S(1)} %pad_maximum_fusion), channel_id=1, source_target_pairs={{0,16},{2,24},{4,0},{6,8},{8,18},{10,26},{12,2},{14,10},{16,20},{1... | collective-permute-start | bytes 147464 | tf_op jit(solution)/shard_map/ppermute | solution.py:492
  117.1 8.1 %collective-permute-start.19 = (f32[16,768]{1,0:T(8,128)S(1)}, f32[16,768]{1,0:T(8,128)S(1)}, u32[]{:S(2)}, u32[]{:S(2)}) collective-permute-start(f32[16,768]{1,0:T(8,128)S(1)} %pad_maximum_fusion), channel_id=1, source_target_pairs={{0,24},{2,0},{4,8},{6,16},{8,26},{10,2},{12,10},{14,18},{16,28},{1... | collective-permute-start | bytes 147464 | tf_op jit(solution)/shard_map/ppermute | solution.py:492
  125.8 12.3 %gram.6 = (f32[4,1536]{1,0:T(4,128)}, bf16[1536,768]{1,0:T(8,128)(2,1)}, bf16[1536,768]{1,0:T(8,128)(2,1)}, f32[1536,128]{1,0:T(8,128)}) custom-call(s32[5]{0:T(128)} %stack.23.level_ref, s32[8,128]{1,0:T(8,128)} %get-tuple-element.18.flag_ref, f32[512,768]{1,0:T(8,128)} %bitcast.5.refs_0_, f32[512,768]{1,0:T(8,128)} %bitcast.15, f32[512,768]{1,0:T(8,128)} %bitcast.18, ...), custom_call_target="tpu_custom_call" | custom-call | flops 14300000256 | tf_op jit(solution)/shard_map/gram/pallas_call | solution.py:467
  138.2 1.8 collective-permute-start.14
  140.0 6.5 %collective-permute-start.5 = (f32[512,768]{1,0:T(8,128)}, f32[512,768]{1,0:T(8,128)}, u32[]{:S(2)}, u32[]{:S(2)}) collective-permute-start(f32[512,768]{1,0:T(8,128)} %bitcast.19), channel_id=1, source_target_pairs={{0,2},{2,4},{7,5},{5,3},{8,10},{10,12},{15,13},{13,11},{16,18},{18... | collective-permute-start | bytes 4718600 | tf_op jit(solution)/shard_map/ppermute | solution.py:413
  146.6 1.8 collective-permute-start.11
  149.2 1.8 collective-permute-start.13
  151.1 1.9 gram.7.refs_7_
  153.0 24.1 %collective-permute-done.5.refs_0_ = f32[512,768]{1,0:T(8,128)} collective-permute-done((f32[512,768]{1,0:T(8,128)}, f32[512,768]{1,0:T(8,128)}, u32[]{:S(2)}, u32[]{:S(2)}) %collective-permute-start.5) | collective-permute-done | bytes 1572896 | tf_op jit(solution)/shard_map/ppermute | solution.py:413
  177.0 1.8 collective-permute-start.6
  178.9 1.8 collective-permute-start.10
  180.7 1.7 gram.8.refs_8_
  183.2 1.8 gram.9.refs_5_
  190.9 71.2 %all-to-all-start.3 = ((f32[32,1,192]{2,1,0:T(1,128)}), f32[32,1,192]{2,1,0:T(1,128)S(1)}, u32[]{:S(2)}, u32[]{:S(2)}) async-start(f32[32,1,192]{2,1,0:T(1,128)} %all_to_all.19), calls=%async_computation.3 | async-start | bytes 65536 | tf_op jit(solution)/shard_map/all_to_all | solution.py:496
  262.9 6.6 %all-to-all-done.3 = f32[32,1,192]{2,1,0:T(1,128)S(1)} async-done(((f32[32,1,192]{2,1,0:T(1,128)}), f32[32,1,192]{2,1,0:T(1,128)S(1)}, u32[]{:S(2)}, u32[]{:S(2)}) %all-to-all-start.3) | async-done | bytes 24608 | tf_op jit(solution)/shard_map/all_to_all | solution.py:496
  (60 shorter events, 20.7 us)
Async XLA Ops:
  6.3 28.3 %all-to-all-start = ((f32[8,72,768]{2,1,0:T(8,128)}), f32[8,72,768]{2,1,0:T(8,128)S(1)}, u32[]{:S(2)}, u32[]{:S(2)}) async-start(f32[8,72,768]{2,1,0:T(8,128)} %get-tuple-element.17), calls=%async_computation | async-start | bytes 3538944 | tf_op jit(solution)/shard_map/all_to_all | solution.py:377
  34.6 1.7 copy-start
  36.3 26.6 %all-to-all-start.1 = ((f32[8,72,768]{2,1,0:T(8,128)}), f32[8,72,768]{2,1,0:T(8,128)S(1)}, u32[]{:S(2)}, u32[]{:S(2)}) async-start(f32[8,72,768]{2,1,0:T(8,128)} %get-tuple-element.24), calls=%async_computation.1 | async-start | bytes 3538944 | tf_op jit(solution)/shard_map/all_to_all | solution.py:377
  39.9 41.7 %collective-permute-start = (f32[512,768]{1,0:T(8,128)}, f32[512,768]{1,0:T(8,128)}, u32[]{:S(2)}, u32[]{:S(2)}) collective-permute-start(f32[512,768]{1,0:T(8,128)} %bitcast.5.refs_0_), channel_id=1, source_target_pairs={{0,2},{2,4},{7,5},{5,3},{8,10},{10,12},{15,13},{13,11},{16,18},{18... | collective-permute-start | bytes 4718600 | tf_op jit(solution)/shard_map/ppermute | solution.py:413
  64.3 26.6 %all-to-all-start.2 = ((f32[8,72,768]{2,1,0:T(8,128)}), f32[8,72,768]{2,1,0:T(8,128)S(1)}, u32[]{:S(2)}, u32[]{:S(2)}) async-start(f32[8,72,768]{2,1,0:T(8,128)} %get-tuple-element.25), calls=%async_computation.2 | async-start | bytes 3538944 | tf_op jit(solution)/shard_map/all_to_all | solution.py:377
  69.4 14.2 %copy-start.4 = (f32[8,1,192]{2,0,1:T(8,128)}, f32[8,1,192]{2,0,1:T(8,128)S(1)}, u32[]{:S(2)}) copy-start(f32[8,1,192]{2,0,1:T(8,128)S(1)} %copy.16) | copy-start | bytes 18436
  69.4 21.5 %collective-permute-start.1 = (f32[8,192]{1,0:T(8,128)S(1)}, f32[8,192]{1,0:T(8,128)S(1)}, u32[]{:S(2)}, u32[]{:S(2)}) collective-permute-start(f32[8,192]{1,0:T(8,128)S(1)} %bitcast.22), channel_id=1, source_target_pairs={{0,2},{2,4},{7,5},{5,3},{8,10},{10,12},{15,13},{13,11},{16,18},{18... | collective-permute-start | bytes 18440 | tf_op jit(solution)/shard_map/ppermute | solution.py:408
  72.9 22.8 %collective-permute-start.2 = (f32[8,192]{1,0:T(8,128)S(1)}, f32[8,192]{1,0:T(8,128)}, u32[]{:S(2)}, u32[]{:S(2)}) collective-permute-start(f32[8,192]{1,0:T(8,128)S(1)} %bitcast.23), channel_id=1, source_target_pairs={{6,4},{1,3},{14,12},{9,11},{22,20},{17,19},{30,28},{25,27}} | collective-permute-start | bytes 18440 | tf_op jit(solution)/shard_map/ppermute | solution.py:409
  74.1 23.3 %collective-permute-start.3 = (f32[8,192]{1,0:T(8,128)S(1)}, f32[8,192]{1,0:T(8,128)}, u32[]{:S(2)}, u32[]{:S(2)}) collective-permute-start(f32[8,192]{1,0:T(8,128)S(1)} %bitcast.24), channel_id=1, source_target_pairs={{0,4},{2,6},{7,3},{5,1},{8,12},{10,14},{15,11},{13,9},{16,20},{18,... | collective-permute-start | bytes 18440 | tf_op jit(solution)/shard_map/ppermute | solution.py:408
  77.1 21.1 %collective-permute-start.4 = (f32[8,192]{1,0:T(8,128)S(1)}, f32[8,192]{1,0:T(8,128)}, u32[]{:S(2)}, u32[]{:S(2)}) collective-permute-start(f32[8,192]{1,0:T(8,128)S(1)} %bitcast.25), channel_id=1, source_target_pairs={{0,6},{7,1},{8,14},{15,9},{16,22},{23,17},{24,30},{31,25}} | collective-permute-start | bytes 18440 | tf_op jit(solution)/shard_map/ppermute | solution.py:408
  81.6 9.3 %copy-start.3 = (f32[8,768]{1,0:T(8,128)S(1)}, f32[8,768]{1,0:T(8,128)}, u32[]{:S(2)}) copy-start(f32[8,768]{1,0:T(8,128)} %slice_reduce_fusion.1) | copy-start | bytes 73732
  81.6 9.3 %copy-start.1 = (f32[8,64,768]{2,1,0:T(8,128)S(1)}, f32[8,64,768]{2,1,0:T(8,128)}, u32[]{:S(2)}) copy-start(f32[8,64,768]{2,1,0:T(8,128)} %slice.26) | copy-start | bytes 4718596
  81.7 65.0 %collective-permute-start.15 = (f32[512,768]{1,0:T(8,128)}, f32[512,768]{1,0:T(8,128)}, u32[]{:S(2)}, u32[]{:S(2)}) collective-permute-start(f32[512,768]{1,0:T(8,128)} %bitcast.5.refs_0_), channel_id=1, source_target_pairs={{6,4},{1,3},{14,12},{9,11},{22,20},{17,19},{30,28},{25,27}} | collective-permute-start | bytes 4718600 | tf_op jit(solution)/shard_map/ppermute | solution.py:415
  90.9 10.9 %copy-start.7 = (f32[8,192]{1,0:T(8,128)}, f32[8,192]{1,0:T(8,128)S(1)}, u32[]{:S(2)}) copy-start(f32[8,192]{1,0:T(8,128)S(1)} %collective-permute-done.1.refs_1_) | copy-start | bytes 18436
  91.0 57.5 %collective-permute-start.8 = (f32[512,768]{1,0:T(8,128)S(1)}, f32[512,768]{1,0:T(8,128)}, u32[]{:S(2)}, u32[]{:S(2)}) collective-permute-start(f32[512,768]{1,0:T(8,128)S(1)} %bitcast.16), channel_id=1, source_target_pairs={{0,2},{2,4},{7,5},{5,3},{8,10},{10,12},{15,13},{13,11},{16,18},{18... | collective-permute-start | bytes 4718600 | tf_op jit(solution)/shard_map/ppermute | solution.py:413
  95.7 53.5 %collective-permute-start.12 = (f32[512,768]{1,0:T(8,128)}, f32[512,768]{1,0:T(8,128)}, u32[]{:S(2)}, u32[]{:S(2)}) collective-permute-start(f32[512,768]{1,0:T(8,128)} %collective-permute-done.value_ref.refs_0_), channel_id=1, source_target_pairs={{2,4},{4,6},{5,3},{3,1},{10,12},{12,14},{13,11},{11,9},{18,20},{20... | collective-permute-start | bytes 4718600 | tf_op jit(solution)/shard_map/ppermute | solution.py:413
  97.5 7.7 %collective-permute-start.16 = (f32[16,768]{1,0:T(8,128)S(1)}, f32[16,768]{1,0:T(8,128)S(1)}, u32[]{:S(2)}, u32[]{:S(2)}) collective-permute-start(f32[16,768]{1,0:T(8,128)S(1)} %pad_maximum_fusion), channel_id=1, source_target_pairs={{0,0},{2,8},{4,16},{6,24},{8,2},{10,10},{12,18},{14,26},{16,4},{18... | collective-permute-start | bytes 147464 | tf_op jit(solution)/shard_map/ppermute | solution.py:492
  98.2 18.9 %collective-permute-start.17 = (f32[16,768]{1,0:T(8,128)S(1)}, f32[16,768]{1,0:T(8,128)S(1)}, u32[]{:S(2)}, u32[]{:S(2)}) collective-permute-start(f32[16,768]{1,0:T(8,128)S(1)} %pad_maximum_fusion), channel_id=1, source_target_pairs={{0,8},{2,16},{4,24},{6,0},{8,10},{10,18},{12,26},{14,2},{16,12},{1... | collective-permute-start | bytes 147464 | tf_op jit(solution)/shard_map/ppermute | solution.py:492
  105.2 32.9 %collective-permute-start.18 = (f32[16,768]{1,0:T(8,128)S(1)}, f32[16,768]{1,0:T(8,128)S(1)}, u32[]{:S(2)}, u32[]{:S(2)}) collective-permute-start(f32[16,768]{1,0:T(8,128)S(1)} %pad_maximum_fusion), channel_id=1, source_target_pairs={{0,16},{2,24},{4,0},{6,8},{8,18},{10,26},{12,2},{14,10},{16,20},{1... | collective-permute-start | bytes 147464 | tf_op jit(solution)/shard_map/ppermute | solution.py:492
  117.1 22.9 %collective-permute-start.19 = (f32[16,768]{1,0:T(8,128)S(1)}, f32[16,768]{1,0:T(8,128)S(1)}, u32[]{:S(2)}, u32[]{:S(2)}) collective-permute-start(f32[16,768]{1,0:T(8,128)S(1)} %pad_maximum_fusion), channel_id=1, source_target_pairs={{0,24},{2,0},{4,8},{6,16},{8,26},{10,2},{12,10},{14,18},{16,28},{1... | collective-permute-start | bytes 147464 | tf_op jit(solution)/shard_map/ppermute | solution.py:492
  125.8 12.3 %copy-start.2 = (f32[8,64,768]{2,1,0:T(8,128)S(1)}, f32[8,64,768]{2,1,0:T(8,128)}, u32[]{:S(2)}) copy-start(f32[8,64,768]{2,1,0:T(8,128)} %slice.26) | copy-start | bytes 4718596
  138.2 42.6 %collective-permute-start.14 = (f32[512,768]{1,0:T(8,128)S(1)}, f32[512,768]{1,0:T(8,128)}, u32[]{:S(2)}, u32[]{:S(2)}) collective-permute-start(f32[512,768]{1,0:T(8,128)S(1)} %bitcast.17), channel_id=1, source_target_pairs={{6,4},{1,3},{14,12},{9,11},{22,20},{17,19},{30,28},{25,27}} | collective-permute-start | bytes 4718600 | tf_op jit(solution)/shard_map/ppermute | solution.py:415
  140.0 37.1 %collective-permute-start.5 = (f32[512,768]{1,0:T(8,128)}, f32[512,768]{1,0:T(8,128)}, u32[]{:S(2)}, u32[]{:S(2)}) collective-permute-start(f32[512,768]{1,0:T(8,128)} %bitcast.19), channel_id=1, source_target_pairs={{0,2},{2,4},{7,5},{5,3},{8,10},{10,12},{15,13},{13,11},{16,18},{18... | collective-permute-start | bytes 4718600 | tf_op jit(solution)/shard_map/ppermute | solution.py:413
  146.6 36.6 %collective-permute-start.11 = (f32[512,768]{1,0:T(8,128)}, f32[512,768]{1,0:T(8,128)}, u32[]{:S(2)}, u32[]{:S(2)}) collective-permute-start(f32[512,768]{1,0:T(8,128)} %bitcast.20), channel_id=1, source_target_pairs={{6,4},{1,3},{14,12},{9,11},{22,20},{17,19},{30,28},{25,27}} | collective-permute-start | bytes 4718600 | tf_op jit(solution)/shard_map/ppermute | solution.py:415
  148.4 30.4 %collective-permute-start.9 = (f32[512,768]{1,0:T(8,128)}, f32[512,768]{1,0:T(8,128)S(1)}, u32[]{:S(2)}, u32[]{:S(2)}) collective-permute-start(f32[512,768]{1,0:T(8,128)} %collective-permute-done.8.refs_0_), channel_id=1, source_target_pairs={{2,4},{4,6},{5,3},{3,1},{10,12},{12,14},{13,11},{11,9},{18,20},{20... | collective-permute-start | bytes 4718600 | tf_op jit(solution)/shard_map/ppermute | solution.py:413
  149.2 34.0 %collective-permute-start.13 = (f32[512,768]{1,0:T(8,128)}, f32[512,768]{1,0:T(8,128)}, u32[]{:S(2)}, u32[]{:S(2)}) collective-permute-start(f32[512,768]{1,0:T(8,128)} %collective-permute-done.12.refs_2_), channel_id=1, source_target_pairs={{4,6},{3,1},{12,14},{11,9},{20,22},{19,17},{28,30},{27,25}} | collective-permute-start | bytes 4718600 | tf_op jit(solution)/shard_map/ppermute | solution.py:413
  177.0 5.4 %collective-permute-start.6 = (f32[512,768]{1,0:T(8,128)}, f32[512,768]{1,0:T(8,128)}, u32[]{:S(2)}, u32[]{:S(2)}) collective-permute-start(f32[512,768]{1,0:T(8,128)} %collective-permute-done.5.refs_0_), channel_id=1, source_target_pairs={{2,4},{4,6},{5,3},{3,1},{10,12},{12,14},{13,11},{11,9},{18,20},{20... | collective-permute-start | bytes 4718600 | tf_op jit(solution)/shard_map/ppermute | solution.py:413
  178.9 1.9 copy-start.5
  178.9 6.2 %collective-permute-start.10 = (f32[512,768]{1,0:T(8,128)S(1)}, f32[512,768]{1,0:T(8,128)}, u32[]{:S(2)}, u32[]{:S(2)}) collective-permute-start(f32[512,768]{1,0:T(8,128)S(1)} %collective-permute-done.9.refs_2_), channel_id=1, source_target_pairs={{4,6},{3,1},{12,14},{11,9},{20,22},{19,17},{28,30},{27,25}} | collective-permute-start | bytes 4718600 | tf_op jit(solution)/shard_map/ppermute | solution.py:413
  182.4 4.1 %collective-permute-start.7 = (f32[512,768]{1,0:T(8,128)}, f32[512,768]{1,0:T(8,128)S(1)}, u32[]{:S(2)}, u32[]{:S(2)}) collective-permute-start(f32[512,768]{1,0:T(8,128)} %collective-permute-done.6.refs_2_), channel_id=1, source_target_pairs={{4,6},{3,1},{12,14},{11,9},{20,22},{19,17},{28,30},{27,25}} | collective-permute-start | bytes 4718600 | tf_op jit(solution)/shard_map/ppermute | solution.py:413
  186.6 1.2 copy-start.6
  190.9 78.5 %all-to-all-start.3 = ((f32[32,1,192]{2,1,0:T(1,128)}), f32[32,1,192]{2,1,0:T(1,128)S(1)}, u32[]{:S(2)}, u32[]{:S(2)}) async-start(f32[32,1,192]{2,1,0:T(1,128)} %all_to_all.19), calls=%async_computation.3 | async-start | bytes 65536 | tf_op jit(solution)/shard_map/all_to_all | solution.py:496

commit v4 on v3

--- a/solution.py
+++ b/solution.py
@@ -102,14 +102,15 @@
     high_ref[...] = high
     low_ref[...] = low
     chunk_ref[:, 0:per, :] = chunk_rows(owner, rank, high, low, 0, owners, per).reshape(owners, per, width)
-    at_rank = hot(iota((width, rows), 0) == rank)
+    at_rank = hot(iota((cap, rows), 0) == rank)
     coarse = (ids + 1) // 16
     fine = ids + 1 - coarse * 16
     coarse = jnp.where(mine, coarse.astype(jnp.float32), 0.0).astype(jnp.bfloat16)
     fine = jnp.where(mine, fine.astype(jnp.float32), 0.0).astype(jnp.bfloat16)
     sid = mm_nt(coarse, at_rank) * 16.0 + mm_nt(fine, at_rank) - 1.0
     for p in range(owners):
-        chunk_ref[p, per:, :] = jnp.broadcast_to(sid[p : p + 1, :], chunk_ref[p, per:, :].shape)
+        chunk_ref[p, per:, :] = jnp.zeros(chunk_ref[p, per:, :].shape, jnp.float32)
+        chunk_ref[p, per : per + 1, 0:cap] = sid[p : p + 1, :]
 
 
 def back_body(owners, per, chunks, held, high_ref, low_ref, info_ref, so_ref, *outs):
@@ -122,10 +123,9 @@
     clusters = owners * held
     pick = hot(iota((clusters, rows), 0) == position)
     sums = (mm(pick, high) + mm(pick, low)).reshape(owners, held, width)
-    share = held // (chunks - 1)
     for k in range(1, chunks):
         outs[k - 1][:, 0:per, :] = chunk_rows(owner, rank, high, low, k, owners, per).reshape(owners, per, width)
-        outs[k - 1][:, per:, :] = sums[:, (k - 1) * share : k * share, :]
+    outs[0][:, per:, :] = sums
     q_ref = outs[chunks - 1]
     target = hot(iota((rows, rows), 0) == so_ref[...].reshape(1, rows))
     values = info_ref[...].astype(jnp.float32).astype(jnp.bfloat16)
@@ -351,18 +351,17 @@
     per = cap // CHUNKS
     size = owners * per
     slots = CHUNKS * size
-    share = held // (CHUNKS - 1)
     bf, i32 = jnp.bfloat16, jnp.int32
-    dealt = out((owners, per + share, width))
+    dealt = [out((owners, per + extra, width)) for extra in (8, held, 0)]
 
     first, high, low, info = call(
         functools.partial(front_body, owners, per, cap),
-        (dealt, out((rows, width), bf), out((rows, width), bf), out((8, rows), i32)),
+        (dealt[0], out((rows, width), bf), out((rows, width), bf), out((8, rows), i32)),
         embeddings, cluster_ids, owner_map, micros=5,
     )
     back = call(
         functools.partial(back_body, owners, per, CHUNKS, held),
-        (dealt,) * (CHUNKS - 1) + (out((8, rows), i32),),
+        tuple(dealt[1:]) + (out((8, rows), i32),),
         high, low, info, source_order, micros=6,
     )
     sends = (first,) + tuple(back[: CHUNKS - 1])
@@ -377,7 +376,7 @@
         got.append(lax.all_to_all(send, PLANE, 0, 0, tiled=True))
         mine.append(got[k][:, :per, :].reshape(size, width))
     own_ids = got[0][:, per, :cap].reshape(owners, cap)
-    piece = jnp.concatenate([jnp.sum(got[k][:, per:, :], axis=0) for k in range(1, CHUNKS)], axis=0)
+    piece = jnp.sum(got[1][:, per:, :], axis=0)
 
     level = lax.axis_index("outer")
     down = lax.axis_index("inner") % 2
@@ -477,10 +476,10 @@
     plan = [
         ([("own", k) for k in range(CHUNKS)], 13),
         ([(1, 0), ("b", 0), (2, 0)], 14),
-        ([(1, 1), ("b", 1), (2, 1)], 14),
-        ([(1, 2), ("b", 2), (2, 2), (3, 0)], 17),
+        ([(1, 1), ("b", 1)], 11),
+        ([(2, 1), (1, 2), (2, 2), (3, 0)], 17),
         ([(3, 1)], 8),
-        ([(3, 2)], 8),
+        ([("b", 2), (3, 2)], 8),
     ]
     held_here = ()
     for items, micros in plan:

time: 273 us -> 245 us (0.90)
  starting transfers between devices: 150 us -> 103 us
  waiting for transfers between devices: 72.3 us -> 92.1 us
    all_to_all x1, starting transfers between devices: 71.2 us -> 42 us  [body(): home = lax.all_to_all(parts, BY_LEVEL, 0, 0, tiled=True)]
    ppermute x9, waiting for transfers between devices: 24.1 us -> 43.8 us  [body(): value = lax.ppermute(value, LINE, pairs(moves[s - 1]))]
    ppermute x4, starting transfers between devices: 24.4 us -> 10.2 us  [body(): came = lax.ppermute(piece, ('grp', 'outer'), route)]
    ppermute x4, waiting for transfers between devices: 0.01 us -> 4.07 us  [body(): came = lax.ppermute(piece, ('grp', 'outer'), route)]
    all_to_all x3, waiting for transfers between devices: 41.6 us -> 37.6 us  [body(): got.append(lax.all_to_all(send, PLANE, 0, 0, tiled=True))]
    ppermute x9, starting transfers between devices: 24.7 us -> 21.5 us  [body(): value = lax.ppermute(value, LINE, pairs(moves[s - 1]))]
  transfers between devices with their start and end apart: 24 -> 24, of which waited for: 5 -> 6; matrix products, arithmetic and copies ran while one was open for 2% -> 2% of each run, Pallas kernels for 10% -> 12%
where the time goes in v4:
time: 245 us; the launch traced here: 243 us
  starting transfers between devices  103 us (42%)
  waiting for transfers between devices  92.1 us (38%)
  Pallas kernels  36.7 us (15%)
  local copies, waits for them, and re-layouts  8.94 us (4%)
    ppermute x9, waiting for transfers between devices, body(): value = lax.ppermute(value, LINE, pairs(moves[s - 1]))  43.8 us
    all_to_all x1, starting transfers between devices, body(): home = lax.all_to_all(parts, BY_LEVEL, 0, 0, tiled=True)  42 us
    all_to_all x3, waiting for transfers between devices, body(): got.append(lax.all_to_all(send, PLANE, 0, 0, tiled=True))  37.6 us
    ppermute x9, starting transfers between devices, body(): value = lax.ppermute(value, LINE, pairs(moves[s - 1]))  21.5 us
    pallas_call x6, Pallas kernels, gram(): pl.pallas_call(functools.partial(gram_body, owners, at, own, len(held)),...  20.7 us
    pallas_call x4, Pallas kernels, call(): pl.pallas_call(body, out_shape=outs, in_specs=spec, out_specs=jax.tree.ma...  14.7 us
    all_to_all x3, starting transfers between devices, body(): got.append(lax.all_to_all(send, PLANE, 0, 0, tiled=True))  12.4 us
    ppermute x3, starting transfers between devices, body(): ids_of.append(lax.ppermute(own_ids, LINE, pairs(direct(s))))  10.4 us
  transfers between devices with their start and end apart: 24, of which 6 were waited for; matrix products, arithmetic and copies ran while one was open for 2% of the time, Pallas kernels for 12%

profile of v4, /device:TPU:0, one launch (start us, length us, event | category | flops | bytes accessed | tf_op | source)
XLA Modules:
  0.0 243.2 jit_solution(5204312806581834480)
XLA Ops:
  0.6 5.2 %shard_map.59 = (f32[8,72,768]{2,1,0:T(8,128)}, bf16[768,768]{1,0:T(8,128)(2,1)}, bf16[768,768]{1,0:T(8,128)(2,1)}, s32[8,768]{1,0:T(8,128)}) custom-call(f32[768,768]{1,0:T(8,128)} %x_ref.1, s32[768]{0:T(1024)} %ids_ref.1, s32[128]{0:T(128)} %om_ref.1), custom_call_target="tpu_custom_call" | custom-call | flops 5500000256 | tf_op jit(solution)/shard_map/pallas_call | solution.py:55
  5.8 5.2 %all-to-all-start = ((f32[8,72,768]{2,1,0:T(8,128)}), f32[8,72,768]{2,1,0:T(8,128)S(1)}, u32[]{:S(2)}, u32[]{:S(2)}) async-start(f32[8,72,768]{2,1,0:T(8,128)} %get-tuple-element.17), calls=%async_computation | async-start | bytes 3538944 | tf_op jit(solution)/shard_map/all_to_all | solution.py:376
  11.0 5.9 %shard_map.62 = (f32[8,80,768]{2,1,0:T(8,128)}, f32[8,64,768]{2,1,0:T(8,128)}, s32[8,768]{1,0:T(8,128)}) custom-call(bf16[768,768]{1,0:T(8,128)(2,1)} %get-tuple-element.19.high_ref, bf16[768,768]{1,0:T(8,128)(2,1)} %get-tuple-element.20.low_ref, s32[8,768]{1,0:T(8,128)} %get-tuple-element.21.info_ref, s32[768]{0:T(1024)} %so_ref.1), custom_call_target="tpu_custom_call" | custom-call | flops 6600000000 | tf_op jit(solution)/shard_map/pallas_call | solution.py:55
  16.9 17.2 %all-to-all-done = f32[8,72,768]{2,1,0:T(8,128)S(1)} async-done(((f32[8,72,768]{2,1,0:T(8,128)}), f32[8,72,768]{2,1,0:T(8,128)S(1)}, u32[]{:S(2)}, u32[]{:S(2)}) %all-to-all-start) | async-done | bytes 1769504 | tf_op jit(solution)/shard_map/all_to_all | solution.py:376
  35.8 3.6 %all-to-all-start.1 = ((f32[8,80,768]{2,1,0:T(8,128)}), f32[8,80,768]{2,1,0:T(8,128)S(1)}, u32[]{:S(2)}, u32[]{:S(2)}) async-start(f32[8,80,768]{2,1,0:T(8,128)} %get-tuple-element.24), calls=%async_computation.1 | async-start | bytes 3932160 | tf_op jit(solution)/shard_map/all_to_all | solution.py:376
  39.4 4.7 %collective-permute-start = (f32[512,768]{1,0:T(8,128)}, f32[512,768]{1,0:T(8,128)}, u32[]{:S(2)}, u32[]{:S(2)}) collective-permute-start(f32[512,768]{1,0:T(8,128)} %bitcast.5.refs_0_), channel_id=1, source_target_pairs={{0,2},{2,4},{7,5},{5,3},{8,10},{10,12},{15,13},{13,11},{16,18},{18... | collective-permute-start | bytes 4718600 | tf_op jit(solution)/shard_map/ppermute | solution.py:412
  44.1 20.4 %all-to-all-done.1 = f32[8,80,768]{2,1,0:T(8,128)S(1)} async-done(((f32[8,80,768]{2,1,0:T(8,128)}), f32[8,80,768]{2,1,0:T(8,128)S(1)}, u32[]{:S(2)}, u32[]{:S(2)}) %all-to-all-start.1) | async-done | bytes 1966112 | tf_op jit(solution)/shard_map/all_to_all | solution.py:376
  65.8 3.6 %all-to-all-start.2 = ((f32[8,64,768]{2,1,0:T(8,128)}), f32[8,64,768]{2,1,0:T(8,128)S(1)}, u32[]{:S(2)}, u32[]{:S(2)}) async-start(f32[8,64,768]{2,1,0:T(8,128)} %get-tuple-element.25), calls=%async_computation.2 | async-start | bytes 3145728 | tf_op jit(solution)/shard_map/all_to_all | solution.py:376
  71.0 3.5 %collective-permute-start.1 = (f32[8,192]{1,0:T(8,128)S(1)}, f32[8,192]{1,0:T(8,128)S(1)}, u32[]{:S(2)}, u32[]{:S(2)}) collective-permute-start(f32[8,192]{1,0:T(8,128)S(1)} %bitcast.22), channel_id=1, source_target_pairs={{0,2},{2,4},{7,5},{5,3},{8,10},{10,12},{15,13},{13,11},{16,18},{18... | collective-permute-start | bytes 18440 | tf_op jit(solution)/shard_map/ppermute | solution.py:407
  75.7 2.9 %collective-permute-start.3 = (f32[8,192]{1,0:T(8,128)S(1)}, f32[8,192]{1,0:T(8,128)}, u32[]{:S(2)}, u32[]{:S(2)}) collective-permute-start(f32[8,192]{1,0:T(8,128)S(1)} %bitcast.24), channel_id=1, source_target_pairs={{0,4},{2,6},{7,3},{5,1},{8,12},{10,14},{15,11},{13,9},{16,20},{18,... | collective-permute-start | bytes 18440 | tf_op jit(solution)/shard_map/ppermute | solution.py:407
  78.6 3.9 %collective-permute-start.4 = (f32[8,192]{1,0:T(8,128)S(1)}, f32[8,192]{1,0:T(8,128)}, u32[]{:S(2)}, u32[]{:S(2)}) collective-permute-start(f32[8,192]{1,0:T(8,128)S(1)} %bitcast.25), channel_id=1, source_target_pairs={{0,6},{7,1},{8,14},{15,9},{16,22},{23,17},{24,30},{31,25}} | collective-permute-start | bytes 18440 | tf_op jit(solution)/shard_map/ppermute | solution.py:407
  82.6 1.8 collective-permute-start.15
  88.0 2.5 %collective-permute-start.17 = (f32[16,768]{1,0:T(8,128)}, f32[16,768]{1,0:T(8,128)S(1)}, u32[]{:S(2)}, u32[]{:S(2)}) collective-permute-start(f32[16,768]{1,0:T(8,128)} %slice_reduce_fusion), channel_id=1, source_target_pairs={{0,8},{2,16},{4,24},{6,0},{8,10},{10,18},{12,26},{14,2},{16,12},{1... | collective-permute-start | bytes 147464 | tf_op jit(solution)/shard_map/ppermute | solution.py:491
  90.4 3.7 %collective-permute-start.18 = (f32[16,768]{1,0:T(8,128)}, f32[16,768]{1,0:T(8,128)S(1)}, u32[]{:S(2)}, u32[]{:S(2)}) collective-permute-start(f32[16,768]{1,0:T(8,128)} %slice_reduce_fusion), channel_id=1, source_target_pairs={{0,16},{2,24},{4,0},{6,8},{8,18},{10,26},{12,2},{14,10},{16,20},{1... | collective-permute-start | bytes 147464 | tf_op jit(solution)/shard_map/ppermute | solution.py:491
  94.1 2.4 collective-permute-start.19
  96.5 2.0 shard_map.61
  98.6 1.8 collective-permute-start.12
  100.4 4.1 %collective-permute-done.17 = f32[16,768]{1,0:T(8,128)S(1)} collective-permute-done((f32[16,768]{1,0:T(8,128)}, f32[16,768]{1,0:T(8,128)S(1)}, u32[]{:S(2)}, u32[]{:S(2)}) %collective-permute-start.17) | collective-permute-done | bytes 49184 | tf_op jit(solution)/shard_map/ppermute | solution.py:491
  104.4 5.0 %collective-permute-start.9 = (f32[512,768]{1,0:T(8,128)S(1)}, f32[512,768]{1,0:T(8,128)}, u32[]{:S(2)}, u32[]{:S(2)}) collective-permute-start(f32[512,768]{1,0:T(8,128)S(1)} %bitcast.19), channel_id=1, source_target_pairs={{0,2},{2,4},{7,5},{5,3},{8,10},{10,12},{15,13},{13,11},{16,18},{18... | collective-permute-start | bytes 4718600 | tf_op jit(solution)/shard_map/ppermute | solution.py:412
  109.5 1.8 collective-permute-start.14
  111.3 3.0 %collective-permute-start.6 = (f32[512,768]{1,0:T(8,128)S(1)}, f32[512,768]{1,0:T(8,128)}, u32[]{:S(2)}, u32[]{:S(2)}) collective-permute-start(f32[512,768]{1,0:T(8,128)S(1)} %bitcast.15), channel_id=1, source_target_pairs={{0,2},{2,4},{7,5},{5,3},{8,10},{10,12},{15,13},{13,11},{16,18},{18... | collective-permute-start | bytes 4718600 | tf_op jit(solution)/shard_map/ppermute | solution.py:412
  115.0 12.2 %gram.6 = (f32[4,1536]{1,0:T(4,128)}, bf16[1536,768]{1,0:T(8,128)(2,1)}, bf16[1536,768]{1,0:T(8,128)(2,1)}, f32[1536,128]{1,0:T(8,128)}) custom-call(s32[5]{0:T(128)} %stack.23.level_ref, s32[8,128]{1,0:T(8,128)} %get-tuple-element.18.flag_ref, f32[512,768]{1,0:T(8,128)} %bitcast.5.refs_0_, f32[512,768]{1,0:T(8,128)} %bitcast.18, f32[512,768]{1,0:T(8,128)} %bitcast.16, ...), custom_call_target="tpu_custom_call" | custom-call | flops 14300000256 | tf_op jit(solution)/shard_map/gram/pallas_call | solution.py:466
  127.3 1.8 collective-permute-start.5
  129.1 1.8 collective-permute-start.13
  130.9 12.2 %collective-permute-done.9.refs_0_ = f32[512,768]{1,0:T(8,128)} collective-permute-done((f32[512,768]{1,0:T(8,128)S(1)}, f32[512,768]{1,0:T(8,128)}, u32[]{:S(2)}, u32[]{:S(2)}) %collective-permute-start.9) | collective-permute-done | bytes 1572896 | tf_op jit(solution)/shard_map/ppermute | solution.py:412
  143.1 1.8 collective-permute-start.10
  144.9 31.6 %collective-permute-done.6.refs_1_ = f32[512,768]{1,0:T(8,128)} collective-permute-done((f32[512,768]{1,0:T(8,128)S(1)}, f32[512,768]{1,0:T(8,128)}, u32[]{:S(2)}, u32[]{:S(2)}) %collective-permute-start.6) | collective-permute-done | bytes 1572896 | tf_op jit(solution)/shard_map/ppermute | solution.py:412
  177.2 1.9 gram.7.refs_6_
  180.8 1.9 collective-permute-start.11
  183.9 1.8 gram.9.refs_5_
  191.7 42.0 %all-to-all-start.3 = ((f32[32,1,192]{2,1,0:T(1,128)}), f32[32,1,192]{2,1,0:T(1,128)S(1)}, u32[]{:S(2)}, u32[]{:S(2)}) async-start(f32[32,1,192]{2,1,0:T(1,128)} %all_to_all.19), calls=%async_computation.3 | async-start | bytes 65536 | tf_op jit(solution)/shard_map/all_to_all | solution.py:495
  234.4 6.6 %all-to-all-done.3 = f32[32,1,192]{2,1,0:T(1,128)S(1)} async-done(((f32[32,1,192]{2,1,0:T(1,128)}), f32[32,1,192]{2,1,0:T(1,128)S(1)}, u32[]{:S(2)}, u32[]{:S(2)}) %all-to-all-start.3) | async-done | bytes 24608 | tf_op jit(solution)/shard_map/all_to_all | solution.py:495
  (55 shorter events, 22.4 us)
Async XLA Ops:
  5.8 28.3 %all-to-all-start = ((f32[8,72,768]{2,1,0:T(8,128)}), f32[8,72,768]{2,1,0:T(8,128)S(1)}, u32[]{:S(2)}, u32[]{:S(2)}) async-start(f32[8,72,768]{2,1,0:T(8,128)} %get-tuple-element.17), calls=%async_computation | async-start | bytes 3538944 | tf_op jit(solution)/shard_map/all_to_all | solution.py:376
  34.1 1.7 copy-start
  35.8 28.7 %all-to-all-start.1 = ((f32[8,80,768]{2,1,0:T(8,128)}), f32[8,80,768]{2,1,0:T(8,128)S(1)}, u32[]{:S(2)}, u32[]{:S(2)}) async-start(f32[8,80,768]{2,1,0:T(8,128)} %get-tuple-element.24), calls=%async_computation.1 | async-start | bytes 3932160 | tf_op jit(solution)/shard_map/all_to_all | solution.py:376
  39.4 43.2 %collective-permute-start = (f32[512,768]{1,0:T(8,128)}, f32[512,768]{1,0:T(8,128)}, u32[]{:S(2)}, u32[]{:S(2)}) collective-permute-start(f32[512,768]{1,0:T(8,128)} %bitcast.5.refs_0_), channel_id=1, source_target_pairs={{0,2},{2,4},{7,5},{5,3},{8,10},{10,12},{15,13},{13,11},{16,18},{18... | collective-permute-start | bytes 4718600 | tf_op jit(solution)/shard_map/ppermute | solution.py:412
  65.8 45.5 %all-to-all-start.2 = ((f32[8,64,768]{2,1,0:T(8,128)}), f32[8,64,768]{2,1,0:T(8,128)S(1)}, u32[]{:S(2)}, u32[]{:S(2)}) async-start(f32[8,64,768]{2,1,0:T(8,128)} %get-tuple-element.25), calls=%async_computation.2 | async-start | bytes 3145728 | tf_op jit(solution)/shard_map/all_to_all | solution.py:376
  70.9 13.5 %copy-start.3 = (f32[8,1,192]{2,0,1:T(8,128)}, f32[8,1,192]{2,0,1:T(8,128)S(1)}, u32[]{:S(2)}) copy-start(f32[8,1,192]{2,0,1:T(8,128)S(1)} %copy.16) | copy-start | bytes 18436
  71.0 15.4 %collective-permute-start.1 = (f32[8,192]{1,0:T(8,128)S(1)}, f32[8,192]{1,0:T(8,128)S(1)}, u32[]{:S(2)}, u32[]{:S(2)}) collective-permute-start(f32[8,192]{1,0:T(8,128)S(1)} %bitcast.22), channel_id=1, source_target_pairs={{0,2},{2,4},{7,5},{5,3},{8,10},{10,12},{15,13},{13,11},{16,18},{18... | collective-permute-start | bytes 18440 | tf_op jit(solution)/shard_map/ppermute | solution.py:407
  74.4 13.5 %collective-permute-start.2 = (f32[8,192]{1,0:T(8,128)S(1)}, f32[8,192]{1,0:T(8,128)}, u32[]{:S(2)}, u32[]{:S(2)}) collective-permute-start(f32[8,192]{1,0:T(8,128)S(1)} %bitcast.23), channel_id=1, source_target_pairs={{6,4},{1,3},{14,12},{9,11},{22,20},{17,19},{30,28},{25,27}} | collective-permute-start | bytes 18440 | tf_op jit(solution)/shard_map/ppermute | solution.py:408
  75.7 14.8 %collective-permute-start.3 = (f32[8,192]{1,0:T(8,128)S(1)}, f32[8,192]{1,0:T(8,128)}, u32[]{:S(2)}, u32[]{:S(2)}) collective-permute-start(f32[8,192]{1,0:T(8,128)S(1)} %bitcast.24), channel_id=1, source_target_pairs={{0,4},{2,6},{7,3},{5,1},{8,12},{10,14},{15,11},{13,9},{16,20},{18,... | collective-permute-start | bytes 18440 | tf_op jit(solution)/shard_map/ppermute | solution.py:407
  78.6 15.5 %collective-permute-start.4 = (f32[8,192]{1,0:T(8,128)S(1)}, f32[8,192]{1,0:T(8,128)}, u32[]{:S(2)}, u32[]{:S(2)}) collective-permute-start(f32[8,192]{1,0:T(8,128)S(1)} %bitcast.25), channel_id=1, source_target_pairs={{0,6},{7,1},{8,14},{15,9},{16,22},{23,17},{24,30},{31,25}} | collective-permute-start | bytes 18440 | tf_op jit(solution)/shard_map/ppermute | solution.py:407
  82.6 44.7 %collective-permute-start.15 = (f32[512,768]{1,0:T(8,128)}, f32[512,768]{1,0:T(8,128)}, u32[]{:S(2)}, u32[]{:S(2)}) collective-permute-start(f32[512,768]{1,0:T(8,128)} %bitcast.5.refs_0_), channel_id=1, source_target_pairs={{6,4},{1,3},{14,12},{9,11},{22,20},{17,19},{30,28},{25,27}} | collective-permute-start | bytes 4718600 | tf_op jit(solution)/shard_map/ppermute | solution.py:414
  86.4 18.1 %copy-start.2 = (f32[8,64,768]{2,1,0:T(8,128)S(1)}, f32[8,64,768]{2,1,0:T(8,128)}, u32[]{:S(2)}) copy-start(f32[8,64,768]{2,1,0:T(8,128)} %slice.18) | copy-start | bytes 4718596
  86.4 10.2 %copy-start.6 = (f32[8,192]{1,0:T(8,128)}, f32[8,192]{1,0:T(8,128)S(1)}, u32[]{:S(2)}) copy-start(f32[8,192]{1,0:T(8,128)S(1)} %collective-permute-done.1.refs_1_) | copy-start | bytes 18436
  86.4 12.2 %collective-permute-start.16 = (f32[16,768]{1,0:T(8,128)}, f32[16,768]{1,0:T(8,128)S(1)}, u32[]{:S(2)}, u32[]{:S(2)}) collective-permute-start(f32[16,768]{1,0:T(8,128)} %slice_reduce_fusion), channel_id=1, source_target_pairs={{0,0},{2,8},{4,16},{6,24},{8,2},{10,10},{12,18},{14,26},{16,4},{18... | collective-permute-start | bytes 147464 | tf_op jit(solution)/shard_map/ppermute | solution.py:491
  88.0 16.5 %collective-permute-start.17 = (f32[16,768]{1,0:T(8,128)}, f32[16,768]{1,0:T(8,128)S(1)}, u32[]{:S(2)}, u32[]{:S(2)}) collective-permute-start(f32[16,768]{1,0:T(8,128)} %slice_reduce_fusion), channel_id=1, source_target_pairs={{0,8},{2,16},{4,24},{6,0},{8,10},{10,18},{12,26},{14,2},{16,12},{1... | collective-permute-start | bytes 147464 | tf_op jit(solution)/shard_map/ppermute | solution.py:491
  90.4 19.0 %collective-permute-start.18 = (f32[16,768]{1,0:T(8,128)}, f32[16,768]{1,0:T(8,128)S(1)}, u32[]{:S(2)}, u32[]{:S(2)}) collective-permute-start(f32[16,768]{1,0:T(8,128)} %slice_reduce_fusion), channel_id=1, source_target_pairs={{0,16},{2,24},{4,0},{6,8},{8,18},{10,26},{12,2},{14,10},{16,20},{1... | collective-permute-start | bytes 147464 | tf_op jit(solution)/shard_map/ppermute | solution.py:491
  94.1 17.2 %collective-permute-start.19 = (f32[16,768]{1,0:T(8,128)}, f32[16,768]{1,0:T(8,128)S(1)}, u32[]{:S(2)}, u32[]{:S(2)}) collective-permute-start(f32[16,768]{1,0:T(8,128)} %slice_reduce_fusion), channel_id=1, source_target_pairs={{0,24},{2,0},{4,8},{6,16},{8,26},{10,2},{12,10},{14,18},{16,28},{1... | collective-permute-start | bytes 147464 | tf_op jit(solution)/shard_map/ppermute | solution.py:491
  98.6 30.5 %collective-permute-start.12 = (f32[512,768]{1,0:T(8,128)}, f32[512,768]{1,0:T(8,128)}, u32[]{:S(2)}, u32[]{:S(2)}) collective-permute-start(f32[512,768]{1,0:T(8,128)} %collective-permute-done.value_ref.refs_0_), channel_id=1, source_target_pairs={{2,4},{4,6},{5,3},{3,1},{10,12},{12,14},{13,11},{11,9},{18,20},{20... | collective-permute-start | bytes 4718600 | tf_op jit(solution)/shard_map/ppermute | solution.py:412
  104.4 38.6 %collective-permute-start.9 = (f32[512,768]{1,0:T(8,128)S(1)}, f32[512,768]{1,0:T(8,128)}, u32[]{:S(2)}, u32[]{:S(2)}) collective-permute-start(f32[512,768]{1,0:T(8,128)S(1)} %bitcast.19), channel_id=1, source_target_pairs={{0,2},{2,4},{7,5},{5,3},{8,10},{10,12},{15,13},{13,11},{16,18},{18... | collective-permute-start | bytes 4718600 | tf_op jit(solution)/shard_map/ppermute | solution.py:412
  109.5 69.7 %collective-permute-start.14 = (f32[512,768]{1,0:T(8,128)S(1)}, f32[512,768]{1,0:T(8,128)}, u32[]{:S(2)}, u32[]{:S(2)}) collective-permute-start(f32[512,768]{1,0:T(8,128)S(1)} %bitcast.20), channel_id=1, source_target_pairs={{6,4},{1,3},{14,12},{9,11},{22,20},{17,19},{30,28},{25,27}} | collective-permute-start | bytes 4718600 | tf_op jit(solution)/shard_map/ppermute | solution.py:414
  111.3 3.7 %copy-start.1 = (f32[8,64,768]{2,1,0:T(8,128)}, f32[8,64,768]{2,1,0:T(8,128)S(1)}, u32[]{:S(2)}) copy-start(f32[8,64,768]{2,1,0:T(8,128)S(1)} %all-to-all-done.2) | copy-start | bytes 4718596
  111.3 65.2 %collective-permute-start.6 = (f32[512,768]{1,0:T(8,128)S(1)}, f32[512,768]{1,0:T(8,128)}, u32[]{:S(2)}, u32[]{:S(2)}) collective-permute-start(f32[512,768]{1,0:T(8,128)S(1)} %bitcast.15), channel_id=1, source_target_pairs={{0,2},{2,4},{7,5},{5,3},{8,10},{10,12},{15,13},{13,11},{16,18},{18... | collective-permute-start | bytes 4718600 | tf_op jit(solution)/shard_map/ppermute | solution.py:412
  127.3 60.0 %collective-permute-start.5 = (f32[512,768]{1,0:T(8,128)}, f32[512,768]{1,0:T(8,128)}, u32[]{:S(2)}, u32[]{:S(2)}) collective-permute-start(f32[512,768]{1,0:T(8,128)} %bitcast.17), channel_id=1, source_target_pairs={{6,4},{1,3},{14,12},{9,11},{22,20},{17,19},{30,28},{25,27}} | collective-permute-start | bytes 4718600 | tf_op jit(solution)/shard_map/ppermute | solution.py:414
  129.1 54.3 %collective-permute-start.13 = (f32[512,768]{1,0:T(8,128)}, f32[512,768]{1,0:T(8,128)}, u32[]{:S(2)}, u32[]{:S(2)}) collective-permute-start(f32[512,768]{1,0:T(8,128)} %collective-permute-done.12.refs_2_), channel_id=1, source_target_pairs={{4,6},{3,1},{12,14},{11,9},{20,22},{19,17},{28,30},{27,25}} | collective-permute-start | bytes 4718600 | tf_op jit(solution)/shard_map/ppermute | solution.py:412
  143.1 37.7 %collective-permute-start.10 = (f32[512,768]{1,0:T(8,128)}, f32[512,768]{1,0:T(8,128)}, u32[]{:S(2)}, u32[]{:S(2)}) collective-permute-start(f32[512,768]{1,0:T(8,128)} %collective-permute-done.9.refs_0_), channel_id=1, source_target_pairs={{2,4},{4,6},{5,3},{3,1},{10,12},{12,14},{13,11},{11,9},{18,20},{20... | collective-permute-start | bytes 4718600 | tf_op jit(solution)/shard_map/ppermute | solution.py:412
  176.5 6.2 %collective-permute-start.7 = (f32[512,768]{1,0:T(8,128)}, f32[512,768]{1,0:T(8,128)S(1)}, u32[]{:S(2)}, u32[]{:S(2)}) collective-permute-start(f32[512,768]{1,0:T(8,128)} %collective-permute-done.6.refs_1_), channel_id=1, source_target_pairs={{2,4},{4,6},{5,3},{3,1},{10,12},{12,14},{13,11},{11,9},{18,20},{20... | collective-permute-start | bytes 4718600 | tf_op jit(solution)/shard_map/ppermute | solution.py:412
  180.8 4.9 %collective-permute-start.11 = (f32[512,768]{1,0:T(8,128)}, f32[512,768]{1,0:T(8,128)}, u32[]{:S(2)}, u32[]{:S(2)}) collective-permute-start(f32[512,768]{1,0:T(8,128)} %collective-permute-done.10.refs_0_), channel_id=1, source_target_pairs={{4,6},{3,1},{12,14},{11,9},{20,22},{19,17},{28,30},{27,25}} | collective-permute-start | bytes 4718600 | tf_op jit(solution)/shard_map/ppermute | solution.py:412
  182.7 1.2 copy-start.4
  182.7 4.6 %collective-permute-start.8 = (f32[512,768]{1,0:T(8,128)S(1)}, f32[512,768]{1,0:T(8,128)S(1)}, u32[]{:S(2)}, u32[]{:S(2)}) collective-permute-start(f32[512,768]{1,0:T(8,128)S(1)} %collective-permute-done.7.refs_2_), channel_id=1, source_target_pairs={{4,6},{3,1},{12,14},{11,9},{20,22},{19,17},{28,30},{27,25}} | collective-permute-start | bytes 4718600 | tf_op jit(solution)/shard_map/ppermute | solution.py:412
  187.3 1.2 copy-start.5
  191.7 49.3 %all-to-all-start.3 = ((f32[32,1,192]{2,1,0:T(1,128)}), f32[32,1,192]{2,1,0:T(1,128)S(1)}, u32[]{:S(2)}, u32[]{:S(2)}) async-start(f32[32,1,192]{2,1,0:T(1,128)} %all_to_all.19), calls=%async_computation.3 | async-start | bytes 65536 | tf_op jit(solution)/shard_map/all_to_all | solution.py:495

commit v5 on v4

--- a/solution.py
+++ b/solution.py
@@ -67,6 +67,10 @@
     return jax.ShapeDtypeStruct(shape, dtype)
 
 
+def unit_halves(x):
+    return halves(x * lax.rsqrt(jnp.sum(x * x, axis=1, keepdims=True) + 1e-6))
+
+
 def chunk_rows(owner, rank, high, low, k, owners, per):
     inside = (rank >= k * per) & (rank < (k + 1) * per)
     dest = jnp.where(inside, owner * per + rank - k * per, -1)
@@ -74,7 +78,7 @@
     return mm(pick, high) + mm(pick, low)
 
 
-def front_body(owners, per, cap, x_ref, ids_ref, om_ref, chunk_ref, high_ref, low_ref, info_ref):
+def front_body(owners, per, cap, x_ref, ids_ref, om_ref, chunk_ref, info_ref):
     x = x_ref[...]
     rows, width = x.shape
     clusters = om_ref.shape[0]
@@ -87,7 +91,15 @@
     owner = jnp.sum(jnp.where(here, om, 0), axis=0, keepdims=True)
     mine = iota((owners, rows), 0) == owner
     member = hot(here)
-    within = mm(member, hot(iota((rows, rows), 0) < iota((rows, rows), 1)))
+    step = LANES if rows % LANES == 0 else rows
+    ahead = hot(iota((step, step), 0) < iota((step, step), 1))
+    every = jnp.ones((step, step), jnp.bfloat16)
+    seen, within = jnp.zeros((clusters, step), jnp.float32), []
+    for b in range(0, rows, step):
+        part = member[:, b : b + step]
+        within.append(mm(part, ahead) + seen)
+        seen = seen + mm(part, every)
+    within = jnp.concatenate(within, axis=1)
     earlier = (om_col == om_row) & (iota(square, 1) < iota(square, 0))
     base = jnp.sum(mm(hot(earlier), member), axis=1, keepdims=True)
     rank = jnp.sum(jnp.where(here, within + base, 0.0), axis=0, keepdims=True)
@@ -97,10 +109,7 @@
     order = om * (clusters // owners) + jnp.sum(earlier.astype(jnp.int32), axis=1, keepdims=True)
     position = jnp.sum(jnp.where(here, order, 0), axis=0, keepdims=True)
     info_ref[...] = jnp.concatenate([owner, rank, position, position] * 2, axis=0)
-    unit = x * lax.rsqrt(jnp.sum(x * x, axis=1, keepdims=True) + 1e-6)
-    high, low = halves(unit)
-    high_ref[...] = high
-    low_ref[...] = low
+    high, low = unit_halves(x)
     chunk_ref[:, 0:per, :] = chunk_rows(owner, rank, high, low, 0, owners, per).reshape(owners, per, width)
     at_rank = hot(iota((cap, rows), 0) == rank)
     coarse = (ids + 1) // 16
@@ -113,9 +122,8 @@
         chunk_ref[p, per : per + 1, 0:cap] = sid[p : p + 1, :]
 
 
-def back_body(owners, per, chunks, held, high_ref, low_ref, info_ref, so_ref, *outs):
-    high = high_ref[...]
-    low = low_ref[...]
+def back_body(owners, per, chunks, held, x_ref, info_ref, so_ref, *outs):
+    high, low = unit_halves(x_ref[...])
     owner = info_ref[0:1, :]
     rank = info_ref[1:2, :]
     position = info_ref[2:3, :]
@@ -206,7 +214,8 @@
     slots = high_ref.shape[0]
     tile = size // TILES
     blocks = slots // tile
-    part_out[...] = part_ref[...]
+    sums = pltpu.make_async_copy(part_ref, part_out, own_sem.at[5])
+    sums.start()
     alive = level_ref[items[0][0]] >= 0
     for at, k in items[1:]:
         alive = alive | (level_ref[at] >= 0)
@@ -262,6 +271,7 @@
                 pair_ref[5, total] = (used < end).astype(jnp.int32)
                 total = total + (live & (start <= end)).astype(jnp.int32)
 
+    sums.wait()
     for n, (at, k) in enumerate(items):
 
         @pl.when(level_ref[at] >= 0)
@@ -354,15 +364,15 @@
     bf, i32 = jnp.bfloat16, jnp.int32
     dealt = [out((owners, per + extra, width)) for extra in (8, held, 0)]
 
-    first, high, low, info = call(
+    first, info = call(
         functools.partial(front_body, owners, per, cap),
-        (dealt[0], out((rows, width), bf), out((rows, width), bf), out((8, rows), i32)),
+        (dealt[0], out((8, rows), i32)),
         embeddings, cluster_ids, owner_map, micros=5,
     )
     back = call(
         functools.partial(back_body, owners, per, CHUNKS, held),
         tuple(dealt[1:]) + (out((8, rows), i32),),
-        high, low, info, source_order, micros=6,
+        embeddings, info, source_order, micros=6,
     )
     sends = (first,) + tuple(back[: CHUNKS - 1])
     q_info = back[CHUNKS - 1]
@@ -462,11 +472,11 @@
         ]
         if not own:
             scratch += [VMEM((count * size, width), bf)] * 2
-        scratch += [pltpu.SemaphoreType.DMA((5,))]
+        scratch += [pltpu.SemaphoreType.DMA((6,))]
         return pl.pallas_call(
             functools.partial(gram_body, owners, at, own, len(held)),
             out_shape=(out((levels, slots)),) + own_out,
-            in_specs=[pl.BlockSpec(memory_space=pltpu.SMEM)] * 2 + [any_] * (count + len(held)) + [vm] * 2,
+            in_specs=[pl.BlockSpec(memory_space=pltpu.SMEM)] * 2 + [any_] * (count + len(held)) + [vm, any_],
             out_specs=(vm,) * (1 + len(own_out)),
             scratch_shapes=scratch,
             cost_estimate=cost(micros),
@@ -476,10 +486,10 @@
     plan = [
         ([("own", k) for k in range(CHUNKS)], 13),
         ([(1, 0), ("b", 0), (2, 0)], 14),
-        ([(1, 1), ("b", 1)], 11),
-        ([(2, 1), (1, 2), (2, 2), (3, 0)], 17),
-        ([(3, 1)], 8),
-        ([("b", 2), (3, 2)], 8),
+        ([(1, 1), (2, 1)], 11),
+        ([("b", 1), (1, 2), (2, 2), (3, 0)], 17),
+        ([(3, 1), ("b", 2)], 8),
+        ([(3, 2)], 8),
     ]
     held_here = ()
     for items, micros in plan:

time: 245 us -> 241 us (0.984)
  waiting for transfers between devices: 92.1 us -> 64.4 us
  starting transfers between devices: 103 us -> 126 us
  Pallas kernels: 36.7 us -> 39.4 us
    ppermute x9, waiting for transfers between devices: 43.8 us -> 15 us  [body(): value = lax.ppermute(value, LINE, pairs(moves[s - 1]))]
    all_to_all x1, starting transfers between devices: 42 us -> 64.3 us  [body(): home = lax.all_to_all(parts, BY_LEVEL, 0, 0, tiled=True)]
    ppermute x3, waiting for transfers between devices: 0.01 us -> 5.43 us  [body(): ids_of.append(lax.ppermute(own_ids, LINE, pairs(direct(s))))]
    ppermute x4, waiting for transfers between devices: 4.07 us -> 0.01 us  [body(): came = lax.ppermute(piece, ('grp', 'outer'), route)]
    ppermute x9, starting transfers between devices: 21.5 us -> 25 us  [body(): value = lax.ppermute(value, LINE, pairs(moves[s - 1]))]
    ppermute x3, starting transfers between devices: 10.4 us -> 7.03 us  [body(): ids_of.append(lax.ppermute(own_ids, LINE, pairs(direct(s))))]
    pallas_call x6, Pallas kernels: 20.7 us -> 23.2 us  [gram(): pl.pallas_call(functools.partial(gram_body, owners, at, own, len(held)),...]
  transfers between devices with their start and end apart: 24 -> 24, of which waited for: 6 -> 5; matrix products, arithmetic and copies ran while one was open for 2% -> 2% of each run, Pallas kernels for 12% -> 13%
where the time goes in v5:
time: 241 us; the launch traced here: 240 us
  starting transfers between devices  126 us (52%)
  waiting for transfers between devices  64.4 us (27%)
  Pallas kernels  39.4 us (16%)
  local copies, waits for them, and re-layouts  7.43 us (3%)
    all_to_all x1, starting transfers between devices, body(): home = lax.all_to_all(parts, BY_LEVEL, 0, 0, tiled=True)  64.3 us
    all_to_all x3, waiting for transfers between devices, body(): got.append(lax.all_to_all(send, PLANE, 0, 0, tiled=True))  37.4 us
    ppermute x9, starting transfers between devices, body(): value = lax.ppermute(value, LINE, pairs(moves[s - 1]))  25 us
    pallas_call x6, Pallas kernels, gram(): pl.pallas_call(functools.partial(gram_body, owners, at, own, len(held)),...  23.2 us
    ppermute x9, waiting for transfers between devices, body(): value = lax.ppermute(value, LINE, pairs(moves[s - 1]))  15 us
    pallas_call x4, Pallas kernels, call(): pl.pallas_call(body, out_shape=outs, in_specs=spec, out_specs=jax.tree.ma...  14.9 us
    all_to_all x3, starting transfers between devices, body(): got.append(lax.all_to_all(send, PLANE, 0, 0, tiled=True))  12.4 us
    ppermute x4, starting transfers between devices, body(): came = lax.ppermute(piece, ('grp', 'outer'), route)  10.6 us
  transfers between devices with their start and end apart: 24, of which 5 were waited for; matrix products, arithmetic and copies ran while one was open for 2% of the time, Pallas kernels for 13%

profile of v5, /device:TPU:0, one launch (start us, length us, event | category | flops | bytes accessed | tf_op | source)
XLA Modules:
  0.0 239.7 jit_solution(2108748681072385013)
XLA Ops:
  0.6 5.0 %shard_map.59 = (f32[8,72,768]{2,1,0:T(8,128)}, s32[8,768]{1,0:T(8,128)}) custom-call(f32[768,768]{1,0:T(8,128)} %x_ref.3, s32[768]{0:T(1024)} %ids_ref.1, s32[128]{0:T(128)} %om_ref.1), custom_call_target="tpu_custom_call" | custom-call | flops 5500000256 | tf_op jit(solution)/shard_map/pallas_call | solution.py:55
  5.7 5.2 %all-to-all-start = ((f32[8,72,768]{2,1,0:T(8,128)}), f32[8,72,768]{2,1,0:T(8,128)S(1)}, u32[]{:S(2)}, u32[]{:S(2)}) async-start(f32[8,72,768]{2,1,0:T(8,128)} %get-tuple-element.15), calls=%async_computation | async-start | bytes 3538944 | tf_op jit(solution)/shard_map/all_to_all | solution.py:386
  10.9 6.2 %shard_map.62 = (f32[8,80,768]{2,1,0:T(8,128)}, f32[8,64,768]{2,1,0:T(8,128)}, s32[8,768]{1,0:T(8,128)}) custom-call(f32[768,768]{1,0:T(8,128)} %x_ref.3, s32[8,768]{1,0:T(8,128)} %get-tuple-element.17.info_ref, s32[768]{0:T(1024)} %so_ref.1), custom_call_target="tpu_custom_call" | custom-call | flops 6600000000 | tf_op jit(solution)/shard_map/pallas_call | solution.py:55
  17.1 16.9 %all-to-all-done = f32[8,72,768]{2,1,0:T(8,128)S(1)} async-done(((f32[8,72,768]{2,1,0:T(8,128)}), f32[8,72,768]{2,1,0:T(8,128)S(1)}, u32[]{:S(2)}, u32[]{:S(2)}) %all-to-all-start) | async-done | bytes 1769504 | tf_op jit(solution)/shard_map/all_to_all | solution.py:386
  35.8 3.6 %all-to-all-start.1 = ((f32[8,80,768]{2,1,0:T(8,128)}), f32[8,80,768]{2,1,0:T(8,128)S(1)}, u32[]{:S(2)}, u32[]{:S(2)}) async-start(f32[8,80,768]{2,1,0:T(8,128)} %get-tuple-element.20), calls=%async_computation.1 | async-start | bytes 3932160 | tf_op jit(solution)/shard_map/all_to_all | solution.py:386
  39.4 4.6 %collective-permute-start = (f32[512,768]{1,0:T(8,128)}, f32[512,768]{1,0:T(8,128)}, u32[]{:S(2)}, u32[]{:S(2)}) collective-permute-start(f32[512,768]{1,0:T(8,128)} %bitcast.5.refs_0_), channel_id=1, source_target_pairs={{0,2},{2,4},{7,5},{5,3},{8,10},{10,12},{15,13},{13,11},{16,18},{18... | collective-permute-start | bytes 4718600 | tf_op jit(solution)/shard_map/ppermute | solution.py:422
  44.1 20.5 %all-to-all-done.1 = f32[8,80,768]{2,1,0:T(8,128)S(1)} async-done(((f32[8,80,768]{2,1,0:T(8,128)}), f32[8,80,768]{2,1,0:T(8,128)S(1)}, u32[]{:S(2)}, u32[]{:S(2)}) %all-to-all-start.1) | async-done | bytes 1966112 | tf_op jit(solution)/shard_map/all_to_all | solution.py:386
  65.9 3.6 %all-to-all-start.2 = ((f32[8,64,768]{2,1,0:T(8,128)}), f32[8,64,768]{2,1,0:T(8,128)S(1)}, u32[]{:S(2)}, u32[]{:S(2)}) async-start(f32[8,64,768]{2,1,0:T(8,128)} %get-tuple-element.21), calls=%async_computation.2 | async-start | bytes 3145728 | tf_op jit(solution)/shard_map/all_to_all | solution.py:386
  69.4 4.7 %collective-permute-start.8 = (f32[512,768]{1,0:T(8,128)}, f32[512,768]{1,0:T(8,128)}, u32[]{:S(2)}, u32[]{:S(2)}) collective-permute-start(f32[512,768]{1,0:T(8,128)} %bitcast.18), channel_id=1, source_target_pairs={{0,2},{2,4},{7,5},{5,3},{8,10},{10,12},{15,13},{13,11},{16,18},{18... | collective-permute-start | bytes 4718600 | tf_op jit(solution)/shard_map/ppermute | solution.py:422
  75.6 2.3 collective-permute-start.1
  79.2 1.9 collective-permute-start.3
  81.1 2.8 %collective-permute-start.4 = (f32[8,192]{1,0:T(8,128)S(1)}, f32[8,192]{1,0:T(8,128)}, u32[]{:S(2)}, u32[]{:S(2)}) collective-permute-start(f32[8,192]{1,0:T(8,128)S(1)} %bitcast.25), channel_id=1, source_target_pairs={{0,6},{7,1},{8,14},{15,9},{16,22},{23,17},{24,30},{31,25}} | collective-permute-start | bytes 18440 | tf_op jit(solution)/shard_map/ppermute | solution.py:417
  85.8 5.4 %collective-permute-done.1.refs_1_ = f32[8,192]{1,0:T(8,128)S(1)} collective-permute-done((f32[8,192]{1,0:T(8,128)S(1)}, f32[8,192]{1,0:T(8,128)S(1)}, u32[]{:S(2)}, u32[]{:S(2)}) %collective-permute-start.1) | collective-permute-done | bytes 6176 | tf_op jit(solution)/shard_map/ppermute | solution.py:417
  92.7 4.5 %collective-permute-start.17 = (f32[16,768]{1,0:T(8,128)}, f32[16,768]{1,0:T(8,128)S(1)}, u32[]{:S(2)}, u32[]{:S(2)}) collective-permute-start(f32[16,768]{1,0:T(8,128)} %slice_reduce_fusion), channel_id=1, source_target_pairs={{0,8},{2,16},{4,24},{6,0},{8,10},{10,18},{12,26},{14,2},{16,12},{1... | collective-permute-start | bytes 147464 | tf_op jit(solution)/shard_map/ppermute | solution.py:501
  97.2 3.7 %collective-permute-start.18 = (f32[16,768]{1,0:T(8,128)}, f32[16,768]{1,0:T(8,128)S(1)}, u32[]{:S(2)}, u32[]{:S(2)}) collective-permute-start(f32[16,768]{1,0:T(8,128)} %slice_reduce_fusion), channel_id=1, source_target_pairs={{0,16},{2,24},{4,0},{6,8},{8,18},{10,26},{12,2},{14,10},{16,20},{1... | collective-permute-start | bytes 147464 | tf_op jit(solution)/shard_map/ppermute | solution.py:501
  101.9 2.0 shard_map.61
  107.5 1.8 collective-permute-start.12
  109.4 5.8 %collective-permute-start.5 = (f32[512,768]{1,0:T(8,128)S(1)}, f32[512,768]{1,0:T(8,128)}, u32[]{:S(2)}, u32[]{:S(2)}) collective-permute-start(f32[512,768]{1,0:T(8,128)S(1)} %bitcast.15), channel_id=1, source_target_pairs={{0,2},{2,4},{7,5},{5,3},{8,10},{10,12},{15,13},{13,11},{16,18},{18... | collective-permute-start | bytes 4718600 | tf_op jit(solution)/shard_map/ppermute | solution.py:422
  115.4 1.8 collective-permute-start.9
  117.8 12.3 %gram.6 = (f32[4,1536]{1,0:T(4,128)}, bf16[1536,768]{1,0:T(8,128)(2,1)}, bf16[1536,768]{1,0:T(8,128)(2,1)}, f32[1536,128]{1,0:T(8,128)}) custom-call(s32[5]{0:T(128)} %stack.23.level_ref, s32[8,128]{1,0:T(8,128)} %get-tuple-element.16.flag_ref, f32[512,768]{1,0:T(8,128)} %bitcast.5.refs_0_, f32[512,768]{1,0:T(8,128)} %bitcast.19, f32[512,768]{1,0:T(8,128)} %bitcast.16, ...), custom_call_target="tpu_custom_call" | custom-call | flops 14300000256 | tf_op jit(solution)/shard_map/gram/pallas_call | solution.py:476
  130.1 1.9 collective-permute-start.11
  132.0 1.8 collective-permute-start.14
  133.8 15.0 %collective-permute-done.5.refs_1_ = f32[512,768]{1,0:T(8,128)} collective-permute-done((f32[512,768]{1,0:T(8,128)S(1)}, f32[512,768]{1,0:T(8,128)}, u32[]{:S(2)}, u32[]{:S(2)}) %collective-permute-start.5) | collective-permute-done | bytes 1572896 | tf_op jit(solution)/shard_map/ppermute | solution.py:422
  149.6 2.2 gram.7.refs_6_
  151.8 1.8 collective-permute-start.10
  153.6 2.2 gram.8.refs_8_
  155.8 1.8 collective-permute-start.7
  157.6 2.2 gram.9.refs_6_
  159.9 2.2 gram.10.refs_5_
  162.1 2.2 gram.11
  165.9 64.3 %all-to-all-start.3 = ((f32[32,1,192]{2,1,0:T(1,128)}), f32[32,1,192]{2,1,0:T(1,128)S(1)}, u32[]{:S(2)}, u32[]{:S(2)}) async-start(f32[32,1,192]{2,1,0:T(1,128)} %all_to_all.19), calls=%async_computation.3 | async-start | bytes 65536 | tf_op jit(solution)/shard_map/all_to_all | solution.py:505
  230.9 6.6 %all-to-all-done.3 = f32[32,1,192]{2,1,0:T(1,128)S(1)} async-done(((f32[32,1,192]{2,1,0:T(1,128)}), f32[32,1,192]{2,1,0:T(1,128)S(1)}, u32[]{:S(2)}, u32[]{:S(2)}) %all-to-all-start.3) | async-done | bytes 24608 | tf_op jit(solution)/shard_map/all_to_all | solution.py:505
  (53 shorter events, 19.9 us)
Async XLA Ops:
  5.7 28.3 %all-to-all-start = ((f32[8,72,768]{2,1,0:T(8,128)}), f32[8,72,768]{2,1,0:T(8,128)S(1)}, u32[]{:S(2)}, u32[]{:S(2)}) async-start(f32[8,72,768]{2,1,0:T(8,128)} %get-tuple-element.15), calls=%async_computation | async-start | bytes 3538944 | tf_op jit(solution)/shard_map/all_to_all | solution.py:386
  34.0 1.8 copy-start
  35.8 28.7 %all-to-all-start.1 = ((f32[8,80,768]{2,1,0:T(8,128)}), f32[8,80,768]{2,1,0:T(8,128)S(1)}, u32[]{:S(2)}, u32[]{:S(2)}) async-start(f32[8,80,768]{2,1,0:T(8,128)} %get-tuple-element.20), calls=%async_computation.1 | async-start | bytes 3932160 | tf_op jit(solution)/shard_map/all_to_all | solution.py:386
  39.4 41.6 %collective-permute-start = (f32[512,768]{1,0:T(8,128)}, f32[512,768]{1,0:T(8,128)}, u32[]{:S(2)}, u32[]{:S(2)}) collective-permute-start(f32[512,768]{1,0:T(8,128)} %bitcast.5.refs_0_), channel_id=1, source_target_pairs={{0,2},{2,4},{7,5},{5,3},{8,10},{10,12},{15,13},{13,11},{16,18},{18... | collective-permute-start | bytes 4718600 | tf_op jit(solution)/shard_map/ppermute | solution.py:422
  65.9 43.5 %all-to-all-start.2 = ((f32[8,64,768]{2,1,0:T(8,128)}), f32[8,64,768]{2,1,0:T(8,128)S(1)}, u32[]{:S(2)}, u32[]{:S(2)}) async-start(f32[8,64,768]{2,1,0:T(8,128)} %get-tuple-element.21), calls=%async_computation.2 | async-start | bytes 3145728 | tf_op jit(solution)/shard_map/all_to_all | solution.py:386
  69.4 45.9 %collective-permute-start.8 = (f32[512,768]{1,0:T(8,128)}, f32[512,768]{1,0:T(8,128)}, u32[]{:S(2)}, u32[]{:S(2)}) collective-permute-start(f32[512,768]{1,0:T(8,128)} %bitcast.18), channel_id=1, source_target_pairs={{0,2},{2,4},{7,5},{5,3},{8,10},{10,12},{15,13},{13,11},{16,18},{18... | collective-permute-start | bytes 4718600 | tf_op jit(solution)/shard_map/ppermute | solution.py:422
  75.6 8.3 %copy-start.3 = (f32[8,1,192]{2,0,1:T(8,128)}, f32[8,1,192]{2,0,1:T(8,128)S(1)}, u32[]{:S(2)}) copy-start(f32[8,1,192]{2,0,1:T(8,128)S(1)} %copy.16) | copy-start | bytes 18436
  75.6 15.7 %collective-permute-start.1 = (f32[8,192]{1,0:T(8,128)S(1)}, f32[8,192]{1,0:T(8,128)S(1)}, u32[]{:S(2)}, u32[]{:S(2)}) collective-permute-start(f32[8,192]{1,0:T(8,128)S(1)} %bitcast.22), channel_id=1, source_target_pairs={{0,2},{2,4},{7,5},{5,3},{8,10},{10,12},{15,13},{13,11},{16,18},{18... | collective-permute-start | bytes 18440 | tf_op jit(solution)/shard_map/ppermute | solution.py:417
  77.9 14.8 %collective-permute-start.2 = (f32[8,192]{1,0:T(8,128)S(1)}, f32[8,192]{1,0:T(8,128)}, u32[]{:S(2)}, u32[]{:S(2)}) collective-permute-start(f32[8,192]{1,0:T(8,128)S(1)} %bitcast.23), channel_id=1, source_target_pairs={{6,4},{1,3},{14,12},{9,11},{22,20},{17,19},{30,28},{25,27}} | collective-permute-start | bytes 18440 | tf_op jit(solution)/shard_map/ppermute | solution.py:418
  79.2 18.0 %collective-permute-start.3 = (f32[8,192]{1,0:T(8,128)S(1)}, f32[8,192]{1,0:T(8,128)}, u32[]{:S(2)}, u32[]{:S(2)}) collective-permute-start(f32[8,192]{1,0:T(8,128)S(1)} %bitcast.24), channel_id=1, source_target_pairs={{0,4},{2,6},{7,3},{5,1},{8,12},{10,14},{15,11},{13,9},{16,20},{18,... | collective-permute-start | bytes 18440 | tf_op jit(solution)/shard_map/ppermute | solution.py:417
  81.1 19.8 %collective-permute-start.4 = (f32[8,192]{1,0:T(8,128)S(1)}, f32[8,192]{1,0:T(8,128)}, u32[]{:S(2)}, u32[]{:S(2)}) collective-permute-start(f32[8,192]{1,0:T(8,128)S(1)} %bitcast.25), channel_id=1, source_target_pairs={{0,6},{7,1},{8,14},{15,9},{16,22},{23,17},{24,30},{31,25}} | collective-permute-start | bytes 18440 | tf_op jit(solution)/shard_map/ppermute | solution.py:417
  85.8 21.7 %copy-start.2 = (f32[8,64,768]{2,1,0:T(8,128)S(1)}, f32[8,64,768]{2,1,0:T(8,128)}, u32[]{:S(2)}) copy-start(f32[8,64,768]{2,1,0:T(8,128)} %slice.18) | copy-start | bytes 4718596
  91.3 10.7 %copy-start.5 = (f32[8,192]{1,0:T(8,128)}, f32[8,192]{1,0:T(8,128)S(1)}, u32[]{:S(2)}) copy-start(f32[8,192]{1,0:T(8,128)S(1)} %collective-permute-done.1.refs_1_) | copy-start | bytes 18436
  91.3 12.7 %collective-permute-start.16 = (f32[16,768]{1,0:T(8,128)}, f32[16,768]{1,0:T(8,128)S(1)}, u32[]{:S(2)}, u32[]{:S(2)}) collective-permute-start(f32[16,768]{1,0:T(8,128)} %slice_reduce_fusion), channel_id=1, source_target_pairs={{0,0},{2,8},{4,16},{6,24},{8,2},{10,10},{12,18},{14,26},{16,4},{18... | collective-permute-start | bytes 147464 | tf_op jit(solution)/shard_map/ppermute | solution.py:501
  92.7 13.0 %collective-permute-start.17 = (f32[16,768]{1,0:T(8,128)}, f32[16,768]{1,0:T(8,128)S(1)}, u32[]{:S(2)}, u32[]{:S(2)}) collective-permute-start(f32[16,768]{1,0:T(8,128)} %slice_reduce_fusion), channel_id=1, source_target_pairs={{0,8},{2,16},{4,24},{6,0},{8,10},{10,18},{12,26},{14,2},{16,12},{1... | collective-permute-start | bytes 147464 | tf_op jit(solution)/shard_map/ppermute | solution.py:501
  97.2 10.4 %collective-permute-start.18 = (f32[16,768]{1,0:T(8,128)}, f32[16,768]{1,0:T(8,128)S(1)}, u32[]{:S(2)}, u32[]{:S(2)}) collective-permute-start(f32[16,768]{1,0:T(8,128)} %slice_reduce_fusion), channel_id=1, source_target_pairs={{0,16},{2,24},{4,0},{6,8},{8,18},{10,26},{12,2},{14,10},{16,20},{1... | collective-permute-start | bytes 147464 | tf_op jit(solution)/shard_map/ppermute | solution.py:501
  100.9 8.5 %collective-permute-start.19 = (f32[16,768]{1,0:T(8,128)}, f32[16,768]{1,0:T(8,128)S(1)}, u32[]{:S(2)}, u32[]{:S(2)}) collective-permute-start(f32[16,768]{1,0:T(8,128)} %slice_reduce_fusion), channel_id=1, source_target_pairs={{0,24},{2,0},{4,8},{6,16},{8,26},{10,2},{12,10},{14,18},{16,28},{1... | collective-permute-start | bytes 147464 | tf_op jit(solution)/shard_map/ppermute | solution.py:501
  103.9 26.1 %collective-permute-start.15 = (f32[512,768]{1,0:T(8,128)}, f32[512,768]{1,0:T(8,128)}, u32[]{:S(2)}, u32[]{:S(2)}) collective-permute-start(f32[512,768]{1,0:T(8,128)} %bitcast.5.refs_0_), channel_id=1, source_target_pairs={{6,4},{1,3},{14,12},{9,11},{22,20},{17,19},{30,28},{25,27}} | collective-permute-start | bytes 4718600 | tf_op jit(solution)/shard_map/ppermute | solution.py:424
  105.7 26.2 %collective-permute-start.13 = (f32[512,768]{1,0:T(8,128)}, f32[512,768]{1,0:T(8,128)}, u32[]{:S(2)}, u32[]{:S(2)}) collective-permute-start(f32[512,768]{1,0:T(8,128)} %collective-permute-done.value_ref.refs_0_), channel_id=1, source_target_pairs={{2,4},{4,6},{5,3},{3,1},{10,12},{12,14},{13,11},{11,9},{18,20},{20... | collective-permute-start | bytes 4718600 | tf_op jit(solution)/shard_map/ppermute | solution.py:422
  107.5 50.1 %collective-permute-start.12 = (f32[512,768]{1,0:T(8,128)S(1)}, f32[512,768]{1,0:T(8,128)}, u32[]{:S(2)}, u32[]{:S(2)}) collective-permute-start(f32[512,768]{1,0:T(8,128)S(1)} %bitcast.20), channel_id=1, source_target_pairs={{6,4},{1,3},{14,12},{9,11},{22,20},{17,19},{30,28},{25,27}} | collective-permute-start | bytes 4718600 | tf_op jit(solution)/shard_map/ppermute | solution.py:424
  109.4 8.4 %copy-start.1 = (f32[8,64,768]{2,1,0:T(8,128)}, f32[8,64,768]{2,1,0:T(8,128)S(1)}, u32[]{:S(2)}) copy-start(f32[8,64,768]{2,1,0:T(8,128)S(1)} %all-to-all-done.2) | copy-start | bytes 4718596
  109.4 39.4 %collective-permute-start.5 = (f32[512,768]{1,0:T(8,128)S(1)}, f32[512,768]{1,0:T(8,128)}, u32[]{:S(2)}, u32[]{:S(2)}) collective-permute-start(f32[512,768]{1,0:T(8,128)S(1)} %bitcast.15), channel_id=1, source_target_pairs={{0,2},{2,4},{7,5},{5,3},{8,10},{10,12},{15,13},{13,11},{16,18},{18... | collective-permute-start | bytes 4718600 | tf_op jit(solution)/shard_map/ppermute | solution.py:422
  115.4 36.4 %collective-permute-start.9 = (f32[512,768]{1,0:T(8,128)}, f32[512,768]{1,0:T(8,128)}, u32[]{:S(2)}, u32[]{:S(2)}) collective-permute-start(f32[512,768]{1,0:T(8,128)} %collective-permute-done.8.refs_0_), channel_id=1, source_target_pairs={{2,4},{4,6},{5,3},{3,1},{10,12},{12,14},{13,11},{11,9},{18,20},{20... | collective-permute-start | bytes 4718600 | tf_op jit(solution)/shard_map/ppermute | solution.py:422
  130.1 29.8 %collective-permute-start.11 = (f32[512,768]{1,0:T(8,128)}, f32[512,768]{1,0:T(8,128)}, u32[]{:S(2)}, u32[]{:S(2)}) collective-permute-start(f32[512,768]{1,0:T(8,128)} %bitcast.17), channel_id=1, source_target_pairs={{6,4},{1,3},{14,12},{9,11},{22,20},{17,19},{30,28},{25,27}} | collective-permute-start | bytes 4718600 | tf_op jit(solution)/shard_map/ppermute | solution.py:424
  132.0 25.6 %collective-permute-start.14 = (f32[512,768]{1,0:T(8,128)}, f32[512,768]{1,0:T(8,128)}, u32[]{:S(2)}, u32[]{:S(2)}) collective-permute-start(f32[512,768]{1,0:T(8,128)} %collective-permute-done.13.refs_2_), channel_id=1, source_target_pairs={{4,6},{3,1},{12,14},{11,9},{20,22},{19,17},{28,30},{27,25}} | collective-permute-start | bytes 4718600 | tf_op jit(solution)/shard_map/ppermute | solution.py:422
  148.8 7.0 %collective-permute-start.6 = (f32[512,768]{1,0:T(8,128)}, f32[512,768]{1,0:T(8,128)S(1)}, u32[]{:S(2)}, u32[]{:S(2)}) collective-permute-start(f32[512,768]{1,0:T(8,128)} %collective-permute-done.5.refs_1_), channel_id=1, source_target_pairs={{2,4},{4,6},{5,3},{3,1},{10,12},{12,14},{13,11},{11,9},{18,20},{20... | collective-permute-start | bytes 4718600 | tf_op jit(solution)/shard_map/ppermute | solution.py:422
  151.8 8.1 %collective-permute-start.10 = (f32[512,768]{1,0:T(8,128)}, f32[512,768]{1,0:T(8,128)}, u32[]{:S(2)}, u32[]{:S(2)}) collective-permute-start(f32[512,768]{1,0:T(8,128)} %collective-permute-done.9.refs_1_), channel_id=1, source_target_pairs={{4,6},{3,1},{12,14},{11,9},{20,22},{19,17},{28,30},{27,25}} | collective-permute-start | bytes 4718600 | tf_op jit(solution)/shard_map/ppermute | solution.py:422
  155.8 1.8 copy-start.4
  155.8 6.3 %collective-permute-start.7 = (f32[512,768]{1,0:T(8,128)S(1)}, f32[512,768]{1,0:T(8,128)}, u32[]{:S(2)}, u32[]{:S(2)}) collective-permute-start(f32[512,768]{1,0:T(8,128)S(1)} %collective-permute-done.6.refs_2_), channel_id=1, source_target_pairs={{4,6},{3,1},{12,14},{11,9},{20,22},{19,17},{28,30},{27,25}} | collective-permute-start | bytes 4718600 | tf_op jit(solution)/shard_map/ppermute | solution.py:422
  165.9 71.6 %all-to-all-start.3 = ((f32[32,1,192]{2,1,0:T(1,128)}), f32[32,1,192]{2,1,0:T(1,128)S(1)}, u32[]{:S(2)}, u32[]{:S(2)}) async-start(f32[32,1,192]{2,1,0:T(1,128)} %all_to_all.19), calls=%async_computation.3 | async-start | bytes 65536 | tf_op jit(solution)/shard_map/all_to_all | solution.py:505
